TPU v7x, 256 devices: a whole 4x4x8 slice. The times are simulated.
256 devices in a mesh: dom: 128 (over x, y, z), feat: 2 (over core).
Axes of the slice: x: 4, y: 4, z: 8, core: 2. Of those that a mesh axis runs over, the one named last changes fastest.
Arguments:
- increments: bfloat16 [524288, 128], P('dom'), may hold values from -6 to 6
- w_in: bfloat16 [128, 256], replicated, may hold values from -0.5 to 0.5
- w_node1: bfloat16 [512, 512], replicated, may hold values from -0.25 to 0.25
- w_node2: bfloat16 [512, 256], replicated, may hold values from -0.25 to 0.25
- w_out: bfloat16 [256, 128], replicated, may hold values from -0.375 to 0.375
- grid_edges: int32 [131072, 4], P('dom'), may hold values from 0 to 4095
- mesh_edges: int32 [131072, 6], P('dom'), may hold values from 0 to 3071
- mesh_mask: int32 [131072, 6], P('dom'), may hold values 0 or 1
- send_rows: int32 [128, 128, 16], P('dom'), may hold values from 0 to 1023
- site_owner: int32 [32768, 1], P('dom'), may hold values from 0 to 127; in each aligned block of 256 rows (0 to 255, 256 to 511, ...) at most 4 rows name the same one
- site_nodes: int32 [32768, 8], P('dom'), may hold values from 0 to 1023
- site_obs: bfloat16 [32768, 128], P('dom'), may hold values from -4 to 4
Outputs:
- grad_grid: float32 [524288, 128], P('dom', 'feat')
- site_pred: bfloat16 [32768, 128], P('dom')
Inputs may be any that keep to these rules, and one draw needn't show every extreme that they name: `site_owner`: among the rows of one partition, at most 4 sites name the same owner, and that many do in some partition.
All inputs are finite; a program needn't handle non-finite values. No bound on the sum of `mesh_mask` on one device may be relied on, other than what follows from the above.
Results may differ from a plain program's by a relative error of at most 0.012.
Values may be sent and summed in bfloat16 or wider, within the bound.
No kernel may reach another device: no remote copies, remote signals or barrier semaphores. Data moves between devices by JAX's collectives and lax.ppermute only.
A program may use at most 64 MiB of HBM per device.

v0:
```python
import jax
import jax.numpy as jnp
from jax import lax
from jax.sharding import PartitionSpec as P


def silu_slope(pre):
    sig = jax.nn.sigmoid(pre)
    return sig * (1.0 + pre * (1.0 - sig))


def local(
    increments,
    w_in,
    w_node1,
    w_node2,
    w_out,
    grid_edges,
    mesh_edges,
    mesh_mask,
    send_rows,
    site_owner,
    site_nodes,
    site_obs,
):
    domains = lax.axis_size("dom")
    halves = lax.axis_size("feat")
    feat_index = lax.axis_index("feat")
    width = w_node2.shape[1]
    inner = w_node2.shape[0]
    mesh_rows = mesh_edges.shape[0]
    grid_rows = increments.shape[0]
    grid_degree = grid_edges.shape[1]
    site_degree = site_nodes.shape[1]
    halo_depth = send_rows.shape[2]
    site_count = site_obs.shape[0]
    variables = site_obs.shape[1]
    capacity = max(2, 2 * site_count // domains)
    half_width = width // halves
    half_inner = inner // halves
    in_cols = lax.dynamic_slice_in_dim(w_in, feat_index * half_width, half_width, 1)
    first_rows = w_node1[:width]
    second_rows = w_node1[width:]
    down_rows = lax.dynamic_slice_in_dim(w_node2, feat_index * half_inner, half_inner, 0)
    out_rows = lax.dynamic_slice_in_dim(w_out, feat_index * half_width, half_width, 0)
    embedded = jnp.dot(increments, in_cols, preferred_element_type=jnp.float32).astype(jnp.bfloat16)
    latent = (jnp.sum(embedded[grid_edges].astype(jnp.float32), axis=1) / grid_degree).astype(
        jnp.bfloat16
    )
    outgoing = latent[send_rows[0]]
    incoming = lax.all_to_all(outgoing, "dom", split_axis=0, concat_axis=0, tiled=True)
    extended = jnp.concatenate([latent, incoming.reshape(domains * halo_depth, half_width)], axis=0)
    edge_weight = mesh_mask.astype(jnp.float32)
    aggregate = jnp.sum(
        extended[mesh_edges].astype(jnp.float32) * edge_weight[:, :, None], axis=1
    ).astype(jnp.bfloat16)
    first_part = lax.dynamic_slice_in_dim(first_rows, feat_index * half_inner, half_inner, 1)
    second_part = lax.dynamic_slice_in_dim(second_rows, feat_index * half_inner, half_inner, 1)
    full_latent, full_aggregate = (
        lax.all_gather(latent, "feat", axis=1, tiled=True),
        lax.all_gather(aggregate, "feat", axis=1, tiled=True),
    )
    pre = jnp.dot(full_latent, first_part, preferred_element_type=jnp.float32) + jnp.dot(
        full_aggregate, second_part, preferred_element_type=jnp.float32
    )
    hidden = jax.nn.silu(pre).astype(jnp.bfloat16)
    mixed = lax.psum_scatter(
        jnp.dot(hidden, down_rows, preferred_element_type=jnp.float32),
        "feat",
        scatter_dimension=1,
        tiled=True,
    )
    latent_next = (latent.astype(jnp.float32) + mixed).astype(jnp.bfloat16)
    owner = site_owner[:, 0]
    member = (owner[:, None] == jnp.arange(domains, dtype=jnp.int32)[None, :]).astype(jnp.int32)
    before = jnp.cumsum(member, axis=0) - member
    rank = jnp.sum(before * member, axis=1)
    slot = owner * capacity + rank
    obs_buffer = jnp.zeros((domains * capacity, variables), jnp.bfloat16).at[slot].set(site_obs)
    node_buffer = (
        jnp.full((domains * capacity, site_degree), -1, jnp.int32).at[slot].set(site_nodes)
    )
    recv_obs, recv_nodes = (
        lax.all_to_all(
            obs_buffer.reshape(domains, capacity, variables),
            "dom",
            split_axis=0,
            concat_axis=0,
            tiled=True,
        ),
        lax.all_to_all(
            node_buffer.reshape(domains, capacity, site_degree),
            "dom",
            split_axis=0,
            concat_axis=0,
            tiled=True,
        ),
    )
    recv_obs = recv_obs.reshape(domains * capacity, variables)
    recv_nodes = recv_nodes.reshape(domains * capacity, site_degree)
    valid = (recv_nodes[:, 0:1] >= 0).astype(jnp.float32)
    node_index = jnp.maximum(recv_nodes, 0)
    pooled = jnp.sum(latent_next[node_index].astype(jnp.float32), axis=1).astype(jnp.bfloat16)
    values = lax.psum(jnp.dot(pooled, out_rows, preferred_element_type=jnp.float32), "feat")
    returned_values = lax.all_to_all(
        values.astype(jnp.bfloat16).reshape(domains, capacity, variables),
        "dom",
        split_axis=0,
        concat_axis=0,
        tiled=True,
    )
    site_pred = returned_values.reshape(domains * capacity, variables)[slot]
    diff = ((values - recv_obs.astype(jnp.float32)) * valid).astype(jnp.bfloat16)
    pool_grad = jnp.dot(diff, out_rows.T, preferred_element_type=jnp.float32) * valid
    spread_sites = jnp.broadcast_to(
        pool_grad[:, None, :], (domains * capacity, site_degree, half_width)
    ).reshape(-1, half_width)
    next_grad = jax.ops.segment_sum(spread_sites, node_index.reshape(-1), num_segments=mesh_rows)
    full_grad = lax.all_gather(next_grad.astype(jnp.bfloat16), "feat", axis=1, tiled=True)
    slope = jnp.dot(full_grad, down_rows.T, preferred_element_type=jnp.float32)
    inner_grad = (slope * silu_slope(pre)).astype(jnp.bfloat16)
    own_part = jnp.dot(inner_grad, first_part.T, preferred_element_type=jnp.float32)
    agg_part = jnp.dot(inner_grad, second_part.T, preferred_element_type=jnp.float32)
    own_grad, agg_grad = (
        lax.psum_scatter(own_part, "feat", scatter_dimension=1, tiled=True),
        lax.psum_scatter(agg_part, "feat", scatter_dimension=1, tiled=True),
    )
    spread_edges = (agg_grad[:, None, :] * edge_weight[:, :, None]).reshape(-1, half_width)
    ext_grad = jax.ops.segment_sum(
        spread_edges, mesh_edges.reshape(-1), num_segments=mesh_rows + domains * halo_depth
    )
    back_halo = lax.all_to_all(
        ext_grad[mesh_rows:].reshape(domains, halo_depth, half_width),
        "dom",
        split_axis=0,
        concat_axis=0,
        tiled=True,
    )
    latent_grad = next_grad + own_grad + ext_grad[:mesh_rows]
    latent_grad = latent_grad + jax.ops.segment_sum(
        back_halo.reshape(-1, half_width), send_rows[0].reshape(-1), num_segments=mesh_rows
    )
    spread_grid = jnp.broadcast_to(
        (latent_grad / grid_degree)[:, None, :], (mesh_rows, grid_degree, half_width)
    ).reshape(-1, half_width)
    emb_grad = jax.ops.segment_sum(
        spread_grid, grid_edges.reshape(-1), num_segments=grid_rows
    ).astype(jnp.bfloat16)
    grad_part = jnp.dot(emb_grad, in_cols.T, preferred_element_type=jnp.float32)
    grad_grid = lax.psum_scatter(grad_part, "feat", scatter_dimension=1, tiled=True)
    return (grad_grid, site_pred)


def solution(mesh):
    return jax.shard_map(
        local,
        mesh=mesh,
        in_specs=(
            P("dom", None),
            P(),
            P(),
            P(),
            P(),
            P("dom", None),
            P("dom", None),
            P("dom", None),
            P("dom", None, None),
            P("dom", None),
            P("dom", None),
            P("dom", None),
        ),
        out_specs=(P("dom", "feat"), P("dom", None)),
        check_vma=False,
    )
```

profile of v0, /device:TPU:1, one launch (start us, length us, event | category | flops | bytes accessed | tf_op | source)
XLA Modules:
  0.0 382.1 jit_solution(13720070078227209747)
XLA Ops:
  11.3 15.0 %gather_fusion = bf16[4096,128]{1,0:T(8,128)(2,1)} fusion(bf16[4096,128]{1,0:T(8,128)(2,1)S(1)} %copy.35, s32[4096]{0:T(1024)S(1)} %broadcast_clamp_fusion.2), kind=kCustom, calls=%fused_computation | custom fusion | bytes 2113536 | tf_op jit(solution)/shard_map/gather | solution.py:47
  29.1 8.0 %gather_fusion.1 = bf16[2048,128]{1,0:T(8,128)(2,1)} fusion(bf16[1024,128]{1,0:T(8,128)(2,1)S(1)} %multiply_convert_fusion.1, s32[2048]{0:T(1024)S(1)} %broadcast_clamp_fusion.3), kind=kCustom, calls=%fused_computation.1 | custom fusion | bytes 1056768 | tf_op jit(solution)/shard_map/gather | solution.py:50
  37.0 16.3 %all-to-all-start.1 = ((bf16[128,16,128]{2,1,0:T(8,128)(2,1)}), bf16[128,16,128]{2,1,0:T(8,128)(2,1)S(1)}, u32[]{:S(2)}, u32[]{:S(2)}) async-start(bf16[128,16,128]{2,1,0:T(8,128)(2,1)} %bitcast.11), calls=%async_computation.1 | async-start | bytes 1048576 | tf_op jit(solution)/shard_map/all_to_all | solution.py:51
  61.9 10.6 %all-to-all-done.1 = bf16[128,16,128]{2,1,0:T(8,128)(2,1)S(1)} async-done(((bf16[128,16,128]{2,1,0:T(8,128)(2,1)}), bf16[128,16,128]{2,1,0:T(8,128)(2,1)S(1)}, u32[]{:S(2)}, u32[]{:S(2)}) %all-to-all-start.1) | async-done | bytes 524320 | tf_op jit(solution)/shard_map/all_to_all | solution.py:51
  74.4 22.1 %gather_fusion.2 = bf16[6144,128]{1,0:T(8,128)(2,1)} fusion(bf16[3072,128]{1,0:T(8,128)(2,1)S(1)} %pad_maximum_fusion, s32[6144]{0:T(1024)S(1)} %broadcast_clamp_fusion), kind=kCustom, calls=%fused_computation.2 | custom fusion | bytes 3170304 | tf_op jit(solution)/shard_map/gather | solution.py:55
  96.5 4.0 %reshape.226 = f32[1024,6,128]{2,1,0:T(8,128)} reshape(bf16[6144,128]{1,0:T(8,128)(2,1)} %gather_fusion.2) | data formatting | bytes 4718592 | tf_op jit(solution)/shard_map/convert_element_type | solution.py:55
  100.5 7.2 %multiply_reduce_fusion = bf16[1024,128]{1,0:T(8,128)(2,1)S(1)} fusion(f32[1024,6,128]{2,1,0:T(8,128)} %reshape.226, f32[1024,6]{1,0:T(8,128)S(1)} %copy.38), kind=kLoop, calls=%fused_computation.13 | loop fusion | flops 1441792 | bytes 3432448 | tf_op jit(solution)/shard_map/reduce_sum | solution.py:54
  107.7 4.4 %all_gather.10 = bf16[1024,256]{1,0:T(8,128)(2,1)S(1)} all-gather(bf16[1024,128]{1,0:T(8,128)(2,1)S(1)} %multiply_reduce_fusion), channel_id=1, replica_groups=mesh['dom'=128,'feat'=2] {'feat'}, dimensions={1}, use_global_device_ids=true | all-gather | bytes 786432 | tf_op jit(solution)/shard_map/all_gather | solution.py:61
  116.9 20.1 %all_to_all.25 = s32[128,4,8]{2,1,0:T(4,128)S(1)} all-to-all(s32[128,4,8]{2,1,0:T(4,128)S(1)} %bitcast.57), channel_id=1, replica_groups=mesh['dom'=128,'feat'=2] {'dom'}, dimensions={0} | all-to-all | bytes 32768 | tf_op jit(solution)/shard_map/all_to_all | solution.py:91
  138.5 15.0 %gather_fusion.3 = bf16[4096,128]{1,0:T(8,128)(2,1)} fusion(bf16[1024,128]{1,0:T(8,128)(2,1)S(1)} %add_convert_fusion, s32[4096]{0:T(1024)S(1)} %broadcast_clamp_fusion.1), kind=kCustom, calls=%fused_computation.3 | custom fusion | bytes 2113536 | tf_op jit(solution)/shard_map/gather | solution.py:103
  158.5 6.1 %all-to-all-start.2 = ((bf16[128,4,128]{2,1,0:T(4,128)(2,1)}), bf16[128,4,128]{2,1,0:T(4,128)(2,1)S(1)}, u32[]{:S(2)}, u32[]{:S(2)}) async-start(bf16[128,4,128]{2,1,0:T(4,128)(2,1)} %bitcast.14), calls=%async_computation.3 | async-start | bytes 262144 | tf_op jit(solution)/shard_map/all_to_all | solution.py:84
  164.8 11.2 %all-to-all-done.2 = bf16[128,4,128]{2,1,0:T(4,128)(2,1)S(1)} async-done(((bf16[128,4,128]{2,1,0:T(4,128)(2,1)}), bf16[128,4,128]{2,1,0:T(4,128)(2,1)S(1)}, u32[]{:S(2)}, u32[]{:S(2)}) %all-to-all-start.2) | async-done | bytes 131104 | tf_op jit(solution)/shard_map/all_to_all | solution.py:84
  176.1 4.1 %all-reduce.2.cloned.1.call-done = f32[512,128]{1,0:T(8,128)} async-done(((f32[512,128]{1,0:T(8,128)}), f32[512,128]{1,0:T(8,128)}) %all-reduce.2.cloned.1.call-update) | async-done | bytes 262160 | tf_op jit(solution)/shard_map/psum | solution.py:104
  181.4 22.6 %scatter_custom_fusion.2 = f32[1024,128]{1,0:T(8,128)S(1)} fusion(s32[4096]{0:T(1024)S(1)} %reshape.184, f32[512,128]{1,0:T(8,128)S(1)} %convolution_multiply_fusion.1, f32[]{:T(128)} %constant.14.clone.1), kind=kCustom, calls=%fused_computation.17 | custom fusion | flops 524288 | bytes 786436 | tf_op jit(solution)/shard_map/scatter-add | solution.py:118
  212.0 13.9 %reduce-scatter.9.cloned.1.call-done = f32[1024,128]{1,0:T(8,128)} async-done(((f32[1024,256]{1,0:T(8,128)}), f32[1024,128]{1,0:T(8,128)}) %reduce-scatter.9.cloned.1.call-update) | async-done | bytes 524304 | tf_op jit(solution)/shard_map/reduce_scatter | solution.py:126
  225.8 3.2 mul.93
  229.1 4.6 %mul.94 = f32[6144,128]{1,0:T(8,128)} reshape(f32[1024,6,128]{2,1,0:T(8,128)} %mul.93) | data formatting | bytes 6291456 | tf_op jit(solution)/shard_map/mul | solution.py:128
  233.7 37.0 %scatter_custom_fusion.3 = f32[3072,128]{1,0:T(8,128)S(1)} fusion(s32[6144]{0:T(1024)S(1)} %reshape.192, f32[6144,128]{1,0:T(8,128)} %mul.94, f32[6144]{0:T(1024)S(1)} %mul.95, f32[]{:T(128)} %constant.14.clone.1), kind=kCustom, calls=%fused_computation.14 | custom fusion | flops 1572864 | bytes 4743172 | tf_op jit(solution)/shard_map/scatter-add | solution.py:129
  271.8 14.1 %all-to-all-start.3 = ((f32[128,16,128]{2,1,0:T(8,128)}), f32[128,16,128]{2,1,0:T(8,128)}, u32[]{:S(2)}, u32[]{:S(2)}) async-start(f32[128,16,128]{2,1,0:T(8,128)} %bitcast.52), calls=%async_computation.6 | async-start | bytes 2097152 | tf_op jit(solution)/shard_map/all_to_all | solution.py:132
  288.0 28.4 %all-to-all-done.3 = f32[128,16,128]{2,1,0:T(8,128)} async-done(((f32[128,16,128]{2,1,0:T(8,128)}), f32[128,16,128]{2,1,0:T(8,128)}, u32[]{:S(2)}, u32[]{:S(2)}) %all-to-all-start.3) | async-done | bytes 1048608 | tf_op jit(solution)/shard_map/all_to_all | solution.py:132
  316.4 12.0 %scatter_fusion = f32[1024,128]{1,0:T(8,128)S(1)} fusion(f32[1024,128]{1,0:T(8,128)S(1)} %slice_add_fusion, s32[2048]{0:T(1024)S(1)} %reshape.200, f32[2048,128]{1,0:T(8,128)} %bitcast.19), kind=kCustom, calls=%fused_computation.9 | custom fusion | flops 262144 | bytes 3153920 | tf_op jit(solution)/shard_map/scatter-add | solution.py:140
  330.2 23.2 %scatter_custom_fusion.5 = f32[4096,128]{1,0:T(8,128)S(1)} fusion(s32[4096]{0:T(1024)S(1)} %reshape.208, f32[4096,128]{1,0:T(8,128)} %bitcast.55, f32[]{:T(128)} %constant.14.clone.1), kind=kCustom, calls=%fused_computation.30 | custom fusion | flops 524288 | bytes 2097664 | tf_op jit(solution)/shard_map/scatter-add | solution.py:146
  356.8 6.2 %all-to-all-start.4 = ((bf16[128,4,128]{2,1,0:T(4,128)(2,1)}), bf16[128,4,128]{2,1,0:T(4,128)(2,1)S(1)}, u32[]{:S(2)}, u32[]{:S(2)}) async-start(bf16[128,4,128]{2,1,0:T(4,128)(2,1)} %bitcast.21), calls=%async_computation.8 | async-start | bytes 262144 | tf_op jit(solution)/shard_map/all_to_all | solution.py:105
  363.0 11.1 %all-to-all-done.4 = bf16[128,4,128]{2,1,0:T(4,128)(2,1)S(1)} async-done(((bf16[128,4,128]{2,1,0:T(4,128)(2,1)}), bf16[128,4,128]{2,1,0:T(4,128)(2,1)S(1)}, u32[]{:S(2)}, u32[]{:S(2)}) %all-to-all-start.4) | async-done | bytes 131104 | tf_op jit(solution)/shard_map/all_to_all | solution.py:105
  (112 shorter events, 47.2 us)
Async XLA Ops:
  7.2 2.2 copy-start
  29.0 24.4 %copy-start.13 = (s32[1024,6]{0,1:T(8,128)S(1)}, s32[1024,6]{0,1:T(8,128)}, u32[]{:S(2)}) copy-start(s32[1024,6]{0,1:T(8,128)} %param.19) | copy-start | bytes 73732
  29.0 24.6 %copy-start.8 = (s32[1024,6]{0,1:T(8,128)S(1)}, s32[1024,6]{0,1:T(8,128)}, u32[]{:S(2)}) copy-start(s32[1024,6]{0,1:T(8,128)} %param.18) | copy-start | bytes 73732
  37.0 35.5 %all-to-all-start.1 = ((bf16[128,16,128]{2,1,0:T(8,128)(2,1)}), bf16[128,16,128]{2,1,0:T(8,128)(2,1)S(1)}, u32[]{:S(2)}, u32[]{:S(2)}) async-start(bf16[128,16,128]{2,1,0:T(8,128)(2,1)} %bitcast.11), calls=%async_computation.1 | async-start | bytes 1048576 | tf_op jit(solution)/shard_map/all_to_all | solution.py:51
  53.4 84.0 %reduce-scatter.5.cloned.1.call-start = ((), (), s32[]{:S(2)}) async-start(), calls=%async_computation.9 | async-start | bytes 1572864 | tf_op jit(solution)/shard_map/reduce_scatter | solution.py:67
  100.5 11.7 %copy-start.2 = (f32[1024,256]{1,0:T(8,128)S(1)}, f32[1024,256]{1,0:T(8,128)}, u32[]{:S(2)}) copy-start(f32[1024,256]{1,0:T(8,128)} %fusion.32) | copy-start | bytes 3145732
  100.5 11.7 %copy-start.6 = (bf16[256,512]{1,0:T(8,128)(2,1)S(1)}, bf16[256,512]{1,0:T(8,128)(2,1)}, u32[]{:S(2)}) copy-start(bf16[256,512]{1,0:T(8,128)(2,1)} %get-tuple-element.2) | copy-start | bytes 786436
  107.7 5.8 %copy-start.16 = (bf16[512,256]{1,0:T(8,128)(2,1)S(1)}, bf16[512,256]{1,0:T(8,128)(2,1)}, u32[]{:S(2)}) copy-start(bf16[512,256]{1,0:T(8,128)(2,1)} %param.15) | copy-start | bytes 786436
  112.4 1.0 copy-start.4
  113.4 1.5 copy-start.14
  113.4 1.9 copy-start.15
  114.9 65.3 %all-reduce.2.cloned.1.call-start = ((), (), s32[]{:S(2)}) async-start(), calls=%async_computation.10 | async-start | bytes 524288 | tf_op jit(solution)/shard_map/psum | solution.py:104
  138.5 17.0 %copy-start.11 = (bf16[256,128]{1,0:T(8,128)(2,1)S(1)}, bf16[256,128]{1,0:T(8,128)(2,1)}, u32[]{:S(2)}) copy-start(bf16[256,128]{1,0:T(8,128)(2,1)} %param.16) | copy-start | bytes 196612
  158.5 17.6 %all-to-all-start.2 = ((bf16[128,4,128]{2,1,0:T(4,128)(2,1)}), bf16[128,4,128]{2,1,0:T(4,128)(2,1)S(1)}, u32[]{:S(2)}, u32[]{:S(2)}) async-start(bf16[128,4,128]{2,1,0:T(4,128)(2,1)} %bitcast.14), calls=%async_computation.3 | async-start | bytes 262144 | tf_op jit(solution)/shard_map/all_to_all | solution.py:84
  164.7 61.2 %reduce-scatter.9.cloned.1.call-start = ((), (), s32[]{:S(2)}) async-start(), calls=%async_computation.12 | async-start | bytes 1572864 | tf_op jit(solution)/shard_map/reduce_scatter | solution.py:126
  204.0 4.1 %copy-start.1 = (f32[1024,128]{1,0:T(8,128)}, f32[1024,128]{1,0:T(8,128)S(1)}, u32[]{:S(2)}) copy-start(f32[1024,128]{1,0:T(8,128)S(1)} %scatter_custom_fusion.2) | copy-start | bytes 1572868
  206.2 1.9 copy-start.7
  209.4 77.3 %reduce-scatter.7.cloned.1.call-start = ((), (), s32[]{:S(2)}) async-start(), calls=%async_computation.11 | async-start | bytes 1572864 | tf_op jit(solution)/shard_map/reduce_scatter | solution.py:125
  270.7 15.2 %copy-start.12 = (s32[1,128,16]{1,2,0:T(8,128)S(1)}, s32[1,128,16]{1,2,0:T(8,128)}, u32[]{:S(2)}) copy-start(s32[1,128,16]{1,2,0:T(8,128)} %param.20) | copy-start | bytes 24580
  270.8 15.3 %copy-start.10 = (s32[1024,4]{0,1:T(4,128)S(1)}, s32[1024,4]{0,1:T(4,128)}, u32[]{:S(2)}) copy-start(s32[1024,4]{0,1:T(4,128)} %param.17) | copy-start | bytes 49156
  271.8 44.6 %all-to-all-start.3 = ((f32[128,16,128]{2,1,0:T(8,128)}), f32[128,16,128]{2,1,0:T(8,128)}, u32[]{:S(2)}, u32[]{:S(2)}) async-start(f32[128,16,128]{2,1,0:T(8,128)} %bitcast.52), calls=%async_computation.6 | async-start | bytes 2097152 | tf_op jit(solution)/shard_map/all_to_all | solution.py:132
  285.9 89.6 %reduce-scatter.11.cloned.1.call-start = ((), (), s32[]{:S(2)}) async-start(), calls=%async_computation.13 | async-start | bytes 3145728 | tf_op jit(solution)/shard_map/reduce_scatter | solution.py:150
  328.4 24.9 %copy-start.9 = (bf16[128,256]{1,0:T(8,128)(2,1)S(1)}, bf16[128,256]{1,0:T(8,128)(2,1)}, u32[]{:S(2)}) copy-start(bf16[128,256]{1,0:T(8,128)(2,1)} %param.13) | copy-start | bytes 196612
  356.8 17.3 %all-to-all-start.4 = ((bf16[128,4,128]{2,1,0:T(4,128)(2,1)}), bf16[128,4,128]{2,1,0:T(4,128)(2,1)S(1)}, u32[]{:S(2)}, u32[]{:S(2)}) async-start(bf16[128,4,128]{2,1,0:T(4,128)(2,1)} %bitcast.21), calls=%async_computation.8 | async-start | bytes 262144 | tf_op jit(solution)/shard_map/all_to_all | solution.py:105
  (2 other events, 1.7 us)
Sparse Core Ops, SparseCore 0:
  115.0 6.9 reduce-scatter.4
  156.5 23.6 all-reduce.1
  209.6 16.2 reduce-scatter.8
  228.2 15.0 reduce-scatter.6
  355.3 9.3 reduce-scatter.10
where the time goes:
time: 384 us; the launch traced here: 382 us
  other arithmetic  113 us (29%)
  local copies, waits for them, and re-layouts  90.1 us (23%)
  waiting for transfers between devices  79.4 us (21%)
  starting transfers between devices  43.2 us (11%)
  blocking collectives  29.6 us (8%)
  between operations  14.3 us (4%)
  matrix products  12.5 us (3%)
    scatter-add x1, other arithmetic, local(): jax.ops.segment_sum(spread_edges, mesh_edges.reshape(-1), num_segments=me...  37 us
    all_to_all x1, waiting for transfers between devices, local(): lax.all_to_all(ext_grad[mesh_rows:].reshape(domains, halo_depth, half_wid...  28.4 us
    scatter-add x1, other arithmetic, local(): jax.ops.segment_sum(spread_grid, grid_edges.reshape(-1), num_segments=gri...  23.2 us
    scatter-add x1, other arithmetic, local(): jax.ops.segment_sum(spread_sites, node_index.reshape(-1), num_segments=me...  22.6 us
    gather x1, local copies, waits for them, and re-layouts, local(): extended[mesh_edges].astype(jnp.float32) * edge_weight[:, :, None]  22.1 us
    all_to_all x1, blocking collectives, local(): lax.all_to_all(node_buffer.reshape(domains, capacity, site_degree), 'dom'...  20.1 us
    all_to_all x1, starting transfers between devices, local(): lax.all_to_all(outgoing, 'dom', split_axis=0, concat_axis=0, tiled=True)  16.3 us
    gather x1, local copies, waits for them, and re-layouts, local(): embedded[grid_edges].astype(jnp.float32)  15 us
  transfers between devices with their start and end apart: 9, of which 6 were waited for; matrix products, arithmetic and copies ran while one was open for 16% of the time, Pallas kernels for 0%

commit v1 on v0

v1 whole, which is shorter than its diff:
```python
import jax
import jax.numpy as jnp
from jax import lax
from jax.experimental import pallas as pl
from jax.experimental.pallas import tpu as pltpu
from jax.sharding import PartitionSpec as P

BF = jnp.bfloat16
F32 = jnp.float32
I16 = jnp.int16
I32 = jnp.int32
LANES = 128
HALF_DEPTH = 8
SLOTS = 4
ROWS = HALF_DEPTH + SLOTS
SWAP = [(0, 1), (1, 0)]


def dot(a, b, ca=1, cb=0):
    return lax.dot_general(a, b, (((ca,), (cb,)), ((), ())), preferred_element_type=F32)


def iota(shape, axis):
    return lax.broadcasted_iota(I32, shape, axis)


def eq_bf16(a, b):
    return jnp.where(a == b, jnp.asarray(1, BF), jnp.asarray(0, BF))


def build_counts(dst, load, rows, width, degree, block=64, row0=0):
    start = iota((block, LANES), 1).astype(I16)

    def row_body(i, carry):
        s = pl.multiple_of(i * block, block)
        a = load(s, block)
        cols = [
            jnp.broadcast_to(a[:, k : k + 1], (block, LANES)).astype(I16) for k in range(degree)
        ]

        def lane_body(w, lanes):
            acc = eq_bf16(cols[0], lanes)
            for k in range(1, degree):
                acc = acc + eq_bf16(cols[k], lanes)
            dst[pl.ds(row0 + s, block), pl.ds(pl.multiple_of(w * LANES, LANES), LANES)] = acc
            return lanes + jnp.asarray(LANES, I16)

        lax.fori_loop(0, width // LANES, lane_body, start, unroll=2)
        return carry

    lax.fori_loop(0, rows // block, row_body, 0)


def place_matrix(rows, cols, transposed):
    shape = (cols, rows) if transposed else (rows, cols)
    r_axis, c_axis = (1, 0) if transposed else (0, 1)
    c = iota(shape, c_axis)
    want = (c & 127) * ROWS + HALF_DEPTH + (c >> 7)
    return jnp.where(iota(shape, r_axis) == want, 1.0, 0.0).astype(BF)


def send_index(feat, send, rows):
    peers = send.shape[0]
    picked = jnp.where(feat == 0, send[:, :HALF_DEPTH], send[:, HALF_DEPTH:])
    peer = iota((peers, 1), 0)
    table = jnp.concatenate([picked >> 5, picked & 31, peer], axis=1).astype(F32).astype(BF)
    row = iota((rows, peers), 0)
    first = iota((rows, peers), 1) * ROWS
    spread = jnp.where((row >= first) & (row < first + ROWS), 1.0, 0.0).astype(BF)
    out = dot(spread, table)
    node = out[:, :HALF_DEPTH] * 32.0 + out[:, HALF_DEPTH : 2 * HALF_DEPTH]
    within = iota((rows, 1), 0).astype(F32) - out[:, 2 * HALF_DEPTH :] * ROWS
    hit = iota((rows, HALF_DEPTH), 1).astype(F32) == within
    index = jnp.sum(jnp.where(hit, node, 0.0), axis=1, keepdims=True)
    return jnp.where(within >= HALF_DEPTH, -1.0, index).astype(I32)


def encode_kernel(
    feat_ref, inc, edges, send, owner, nodes, obs, msg, ginc, target, g_s, r_s, idx_s
):
    feat = feat_ref[0]
    rows = msg.shape[0]
    build_counts(g_s, lambda s, b: edges[pl.ds(s, b), :], ginc.shape[0], inc.shape[0], edges.shape[1])
    idx_s[...] = send_index(feat, send[...], rows)
    build_counts(r_s, lambda s, b: idx_s[pl.ds(s, b), :], rows, ginc.shape[0], 1)
    sites = owner.shape[0]
    own = owner[...]
    member = jnp.where(own == iota((sites, LANES), 1), 1.0, 0.0)
    member_b = member.astype(BF)
    lower = jnp.where(iota((sites, sites), 1) < iota((sites, sites), 0), 1.0, 0.0).astype(BF)
    rank = jnp.sum(dot(lower, member_b) * member, axis=1, keepdims=True)
    target[...] = own * ROWS + HALF_DEPTH + rank.astype(I32)
    slot0 = (2 * feat).astype(F32)
    obs_0 = dot(jnp.where(rank == slot0, member, 0.0).astype(BF), obs[...], 0, 0)
    obs_1 = dot(jnp.where(rank == slot0 + 1.0, member, 0.0).astype(BF), obs[...], 0, 0)
    degree = nodes.shape[1]
    lane = iota((sites, LANES), 1)
    mine = (lane >> 3).astype(F32) == rank
    tile = jnp.where((iota((degree, LANES), 1) & 7) == iota((degree, LANES), 0), 1.0, 0.0).astype(BF)
    n = nodes[...]
    high = dot(((n >> 5) + 1).astype(F32).astype(BF), tile)
    low = dot((n & 31).astype(F32).astype(BF), tile)
    n_high = dot(member_b, jnp.where(mine, high, 0.0).astype(BF), 0, 0)
    n_low = dot(member_b, jnp.where(mine, low, 0.0).astype(BF), 0, 0)
    packed = jnp.concatenate([obs_0, obs_1, n_high, n_low], axis=0).astype(BF)
    site_rows = dot(place_matrix(rows, SLOTS * LANES, False), packed)
    mean = (dot(g_s[...], inc[...]) * (1.0 / edges.shape[1])).astype(BF)
    ginc[...] = mean
    msg[...] = (dot(r_s[...], mean) + site_rows).astype(BF)


def prepare_kernel(
    feat_ref, edges, mask, w_in, w_node1, w_node2, w_out, m_out, w_cat, w_ho, w_io, idx_s
):
    feat = feat_ref[0]
    rows = edges.shape[0]
    half = rows // 2
    e = edges[...]
    own_col = e - feat * half
    h = e - rows
    r = h & 15
    halo_col = half + (h >> 4) * ROWS + (r & 7)
    is_own = (e < rows) & (own_col >= 0) & (own_col < half)
    is_halo = (e >= rows) & ((r >> 3) == feat)
    col = jnp.where(is_own, own_col, jnp.where(is_halo, halo_col, -1))
    idx_s[...] = jnp.where(mask[...] > 0, col, -1)
    build_counts(m_out, lambda s, b: idx_s[pl.ds(s, b), :], rows, m_out.shape[1], edges.shape[1])
    width = w_in.shape[1]
    variables = w_in.shape[0]
    wi = w_in[...]
    w_cat[:variables, :] = dot(wi, w_node1[:width, :]).astype(BF)
    w_cat[variables:, :] = dot(wi, w_node1[width:, :]).astype(BF)
    w_ho[...] = dot(w_node2[...], w_out[...]).astype(BF)
    w_io[...] = dot(wi, w_out[...]).astype(BF)


def mix_kernel(feat_ref, msg, ginc, m, part, node):
    feat = feat_ref[0]
    rows = ginc.shape[0]
    half = rows // 2
    own = ginc[pl.ds(pl.multiple_of(feat * half, half), half), :]
    part[:rows, :] = (dot(m[:, :half], own) + dot(m[:, half:], msg[...])).astype(BF)
    got = dot(place_matrix(msg.shape[0], SLOTS * LANES, True), msg[...])
    part[rows:, :] = got[: 2 * LANES, :].astype(BF)
    node[...] = ((got[2 * LANES : 3 * LANES, :] - 1.0) * 32.0 + got[3 * LANES :, :]).astype(I32)


def site_kernel(node, s_out):
    degree = 8
    for slot in range(SLOTS):
        build_counts(
            s_out,
            lambda s, b, slot=slot: node[pl.ds(s, b), slot * degree : (slot + 1) * degree],
            LANES,
            s_out.shape[1],
            degree,
            row0=slot * LANES,
        )


def node_kernel(
    feat_ref, part, other, ginc, m, s, w_cat, w_ho, w_io, msg, own_t, ext_t, slope_s
):
    feat = feat_ref[0]
    rows, variables = ginc.shape
    half = rows // 2
    gi = ginc[...]
    agg = (part[:rows, :].astype(F32) + other[:rows, :].astype(F32)).astype(BF)
    pre = dot(gi, w_cat[:variables, :]) + dot(agg, w_cat[variables:, :])
    sig = 1.0 / (1.0 + jnp.exp(-pre))
    hidden = (pre * sig).astype(BF)
    slope_s[...] = sig * (1.0 + pre * (1.0 - sig))
    readout = (dot(hidden, w_ho[...]) + dot(gi, w_io[...])).astype(BF)
    sites = s[...]
    values = dot(sites, readout)
    mine = part[rows:, :].astype(F32)
    theirs = other[rows:, :].astype(F32)
    first = jnp.where(feat == 0, mine, theirs)
    second = jnp.where(feat == 0, theirs, mine)
    diff = (values - jnp.concatenate([first, second], axis=0)).astype(BF)
    d_t = dot(diff, sites, 0, 0).astype(BF)
    d = d_t.T
    inner = (dot(d, w_ho[...], 1, 1) * slope_s[...]).astype(BF)
    cols = pl.ds(pl.multiple_of(feat * (variables // 2), variables // 2), variables // 2)
    own_t[...] = dot(w_io[cols, :], d_t) + dot(w_cat[cols, :], inner, 1, 1)
    agg_t = dot(w_cat[variables:, :], inner, 1, 1).astype(BF)
    ext = dot(agg_t, m[...])
    ext_t[...] = ext[:, :half]
    site_rows = dot(place_matrix(msg.shape[0], SLOTS * LANES, False), values.astype(BF))
    msg[...] = (ext[:, half:].T + site_rows).astype(BF)


def scatter_kernel(feat_ref, edges, send, g_out, r_out, idx_s):
    build_counts(
        g_out, lambda s, b: edges[pl.ds(s, b), :], g_out.shape[0], g_out.shape[1], edges.shape[1]
    )
    idx_s[...] = send_index(feat_ref[0], send[...], r_out.shape[0])
    build_counts(r_out, lambda s, b: idx_s[pl.ds(s, b), :], r_out.shape[0], r_out.shape[1], 1)


def return_kernel(feat_ref, msg, r, ext_t, own_t, target, keep, give, pred, part_s):
    feat = feat_ref[0]
    back = msg[...]
    half = ext_t.shape[1]
    part = dot(back, r[...], 0, 0)
    e = ext_t[...]
    lane = iota(part.shape, 1)
    inside = (lane >= feat * half) & (lane < feat * half + half)
    part_s[...] = part + jnp.where(inside, jnp.concatenate([e, e], axis=1), 0.0)
    n = keep.shape[0]
    keep[...] = part_s[pl.ds(pl.multiple_of(feat * n, n), n), :] + own_t[...]
    give[...] = part_s[pl.ds(pl.multiple_of((1 - feat) * n, n), n), :].astype(BF)
    pick = jnp.where(target[...] == iota((target.shape[0], msg.shape[0]), 1), 1.0, 0.0).astype(BF)
    pred[...] = dot(pick, back).astype(BF)


def grid_kernel(keep, got, g, out, *, degree):
    lg = ((keep[...] + got[...].astype(F32)) * (1.0 / degree)).astype(BF)
    out[...] = dot(lg, g[...]).T


SCALAR = pl.BlockSpec(memory_space=pltpu.SMEM)
FULL = pl.BlockSpec(memory_space=pltpu.VMEM)


def call(kernel, outs, args, scratch=(), scalar=True, name=None):
    return pl.pallas_call(
        kernel,
        out_shape=[jax.ShapeDtypeStruct(s, t) for s, t in outs],
        in_specs=([SCALAR] if scalar else []) + [FULL] * (len(args) - bool(scalar)),
        out_specs=[FULL] * len(outs),
        scratch_shapes=list(scratch),
        name=name,
    )(*args)


def exchange(msg, domains):
    x = msg.reshape(domains, ROWS // 4, 4, msg.shape[1])
    x = lax.all_to_all(x, "dom", split_axis=0, concat_axis=0, tiled=True)
    return x.reshape(msg.shape)


def local(
    increments,
    w_in,
    w_node1,
    w_node2,
    w_out,
    grid_edges,
    mesh_edges,
    mesh_mask,
    send_rows,
    site_owner,
    site_nodes,
    site_obs,
):
    domains = lax.axis_size("dom")
    feat = lax.axis_index("feat").astype(I32).reshape(1)
    grid_rows, variables = increments.shape
    mesh_rows = mesh_edges.shape[0]
    inner = w_node2.shape[0]
    site_count = site_obs.shape[0]
    half = mesh_rows // 2
    rows = domains * ROWS
    send = send_rows[0]
    msg, ginc, target = call(
        encode_kernel,
        [((rows, variables), BF), ((mesh_rows, variables), BF), ((site_count, 1), I32)],
        (feat, increments, grid_edges, send, site_owner, site_nodes, site_obs),
        [
            pltpu.VMEM((mesh_rows, grid_rows), BF),
            pltpu.VMEM((rows, mesh_rows), BF),
            pltpu.VMEM((rows, 1), I32),
        ],
        name="encode",
    )
    m, w_cat, w_ho, w_io = call(
        prepare_kernel,
        [
            ((mesh_rows, half + rows), BF),
            ((2 * variables, inner), BF),
            ((inner, variables), BF),
            ((variables, variables), BF),
        ],
        (feat, mesh_edges, mesh_mask, w_in, w_node1, w_node2, w_out),
        [pltpu.VMEM(mesh_edges.shape, I32)],
        name="prepare",
    )
    got = exchange(msg, domains)
    part, node = call(
        mix_kernel,
        [((mesh_rows + 2 * LANES, variables), BF), ((LANES, LANES), I32)],
        (feat, got, ginc, m),
        name="mix",
    )
    other = lax.ppermute(part, "feat", SWAP)
    (sites,) = call(
        site_kernel, [((SLOTS * domains, mesh_rows), BF)], (node,), scalar=False, name="sites"
    )
    back, own_t, ext_t = call(
        node_kernel,
        [
            ((rows, variables), BF),
            ((variables // 2, mesh_rows), F32),
            ((variables, half), F32),
        ],
        (feat, part, other, ginc, m, sites, w_cat, w_ho, w_io),
        [pltpu.VMEM((mesh_rows, inner), F32)],
        name="node",
    )
    got_back = exchange(back, domains)
    g, r = call(
        scatter_kernel,
        [((mesh_rows, grid_rows), BF), ((rows, mesh_rows), BF)],
        (feat, grid_edges, send),
        [pltpu.VMEM((rows, 1), I32)],
        name="scatter",
    )
    keep, give, site_pred = call(
        return_kernel,
        [
            ((variables // 2, mesh_rows), F32),
            ((variables // 2, mesh_rows), BF),
            ((site_count, variables), BF),
        ],
        (feat, got_back, r, ext_t, own_t, target),
        [pltpu.VMEM((variables, mesh_rows), F32)],
        name="return",
    )
    take = lax.ppermute(give, "feat", SWAP)
    chunk = 1024
    degree = grid_edges.shape[1]

    def grid_body(keep_ref, got_ref, g_ref, out_ref):
        grid_kernel(keep_ref, got_ref, g_ref, out_ref, degree=degree)

    grad_grid = pl.pallas_call(
        grid_body,
        grid=(grid_rows // chunk,),
        out_shape=jax.ShapeDtypeStruct((grid_rows, variables // 2), F32),
        in_specs=[
            pl.BlockSpec((variables // 2, mesh_rows), lambda i: (0, 0)),
            pl.BlockSpec((variables // 2, mesh_rows), lambda i: (0, 0)),
            pl.BlockSpec((mesh_rows, chunk), lambda i: (0, i)),
        ],
        out_specs=pl.BlockSpec((chunk, variables // 2), lambda i: (i, 0)),
        name="grid",
    )(keep, take, g)
    return (grad_grid, site_pred)


def solution(mesh):
    return jax.shard_map(
        local,
        mesh=mesh,
        in_specs=(
            P("dom", None),
            P(),
            P(),
            P(),
            P(),
            P("dom", None),
            P("dom", None),
            P("dom", None),
            P("dom", None, None),
            P("dom", None),
            P("dom", None),
            P("dom", None),
        ),
        out_specs=(P("dom", "feat"), P("dom", None)),
        check_vma=False,
    )
```

time: 384 us -> 121 us (0.32)
  other arithmetic: 113 us -> 0 us
  local copies, waits for them, and re-layouts: 90.1 us -> 15 us
  waiting for transfers between devices: 79.4 us -> 7.42 us
  Pallas kernels: 0 us -> 69.5 us
  blocking collectives: 29.6 us -> 0 us
  starting transfers between devices: 43.2 us -> 28 us
  between operations: 14.3 us -> 0.67 us
  matrix products: 12.5 us -> 0 us
    scatter-add x4 -> x0, other arithmetic: 94.8 us -> none  [the longest x1 37 us: local(): jax.ops.segment_sum(spread_edges, mesh_edges.reshape(-1), num_segments=me...]
    pallas_call x0 -> x8, Pallas kernels: none -> 69.5 us  [the longest x7 63.1 us: call(): pl.pallas_call(kernel, out_shape=[jax.ShapeDtypeStruct(s, t) for s, t in...]
    gather x5 -> x0, local copies, waits for them, and re-layouts: 61.6 us -> none  [the longest x1 22.1 us: local(): extended[mesh_edges].astype(jnp.float32) * edge_weight[:, :, None]]
    all_to_all x4 -> x2, waiting for transfers between devices: 61.3 us -> 6.22 us  [exchange(): x = lax.all_to_all(x, 'dom', split_axis=0, concat_axis=0, tiled=True)]
    all_to_all x1 -> x0, blocking collectives: 20.1 us -> none  [local(): lax.all_to_all(node_buffer.reshape(domains, capacity, site_degree), 'dom'...]
    all_to_all x4 -> x2, starting transfers between devices: 42.8 us -> 23.9 us  [exchange(): x = lax.all_to_all(x, 'dom', split_axis=0, concat_axis=0, tiled=True)]
    reduce_scatter x4 -> x0, waiting for transfers between devices: 13.9 us -> none  [the longest x1 13.9 us: local(): lax.psum_scatter(agg_part, 'feat', scatter_dimension=1, tiled=True)]
    dot_general x10 -> x0, matrix products: 12.5 us -> none  [the longest x1 1.85 us: local(): slope = jnp.dot(full_grad, down_rows.T, preferred_element_type=jnp.float32)]
  transfers between devices with their start and end apart: 9 -> 4, of which waited for: 6 -> 3; matrix products, arithmetic and copies ran while one was open for 16% -> 2% of each run, Pallas kernels for 0% -> 24%
where the time goes in v1:
time: 121 us
  Pallas kernels  69.5 us (57%)
  starting transfers between devices  28 us (23%)
  local copies, waits for them, and re-layouts  15 us (12%)
  waiting for transfers between devices  7.42 us (6%)
    pallas_call x7, Pallas kernels, call(): pl.pallas_call(kernel, out_shape=[jax.ShapeDtypeStruct(s, t) for s, t in...  63.1 us
    all_to_all x2, starting transfers between devices, exchange(): x = lax.all_to_all(x, 'dom', split_axis=0, concat_axis=0, tiled=True)  23.9 us
    unnamed x17, local copies, waits for them, and re-layouts  15 us
    pallas_call x1, Pallas kernels, local(): pl.pallas_call(grid_body, grid=(grid_rows // chunk,), out_shape=jax.Shape...  6.39 us
    all_to_all x2, waiting for transfers between devices, exchange(): x = lax.all_to_all(x, 'dom', split_axis=0, concat_axis=0, tiled=True)  6.22 us
  transfers between devices with their start and end apart: 4, of which 3 were waited for; matrix products, arithmetic and copies ran while one was open for 2% of the time, Pallas kernels for 24%

profile of v1, /device:TPU:1, one launch (start us, length us, event | category | flops | bytes accessed | tf_op | source)
XLA Modules:
  0.0 120.5 jit_solution(5995320506772658191)
XLA Ops:
  0.6 1.4 %copy.14 = s32[1,128,16]{2,1,0:T(8,128)} copy(s32[1,128,16]{1,2,0:T(8,128)} %param.20) | data formatting | bytes 16384 | tf_op args[8]
  2.1 1.5 %copy.16.owner = s32[256,1]{1,0:T(8,128)} copy(s32[256,1]{0,1:T(1,128)} %param.21) | data formatting | bytes 2048 | tf_op args[9]
  3.5 1.5 %copy.17.nodes = s32[256,8]{1,0:T(8,128)} copy(s32[256,8]{0,1:T(8,128)} %param.22) | data formatting | bytes 16384 | tf_op args[10]
  5.0 1.8 %copy.15.edges = s32[1024,4]{1,0:T(8,128)} copy(s32[1024,4]{0,1:T(4,128)} %param.17) | data formatting | bytes 32768 | tf_op args[5]
  6.8 18.2 %encode.1 = (bf16[1536,128]{1,0:T(8,128)(2,1)}, bf16[1024,128]{1,0:T(8,128)(2,1)}, s32[256,1]{1,0:T(8,128)}) custom-call(s32[1]{0:T(128)} %bitcast.feat_ref, bf16[4096,128]{1,0:T(8,128)(2,1)} %inc.1, s32[1024,4]{1,0:T(8,128)} %copy.15.edges, s32[128,16]{1,0:T(8,128)} %bitcast.8, s32[256,1]{1,0:T(8,128)} %copy.16.owner, s32[256,8]{1,0:T(8,128)} %copy.17.nodes, ...), custom_call_target="tpu_custom_call" | custom-call | tf_op jit(solution)/shard_map/encode/pallas_call | solution.py:227
  24.9 16.3 %all-to-all-start = ((bf16[128,3,4,128]{3,2,1,0:T(4,128)(2,1)}), bf16[128,3,4,128]{3,2,1,0:T(4,128)(2,1)S(1)}, u32[]{:S(2)}, u32[]{:S(2)}) async-start(bf16[128,3,4,128]{3,2,1,0:T(4,128)(2,1)} %bitcast.11), calls=%async_computation | async-start | bytes 786432 | tf_op jit(solution)/shard_map/all_to_all | solution.py:239
  41.3 1.8 %copy.18.edges = s32[1024,6]{1,0:T(8,128)} copy(s32[1024,6]{0,1:T(8,128)} %param.18) | data formatting | bytes 49152 | tf_op args[6]
  43.1 1.0 copy.19.mask
  44.1 9.1 %prepare.1 = (bf16[1024,2048]{1,0:T(8,128)(2,1)}, bf16[256,512]{1,0:T(8,128)(2,1)}, bf16[512,128]{1,0:T(8,128)(2,1)}, bf16[128,128]{1,0:T(8,128)(2,1)}) custom-call(s32[1]{0:T(128)} %bitcast.feat_ref, s32[1024,6]{1,0:T(8,128)} %copy.18.edges, s32[1024,6]{1,0:T(8,128)} %copy.19.mask, bf16[128,256]{1,0:T(8,128)(2,1)} %w_in.1, bf16[512,512]{1,0:T(8,128)(2,1)} %w_node1.1, ...), custom_call_target="tpu_custom_call" | custom-call | tf_op jit(solution)/shard_map/prepare/pallas_call | solution.py:227
  53.2 4.7 %all-to-all-done = bf16[128,3,4,128]{3,2,1,0:T(4,128)(2,1)S(1)} async-done(((bf16[128,3,4,128]{3,2,1,0:T(4,128)(2,1)}), bf16[128,3,4,128]{3,2,1,0:T(4,128)(2,1)S(1)}, u32[]{:S(2)}, u32[]{:S(2)}) %all-to-all-start) | async-done | bytes 393248 | tf_op jit(solution)/shard_map/all_to_all | solution.py:239
  57.9 0.7 copy-done.1
  58.6 4.8 %mix.1 = (bf16[1280,128]{1,0:T(8,128)(2,1)}, s32[128,128]{1,0:T(8,128)}) custom-call(s32[1]{0:T(128)} %bitcast.feat_ref, bf16[1536,128]{1,0:T(8,128)(2,1)} %bitcast.7, bf16[1024,128]{1,0:T(8,128)(2,1)} %get-tuple-element.20.ginc, bf16[1024,2048]{1,0:T(8,128)(2,1)} %get-tuple-element.21.m), custom_call_target="tpu_custom_call" | custom-call | tf_op jit(solution)/shard_map/mix/pallas_call | solution.py:227
  63.5 2.2 %collective-permute-start = (bf16[1280,128]{1,0:T(8,128)(2,1)}, bf16[1280,128]{1,0:T(8,128)(2,1)S(1)}, u32[]{:S(2)}, u32[]{:S(2)}) collective-permute-start(bf16[1280,128]{1,0:T(8,128)(2,1)} %get-tuple-element.22.part), channel_id=1, source_target_pairs={{0,1},{1,0},{2,3},{3,2},{4,5},{5,4},{6,7},{7,6},{8,9},{9,8},{10,11... | collective-permute-start | bytes 983048 | tf_op jit(solution)/shard_map/ppermute | solution.py:296
  65.7 4.0 %sites.1.s = bf16[512,1024]{1,0:T(8,128)(2,1)} custom-call(s32[128,128]{1,0:T(8,128)} %get-tuple-element.23.node), custom_call_target="tpu_custom_call" | custom-call | tf_op jit(solution)/shard_map/sites/pallas_call | solution.py:227
  70.4 7.9 %node.1 = (bf16[1536,128]{1,0:T(8,128)(2,1)}, f32[64,1024]{1,0:T(8,128)}, f32[128,512]{1,0:T(8,128)}) custom-call(s32[1]{0:T(128)} %bitcast.feat_ref, bf16[1280,128]{1,0:T(8,128)(2,1)} %get-tuple-element.22.part, bf16[1280,128]{1,0:T(8,128)(2,1)} %copy-done.2, bf16[1024,128]{1,0:T(8,128)(2,1)} %get-tuple-element.20.ginc, ...), custom_call_target="tpu_custom_call" | custom-call | tf_op jit(solution)/shard_map/node/pallas_call | solution.py:227
  78.4 7.6 %all-to-all-start.1 = ((bf16[128,3,4,128]{3,2,1,0:T(4,128)(2,1)}), bf16[128,3,4,128]{3,2,1,0:T(4,128)(2,1)S(1)}, u32[]{:S(2)}, u32[]{:S(2)}) async-start(bf16[128,3,4,128]{3,2,1,0:T(4,128)(2,1)} %bitcast.10), calls=%async_computation.1 | async-start | bytes 786432 | tf_op jit(solution)/shard_map/all_to_all | solution.py:239
  85.9 15.5 %scatter.1 = (bf16[1024,4096]{1,0:T(8,128)(2,1)}, bf16[1536,1024]{1,0:T(8,128)(2,1)}) custom-call(s32[1]{0:T(128)} %bitcast.feat_ref, s32[1024,4]{1,0:T(8,128)} %copy.15.edges, s32[128,16]{1,0:T(8,128)} %bitcast.9), custom_call_target="tpu_custom_call" | custom-call | tf_op jit(solution)/shard_map/scatter/pallas_call | solution.py:227
  101.4 1.5 %all-to-all-done.1 = bf16[128,3,4,128]{3,2,1,0:T(4,128)(2,1)S(1)} async-done(((bf16[128,3,4,128]{3,2,1,0:T(4,128)(2,1)}), bf16[128,3,4,128]{3,2,1,0:T(4,128)(2,1)S(1)}, u32[]{:S(2)}, u32[]{:S(2)}) %all-to-all-start.1) | async-done | bytes 393248 | tf_op jit(solution)/shard_map/all_to_all | solution.py:239
  102.9 0.7 copy-done
  103.7 3.6 %return.1 = (f32[64,1024]{1,0:T(8,128)}, bf16[64,1024]{1,0:T(8,128)(2,1)}, bf16[256,128]{1,0:T(8,128)(2,1)}) custom-call(s32[1]{0:T(128)} %bitcast.feat_ref, bf16[1536,128]{1,0:T(8,128)(2,1)} %bitcast.6, bf16[1536,1024]{1,0:T(8,128)(2,1)} %get-tuple-element.28.r, f32[128,512]{1,0:T(8,128)} %get-tuple-element.29.ext_t, f32[64,1024]{1,0:T(8,128)} %get-tuple-element.30.own_t, ...), custom_call_target="tpu_custom_call" | custom-call | tf_op jit(solution)/shard_map/return/pallas_call | solution.py:227
  107.3 1.8 %collective-permute-start.1 = (bf16[64,1024]{1,0:T(8,128)(2,1)}, bf16[64,1024]{1,0:T(8,128)(2,1)S(1)}, u32[]{:S(2)}, u32[]{:S(2)}) collective-permute-start(bf16[64,1024]{1,0:T(8,128)(2,1)} %get-tuple-element.33), channel_id=1, source_target_pairs={{0,1},{1,0},{2,3},{3,2},{4,5},{5,4},{6,7},{7,6},{8,9},{9,8},{10,11... | collective-permute-start | bytes 393224 | tf_op jit(solution)/shard_map/ppermute | solution.py:330
  109.1 1.2 collective-permute-done.1.got_ref
  111.0 6.4 %grid.1 = f32[4096,64]{1,0:T(8,128)} custom-call(f32[64,1024]{1,0:T(8,128)} %get-tuple-element.32.keep_ref, bf16[64,1024]{1,0:T(8,128)(2,1)} %copy-done.3, bf16[1024,4096]{1,0:T(8,128)(2,1)} %get-tuple-element.34.g_ref), custom_call_target="tpu_custom_call" | custom-call | tf_op jit(solution)/shard_map/grid/pallas_call | solution.py:337
  117.4 3.1 %copy.21 = f32[4096,64]{0,1:T(8,128)} copy(f32[4096,64]{1,0:T(8,128)} %grid.1) | data formatting | bytes 2097152
  (9 shorter events, 1.4 us)
Async XLA Ops:
  0.6 42.4 %copy-start.4 = (s32[1024,6]{0,1:T(8,128)S(1)}, s32[1024,6]{0,1:T(8,128)}, u32[]{:S(2)}) copy-start(s32[1024,6]{0,1:T(8,128)} %param.19) | copy-start | bytes 73732
  24.9 32.9 %all-to-all-start = ((bf16[128,3,4,128]{3,2,1,0:T(4,128)(2,1)}), bf16[128,3,4,128]{3,2,1,0:T(4,128)(2,1)S(1)}, u32[]{:S(2)}, u32[]{:S(2)}) async-start(bf16[128,3,4,128]{3,2,1,0:T(4,128)(2,1)} %bitcast.11), calls=%async_computation | async-start | bytes 786432 | tf_op jit(solution)/shard_map/all_to_all | solution.py:239
  57.9 0.7 copy-start.1
  63.5 6.2 %collective-permute-start = (bf16[1280,128]{1,0:T(8,128)(2,1)}, bf16[1280,128]{1,0:T(8,128)(2,1)S(1)}, u32[]{:S(2)}, u32[]{:S(2)}) collective-permute-start(bf16[1280,128]{1,0:T(8,128)(2,1)} %get-tuple-element.22.part), channel_id=1, source_target_pairs={{0,1},{1,0},{2,3},{3,2},{4,5},{5,4},{6,7},{7,6},{8,9},{9,8},{10,11... | collective-permute-start | bytes 983048 | tf_op jit(solution)/shard_map/ppermute | solution.py:296
  69.7 0.7 copy-start.2
  78.4 24.6 %all-to-all-start.1 = ((bf16[128,3,4,128]{3,2,1,0:T(4,128)(2,1)}), bf16[128,3,4,128]{3,2,1,0:T(4,128)(2,1)S(1)}, u32[]{:S(2)}, u32[]{:S(2)}) async-start(bf16[128,3,4,128]{3,2,1,0:T(4,128)(2,1)} %bitcast.10), calls=%async_computation.1 | async-start | bytes 786432 | tf_op jit(solution)/shard_map/all_to_all | solution.py:239
  102.9 0.7 copy-start
  107.3 3.0 %collective-permute-start.1 = (bf16[64,1024]{1,0:T(8,128)(2,1)}, bf16[64,1024]{1,0:T(8,128)(2,1)S(1)}, u32[]{:S(2)}, u32[]{:S(2)}) collective-permute-start(bf16[64,1024]{1,0:T(8,128)(2,1)} %get-tuple-element.33), channel_id=1, source_target_pairs={{0,1},{1,0},{2,3},{3,2},{4,5},{5,4},{6,7},{7,6},{8,9},{9,8},{10,11... | collective-permute-start | bytes 393224 | tf_op jit(solution)/shard_map/ppermute | solution.py:330
  110.3 0.7 copy-start.3

commit v2 on v1

v2 whole, which is shorter than its diff:
```python
import jax
import jax.numpy as jnp
from jax import lax
from jax.experimental import pallas as pl
from jax.experimental.pallas import tpu as pltpu
from jax.sharding import PartitionSpec as P

BF = jnp.bfloat16
F32 = jnp.float32
I16 = jnp.int16
I32 = jnp.int32
LANES = 128
HALF_DEPTH = 8
SLOTS = 4
ROWS = HALF_DEPTH + SLOTS
SWAP = [(0, 1), (1, 0)]


def dot(a, b, ca=1, cb=0):
    return lax.dot_general(a, b, (((ca,), (cb,)), ((), ())), preferred_element_type=F32)


def iota(shape, axis):
    return lax.broadcasted_iota(I32, shape, axis)


def eq_bf16(a, b):
    return jnp.where(a == b, jnp.asarray(1, BF), jnp.asarray(0, BF))


def build_counts(dst, tiles, height, lane0=0, sub=16, unroll=4):
    cols = [[jnp.broadcast_to(r, (sub, LANES)).astype(I16) for r in rows] for rows in tiles]
    start = iota((sub, LANES), 0).astype(I16)

    def body(i, at):
        s = pl.multiple_of(i * sub, sub)
        for t, rows in enumerate(cols):
            acc = eq_bf16(rows[0], at)
            for r in rows[1:]:
                acc = acc + eq_bf16(r, at)
            dst[pl.ds(s, sub), lane0 + t * LANES : lane0 + (t + 1) * LANES] = acc
        return at + jnp.asarray(sub, I16)

    lax.fori_loop(0, height // sub, body, start, unroll=unroll)


def lane_tiles(rows, first=0, last=None):
    last = rows.shape[1] // LANES if last is None else last
    return [
        [rows[k : k + 1, t * LANES : (t + 1) * LANES] for k in range(rows.shape[0])]
        for t in range(first, last)
    ]


def block_of(shape):
    row = iota(shape, 1)
    peer = jnp.floor((row.astype(F32) + 0.5) * (1.0 / ROWS)).astype(I32)
    return peer, row - peer * ROWS


def place_rows(dst, slots):
    c = iota((1, slots * LANES), 1)
    build_counts(dst, lane_tiles((c & 127) * ROWS + HALF_DEPTH + (c >> 7)), dst.shape[0])


def take_rows(dst, slots):
    peer, within = block_of((1, dst.shape[1]))
    slot = within - HALF_DEPTH
    build_counts(dst, lane_tiles(jnp.where(slot >= 0, slot * LANES + peer, -1)), slots * LANES)


def send_index(feat, send, rows):
    peers = send.shape[1]
    picked = jnp.where(feat == 0, send[:HALF_DEPTH, :], send[HALF_DEPTH:, :])
    table = jnp.concatenate([picked >> 5, picked & 31], axis=0).astype(F32).astype(BF)
    peer, within = block_of((1, rows))
    spread = jnp.where(iota((peers, rows), 0) == peer, 1.0, 0.0).astype(BF)
    out = dot(table, spread)
    node = out[:HALF_DEPTH, :] * 32.0 + out[HALF_DEPTH:, :]
    hit = iota((HALF_DEPTH, rows), 0) == within
    index = jnp.sum(jnp.where(hit, node, 0.0), axis=0, keepdims=True)
    return jnp.where(within >= HALF_DEPTH, -1.0, index).astype(I32)


def encode_kernel(feat_ref, inc, edges, send, owner, nodes, obs, msg, ginc, target, g, r, c_s):
    feat = feat_ref[0]
    rows = msg.shape[0]
    build_counts(g, lane_tiles(edges[...]), inc.shape[0])
    build_counts(r, lane_tiles(send_index(feat, send[...], rows)), ginc.shape[1])
    place_rows(c_s, 3)
    sites = owner.shape[1]
    own = owner[...]
    member = jnp.where(iota((LANES, sites), 0) == own, 1.0, 0.0)
    member_b = member.astype(BF)
    upper = jnp.where(iota((sites, sites), 0) < iota((sites, sites), 1), 1.0, 0.0).astype(BF)
    rank = jnp.sum(dot(member_b, upper) * member, axis=0, keepdims=True)
    target[...] = own * ROWS + HALF_DEPTH + rank.astype(I32)
    slot0 = (2 * feat).astype(F32)
    obs_0 = dot(jnp.where(rank == slot0, member, 0.0).astype(BF), obs[...])
    obs_1 = dot(jnp.where(rank == slot0 + 1.0, member, 0.0).astype(BF), obs[...])
    n = nodes[...]
    high = ((n >> 5) + 1).astype(F32)
    low = (n & 31).astype(F32)
    lists = [jnp.where(rank == float(k), v, 0.0) for v in (high, low) for k in range(SLOTS)]
    lists.append(jnp.zeros((LANES - 2 * SLOTS * n.shape[0], sites), F32))
    listed = dot(member_b, jnp.concatenate(lists, axis=0).astype(BF), 1, 1)
    site_rows = dot(c_s[...], jnp.concatenate([obs_0, obs_1, listed], axis=0).astype(BF))
    mean = (dot(inc[...], g[...], 0, 0) * (1.0 / edges.shape[0])).astype(BF)
    ginc[...] = mean
    msg[...] = (dot(mean, r[...]).T + site_rows).astype(BF)


def prepare_kernel(
    feat_ref, edges, mask, w_in, w_node1, w_node2, w_out, m, w_cat, w_cat_t, w_ho, w_ho_t, w_io, w_io_t
):
    feat = feat_ref[0]
    rows = edges.shape[1]
    half = rows // 2
    e = edges[...]
    own_row = e - feat * half
    h = e - rows
    r = h & 15
    halo_row = half + (h >> 4) * ROWS + (r & 7)
    is_own = (e < rows) & (own_row >= 0) & (own_row < half)
    is_halo = (e >= rows) & ((r >> 3) == feat)
    at = jnp.where(is_own, own_row, jnp.where(is_halo, halo_row, -1))
    at = jnp.where(mask[...] > 0, at, -1)
    tiles = lane_tiles(at)
    for first in range(0, len(tiles), 4):
        build_counts(m, tiles[first : first + 4], m.shape[0], first * LANES)
    width = w_in.shape[1]
    variables = w_in.shape[0]
    wi = w_in[...]
    for k in range(2):
        w1 = w_node1[k * width : (k + 1) * width, :]
        w_cat[k * variables : (k + 1) * variables, :] = dot(wi, w1).astype(BF)
        w_cat_t[:, k * variables : (k + 1) * variables] = dot(w1, wi, 0, 1).astype(BF)
    w_ho[...] = dot(w_node2[...], w_out[...]).astype(BF)
    w_ho_t[...] = dot(w_out[...], w_node2[...], 0, 1).astype(BF)
    w_io[...] = dot(wi, w_out[...]).astype(BF)
    w_io_t[...] = dot(w_out[...], wi, 0, 1).astype(BF)


def mix_kernel(feat_ref, msg, ginc, m, part, node, c_s):
    feat = feat_ref[0]
    rows = ginc.shape[1]
    half = rows // 2
    take_rows(c_s, 3)
    got = msg[...]
    own = ginc[:, pl.ds(pl.multiple_of(feat * half, half), half)]
    part[:, :rows] = (dot(own, m[:half, :]) + dot(got, m[half:, :], 0, 0)).astype(BF)
    sites = dot(c_s[...], got).T
    part[:, rows:] = sites[:, : 2 * LANES].astype(BF)
    lists = sites[: 2 * node.shape[0], 2 * LANES :]
    node[...] = ((lists[: node.shape[0], :] - 1.0) * 32.0 + lists[node.shape[0] :, :]).astype(I32)


def site_kernel(node, s):
    degree = node.shape[0] // SLOTS
    tiles = [[node[k * degree + j : k * degree + j + 1, :] for j in range(degree)] for k in range(SLOTS)]
    build_counts(s, tiles, s.shape[0])


def node_kernel(
    feat_ref, part, other, ginc, m, s, w_cat, w_cat_t, w_ho, w_ho_t, w_io, w_io_t, msg, own, ext_own, slope_s, c_s
):
    feat = feat_ref[0]
    variables, rows = ginc.shape
    half = rows // 2
    place_rows(c_s, SLOTS)
    gi = ginc[...]
    agg = (part[:, :rows].astype(F32) + other[:, :rows].astype(F32)).astype(BF)
    pre = dot(w_cat_t[...], jnp.concatenate([gi, agg], axis=0))
    sig = 1.0 / (1.0 + jnp.exp(-pre))
    hidden = (pre * sig).astype(BF)
    slope_s[...] = sig * (1.0 + pre * (1.0 - sig))
    readout = (dot(w_ho_t[...], hidden) + dot(w_io_t[...], gi)).astype(BF)
    values = dot(readout, s[...])
    mine = part[:, rows:].astype(F32)
    theirs = other[:, rows:].astype(F32)
    first = jnp.where(feat == 0, mine, theirs)
    second = jnp.where(feat == 0, theirs, mine)
    diff = (values - jnp.concatenate([first, second], axis=1)).astype(BF)
    d = dot(diff, s[...], 1, 1).astype(BF)
    inner = (dot(w_ho[...], d) * slope_s[...]).astype(BF)
    n = variables // 2
    cols = pl.ds(pl.multiple_of(feat * n, n), n)
    both = dot(jnp.concatenate([w_cat[cols, :], w_cat[variables:, :]], axis=0), inner)
    own[...] = dot(w_io[cols, :], d) + both[:n, :]
    ext = dot(m[...], both[n:, :].T.astype(BF))
    ext_own[...] = ext[:half, :].T
    msg[...] = (ext[half:, :] + dot(c_s[...], values.T.astype(BF))).astype(BF)


def scatter_kernel(feat_ref, edges, send, g, r):
    build_counts(g, lane_tiles(edges[...]), g.shape[0])
    build_counts(r, lane_tiles(send_index(feat_ref[0], send[...], r.shape[1])), r.shape[0])


def return_kernel(feat_ref, msg, r, ext_own, own, target, keep, give, pred, part_s, p_s):
    feat = feat_ref[0]
    half = ext_own.shape[1]
    build_counts(p_s, lane_tiles(target[...]), msg.shape[0])
    back = msg[...].T
    part_s[...] = dot(back, r[...], 1, 1)
    at = pl.ds(pl.multiple_of(feat * half, half), half)
    part_s[:, at] = part_s[:, at] + ext_own[...]
    n = keep.shape[0]
    keep[...] = part_s[pl.ds(pl.multiple_of(feat * n, n), n), :] + own[...]
    give[...] = part_s[pl.ds(pl.multiple_of((1 - feat) * n, n), n), :].astype(BF)
    pred[...] = dot(back, p_s[...]).T.astype(BF)


def grid_kernel(keep, got, g, out, *, degree):
    lg = ((keep[...] + got[...].astype(F32)) * (1.0 / degree)).astype(BF)
    out[...] = dot(lg, g[...], 1, 1)


SCALAR = pl.BlockSpec(memory_space=pltpu.SMEM)
FULL = pl.BlockSpec(memory_space=pltpu.VMEM)


def vmem(x):
    return pltpu.with_memory_space_constraint(x, pltpu.VMEM)


def call(kernel, outs, args, scratch=(), scalar=True, name=None):
    return pl.pallas_call(
        kernel,
        out_shape=[
            pltpu.VMEM(s, t) if stay else jax.ShapeDtypeStruct(s, t) for s, t, stay in outs
        ],
        in_specs=([SCALAR] if scalar else []) + [FULL] * (len(args) - bool(scalar)),
        out_specs=[FULL] * len(outs),
        scratch_shapes=list(scratch),
        name=name,
    )(*args)


def exchange(msg, domains):
    x = msg.reshape(domains, ROWS // 4, 4, msg.shape[1])
    x = lax.all_to_all(x, "dom", split_axis=0, concat_axis=0, tiled=True)
    return x.reshape(msg.shape)


def local(
    increments,
    w_in,
    w_node1,
    w_node2,
    w_out,
    grid_edges,
    mesh_edges,
    mesh_mask,
    send_rows,
    site_owner,
    site_nodes,
    site_obs,
):
    domains = lax.axis_size("dom")
    feat = lax.axis_index("feat").astype(I32).reshape(1)
    grid_rows, variables = increments.shape
    mesh_rows = mesh_edges.shape[0]
    inner = w_node2.shape[0]
    site_count = site_obs.shape[0]
    half = mesh_rows // 2
    rows = domains * ROWS
    degree = grid_edges.shape[1]
    n = variables // 2
    msg, ginc, target = call(
        encode_kernel,
        [
            ((rows, variables), BF, False),
            ((variables, mesh_rows), BF, False),
            ((1, site_count), I32, False),
        ],
        (feat, increments, grid_edges.T, send_rows[0].T, site_owner.T, site_nodes.T, site_obs),
        [
            pltpu.VMEM((grid_rows, mesh_rows), BF),
            pltpu.VMEM((mesh_rows, rows), BF),
            pltpu.VMEM((rows, 3 * LANES), BF),
        ],
        name="encode",
    )
    m, *weights = call(
        prepare_kernel,
        [
            ((half + rows, mesh_rows), BF, False),
            ((2 * variables, inner), BF, False),
            ((inner, 2 * variables), BF, False),
            ((inner, variables), BF, False),
            ((variables, inner), BF, False),
            ((variables, variables), BF, False),
            ((variables, variables), BF, False),
        ],
        (feat, mesh_edges.T, mesh_mask.T, w_in, w_node1, w_node2, w_out),
        name="prepare",
    )
    got = exchange(msg, domains)
    part, node = call(
        mix_kernel,
        [
            ((variables, mesh_rows + 2 * LANES), BF, True),
            ((SLOTS * site_nodes.shape[1], LANES), I32, True),
        ],
        (feat, vmem(got), ginc, m),
        [pltpu.VMEM((3 * LANES, rows), BF)],
        name="mix",
    )
    other = lax.ppermute(part, "feat", SWAP)
    (sites,) = call(
        site_kernel, [((mesh_rows, SLOTS * domains), BF, True)], (vmem(node),), scalar=False, name="sites"
    )
    back, own, ext_own = call(
        node_kernel,
        [
            ((rows, variables), BF, False),
            ((n, mesh_rows), F32, False),
            ((variables, half), F32, False),
        ],
        (feat, vmem(part), vmem(other), ginc, m, vmem(sites), *weights),
        [pltpu.VMEM((inner, mesh_rows), F32), pltpu.VMEM((rows, SLOTS * LANES), BF)],
        name="node",
    )
    got_back = exchange(back, domains)
    g, r = call(
        scatter_kernel,
        [((grid_rows, mesh_rows), BF, False), ((mesh_rows, rows), BF, False)],
        (feat, grid_edges.T, send_rows[0].T),
        name="scatter",
    )
    keep, give, site_pred = call(
        return_kernel,
        [
            ((n, mesh_rows), F32, False),
            ((n, mesh_rows), BF, False),
            ((site_count, variables), BF, False),
        ],
        (feat, vmem(got_back), r, ext_own, own, target),
        [pltpu.VMEM((variables, mesh_rows), F32), pltpu.VMEM((rows, site_count), BF)],
        name="return",
    )
    take = lax.ppermute(give, "feat", SWAP)

    def grid_body(keep_ref, got_ref, g_ref, out_ref):
        grid_kernel(keep_ref, got_ref, g_ref, out_ref, degree=degree)

    (grad,) = call(
        grid_body,
        [((n, grid_rows), F32, False)],
        (keep, vmem(take), g),
        scalar=False,
        name="grid",
    )
    return (grad.T, site_pred)


def solution(mesh):
    return jax.shard_map(
        local,
        mesh=mesh,
        in_specs=(
            P("dom", None),
            P(),
            P(),
            P(),
            P(),
            P("dom", None),
            P("dom", None),
            P("dom", None),
            P("dom", None, None),
            P("dom", None),
            P("dom", None),
            P("dom", None),
        ),
        out_specs=(P("dom", "feat"), P("dom", None)),
        check_vma=False,
    )
```

time: 121 us -> 96 us (0.79)
  Pallas kernels: 69.5 us -> 49.1 us
  local copies, waits for them, and re-layouts: 15 us -> 0 us
  waiting for transfers between devices: 7.42 us -> 19 us
    pallas_call x8, Pallas kernels: 69.5 us -> 49.1 us  [call(): pl.pallas_call(kernel, out_shape=[pltpu.VMEM(s, t) if stay else jax.Shape...]
    unnamed x17 -> x0, local copies, waits for them, and re-layouts: 15 us -> none
    all_to_all x2, waiting for transfers between devices: 6.22 us -> 17.5 us  [exchange(): x = lax.all_to_all(x, 'dom', split_axis=0, concat_axis=0, tiled=True)]
    all_to_all x2, starting transfers between devices: 23.9 us -> 22.7 us  [exchange(): x = lax.all_to_all(x, 'dom', split_axis=0, concat_axis=0, tiled=True)]
  transfers between devices with their start and end apart: 4 -> 4, of which waited for: 3 -> 4; matrix products, arithmetic and copies ran while one was open for 2% -> 0% of each run, Pallas kernels for 24% -> 18%
where the time goes in v2:
time: 96 us; the launch traced here: 95.6 us
  Pallas kernels  49.1 us (51%)
  starting transfers between devices  26.9 us (28%)
  waiting for transfers between devices  19 us (20%)
    pallas_call x8, Pallas kernels, call(): pl.pallas_call(kernel, out_shape=[pltpu.VMEM(s, t) if stay else jax.Shape...  49.1 us
    all_to_all x2, starting transfers between devices, exchange(): x = lax.all_to_all(x, 'dom', split_axis=0, concat_axis=0, tiled=True)  22.7 us
    all_to_all x2, waiting for transfers between devices, exchange(): x = lax.all_to_all(x, 'dom', split_axis=0, concat_axis=0, tiled=True)  17.5 us
    ppermute x1, starting transfers between devices, local(): other = lax.ppermute(part, 'feat', SWAP)  2.32 us
  transfers between devices with their start and end apart: 4, of which 4 were waited for; matrix products, arithmetic and copies ran while one was open for 0% of the time, Pallas kernels for 18%

profile of v2, /device:TPU:1, one launch (start us, length us, event | category | flops | bytes accessed | tf_op | source)
XLA Modules:
  0.0 95.6 jit_solution(16343978241495831323)
XLA Ops:
  0.6 9.6 %encode.1 = (bf16[1536,128]{1,0:T(8,128)(2,1)}, bf16[128,1024]{1,0:T(8,128)(2,1)}, s32[1,256]{1,0:T(1,128)}) custom-call(s32[1]{0:T(128)} %bitcast.feat_ref, bf16[4096,128]{1,0:T(8,128)(2,1)} %inc.1, s32[4,1024]{1,0:T(4,128)} %bitcast.19, s32[16,128]{1,0:T(8,128)} %bitcast.21, s32[1,256]{1,0:T(1,128)} %bitcast.26, s32[8,256]{1,0:T(8,128)} %bitcast.25, ...), custom_call_target="tpu_custom_call" | custom-call | tf_op jit(solution)/shard_map/encode/pallas_call | solution.py:228
  10.3 16.3 %all-to-all-start = ((bf16[128,3,4,128]{3,2,1,0:T(4,128)(2,1)}), bf16[128,3,4,128]{3,2,1,0:T(4,128)(2,1)S(1)}, u32[]{:S(2)}, u32[]{:S(2)}) async-start(bf16[128,3,4,128]{3,2,1,0:T(4,128)(2,1)} %bitcast.18), calls=%async_computation | async-start | bytes 786432 | tf_op jit(solution)/shard_map/all_to_all | solution.py:242
  26.6 6.3 %prepare.1 = (bf16[2048,1024]{1,0:T(8,128)(2,1)}, bf16[256,512]{1,0:T(8,128)(2,1)}, bf16[512,256]{1,0:T(8,128)(2,1)}, bf16[512,128]{1,0:T(8,128)(2,1)}, bf16[128...) custom-call(s32[1]{0:T(128)} %bitcast.feat_ref, s32[6,1024]{1,0:T(8,128)} %bitcast.23, ...), custom_call_target="tpu_custom_call" | custom-call | tf_op jit(solution)/shard_map/prepare/pallas_call | solution.py:228
  32.9 10.3 %all-to-all-done = bf16[128,3,4,128]{3,2,1,0:T(4,128)(2,1)S(1)} async-done(((bf16[128,3,4,128]{3,2,1,0:T(4,128)(2,1)}), bf16[128,3,4,128]{3,2,1,0:T(4,128)(2,1)S(1)}, u32[]{:S(2)}, u32[]{:S(2)}) %all-to-all-start) | async-done | bytes 393248 | tf_op jit(solution)/shard_map/all_to_all | solution.py:242
  43.2 3.6 %mix.1 = (bf16[128,1280]{1,0:T(8,128)(2,1)S(1)}, s32[32,128]{1,0:T(8,128)S(1)}) custom-call(s32[1]{0:T(128)} %bitcast.feat_ref, bf16[1536,128]{1,0:T(8,128)(2,1)S(1)} %bitcast.15, bf16[128,1024]{1,0:T(8,128)(2,1)} %get-tuple-element.23.ginc, bf16[2048,1024]{1,0:T(8,128)(2,1)} %get-tuple-element.24.m), custom_call_target="tpu_custom_call" | custom-call | tf_op jit(solution)/shard_map/mix/pallas_call | solution.py:228
  46.8 2.3 %collective-permute-start = (bf16[128,1280]{1,0:T(8,128)(2,1)S(1)}, bf16[128,1280]{1,0:T(8,128)(2,1)S(1)}, u32[]{:S(2)}, u32[]{:S(2)}) collective-permute-start(bf16[128,1280]{1,0:T(8,128)(2,1)S(1)} %get-tuple-element.25.part), channel_id=1, source_target_pairs={{0,1},{1,0},{2,3},{3,2},{4,5},{5,4},{6,7},{7,6},{8,9},{9,8},{10,11... | collective-permute-start | bytes 983048 | tf_op jit(solution)/shard_map/ppermute | solution.py:310
  49.1 1.0 sites.1.s
  50.1 0.3 collective-permute-done.other
  50.4 7.5 %node.1 = (bf16[1536,128]{1,0:T(8,128)(2,1)}, f32[64,1024]{1,0:T(8,128)}, f32[128,512]{1,0:T(8,128)}) custom-call(s32[1]{0:T(128)} %bitcast.feat_ref, bf16[128,1280]{1,0:T(8,128)(2,1)S(1)} %get-tuple-element.25.part, bf16[128,1280]{1,0:T(8,128)(2,1)S(1)} %collective-permute-done.other, bf16[128,1024]{1,0:T(8,128)(2,1)} %get-tuple-element.23.ginc, ...), custom_call_target="tpu_custom_call" | custom-call | tf_op jit(solution)/shard_map/node/pallas_call | solution.py:228
  57.9 6.4 %all-to-all-start.1 = ((bf16[128,3,4,128]{3,2,1,0:T(4,128)(2,1)}), bf16[128,3,4,128]{3,2,1,0:T(4,128)(2,1)S(1)}, u32[]{:S(2)}, u32[]{:S(2)}) async-start(bf16[128,3,4,128]{3,2,1,0:T(4,128)(2,1)} %bitcast.17), calls=%async_computation.1 | async-start | bytes 786432 | tf_op jit(solution)/shard_map/all_to_all | solution.py:242
  64.3 9.7 %scatter.1 = (bf16[4096,1024]{1,0:T(8,128)(2,1)}, bf16[1024,1536]{1,0:T(8,128)(2,1)}) custom-call(s32[1]{0:T(128)} %bitcast.feat_ref, s32[4,1024]{1,0:T(4,128)} %bitcast.20, s32[16,128]{1,0:T(8,128)} %bitcast.22), custom_call_target="tpu_custom_call" | custom-call | tf_op jit(solution)/shard_map/scatter/pallas_call | solution.py:228
  74.0 7.2 %all-to-all-done.1 = bf16[128,3,4,128]{3,2,1,0:T(4,128)(2,1)S(1)} async-done(((bf16[128,3,4,128]{3,2,1,0:T(4,128)(2,1)}), bf16[128,3,4,128]{3,2,1,0:T(4,128)(2,1)S(1)}, u32[]{:S(2)}, u32[]{:S(2)}) %all-to-all-start.1) | async-done | bytes 393248 | tf_op jit(solution)/shard_map/all_to_all | solution.py:242
  81.2 4.2 %return.1 = (f32[64,1024]{1,0:T(8,128)}, bf16[64,1024]{1,0:T(8,128)(2,1)}, bf16[256,128]{1,0:T(8,128)(2,1)}) custom-call(s32[1]{0:T(128)} %bitcast.feat_ref, bf16[1536,128]{1,0:T(8,128)(2,1)S(1)} %bitcast.14, bf16[1024,1536]{1,0:T(8,128)(2,1)} %get-tuple-element.34.r, f32[128,512]{1,0:T(8,128)} %get-tuple-element.35.ext_own, ...), custom_call_target="tpu_custom_call" | custom-call | tf_op jit(solution)/shard_map/return/pallas_call | solution.py:228
  85.4 1.9 %collective-permute-start.1 = (bf16[64,1024]{1,0:T(8,128)(2,1)}, bf16[64,1024]{1,0:T(8,128)(2,1)S(1)}, u32[]{:S(2)}, u32[]{:S(2)}) collective-permute-start(bf16[64,1024]{1,0:T(8,128)(2,1)} %get-tuple-element.39), channel_id=1, source_target_pairs={{0,1},{1,0},{2,3},{3,2},{4,5},{5,4},{6,7},{7,6},{8,9},{9,8},{10,11... | collective-permute-start | bytes 393224 | tf_op jit(solution)/shard_map/ppermute | solution.py:343
  87.3 1.2 %collective-permute-done.1.got_ref = bf16[64,1024]{1,0:T(8,128)(2,1)S(1)} collective-permute-done((bf16[64,1024]{1,0:T(8,128)(2,1)}, bf16[64,1024]{1,0:T(8,128)(2,1)S(1)}, u32[]{:S(2)}, u32[]{:S(2)}) %collective-permute-start.1) | collective-permute-done | bytes 131104 | tf_op jit(solution)/shard_map/ppermute | solution.py:343
  88.5 7.1 %grid.1 = f32[64,4096]{1,0:T(8,128)} custom-call(f32[64,1024]{1,0:T(8,128)} %get-tuple-element.38.keep_ref, bf16[64,1024]{1,0:T(8,128)(2,1)S(1)} %collective-permute-done.1.got_ref, bf16[4096,1024]{1,0:T(8,128)(2,1)} %get-tuple-element.40.g_ref), custom_call_target="tpu_custom_call" | custom-call | tf_op jit(solution)/shard_map/grid/pallas_call | solution.py:228
Async XLA Ops:
  10.3 32.9 %all-to-all-start = ((bf16[128,3,4,128]{3,2,1,0:T(4,128)(2,1)}), bf16[128,3,4,128]{3,2,1,0:T(4,128)(2,1)S(1)}, u32[]{:S(2)}, u32[]{:S(2)}) async-start(bf16[128,3,4,128]{3,2,1,0:T(4,128)(2,1)} %bitcast.18), calls=%async_computation | async-start | bytes 786432 | tf_op jit(solution)/shard_map/all_to_all | solution.py:242
  46.8 3.6 %collective-permute-start = (bf16[128,1280]{1,0:T(8,128)(2,1)S(1)}, bf16[128,1280]{1,0:T(8,128)(2,1)S(1)}, u32[]{:S(2)}, u32[]{:S(2)}) collective-permute-start(bf16[128,1280]{1,0:T(8,128)(2,1)S(1)} %get-tuple-element.25.part), channel_id=1, source_target_pairs={{0,1},{1,0},{2,3},{3,2},{4,5},{5,4},{6,7},{7,6},{8,9},{9,8},{10,11... | collective-permute-start | bytes 983048 | tf_op jit(solution)/shard_map/ppermute | solution.py:310
  57.9 23.3 %all-to-all-start.1 = ((bf16[128,3,4,128]{3,2,1,0:T(4,128)(2,1)}), bf16[128,3,4,128]{3,2,1,0:T(4,128)(2,1)S(1)}, u32[]{:S(2)}, u32[]{:S(2)}) async-start(bf16[128,3,4,128]{3,2,1,0:T(4,128)(2,1)} %bitcast.17), calls=%async_computation.1 | async-start | bytes 786432 | tf_op jit(solution)/shard_map/all_to_all | solution.py:242
  85.4 3.1 %collective-permute-start.1 = (bf16[64,1024]{1,0:T(8,128)(2,1)}, bf16[64,1024]{1,0:T(8,128)(2,1)S(1)}, u32[]{:S(2)}, u32[]{:S(2)}) collective-permute-start(bf16[64,1024]{1,0:T(8,128)(2,1)} %get-tuple-element.39), channel_id=1, source_target_pairs={{0,1},{1,0},{2,3},{3,2},{4,5},{5,4},{6,7},{7,6},{8,9},{9,8},{10,11... | collective-permute-start | bytes 393224 | tf_op jit(solution)/shard_map/ppermute | solution.py:343

commit v3 on v2

v3 whole, which is shorter than its diff:
```python
import jax
import jax.numpy as jnp
from jax import lax
from jax.experimental import pallas as pl
from jax.experimental.pallas import tpu as pltpu
from jax.sharding import PartitionSpec as P

BF = jnp.bfloat16
F32 = jnp.float32
I16 = jnp.int16
I32 = jnp.int32
LANES = 128
HALF_DEPTH = 8
SLOTS = 4
ROWS = HALF_DEPTH + SLOTS
SWAP = [(0, 1), (1, 0)]
CHUNK = 512


def dot(a, b, ca=1, cb=0):
    return lax.dot_general(a, b, (((ca,), (cb,)), ((), ())), preferred_element_type=F32)


def iota(shape, axis):
    return lax.broadcasted_iota(I32, shape, axis)


def eq_bf16(a, b):
    return jnp.where(a == b, jnp.asarray(1, BF), jnp.asarray(0, BF))


def build_counts(dst, tiles, height, lane0=0, row0=0, sub=16, unroll=4):
    cols = [[jnp.broadcast_to(r, (sub, LANES)).astype(I16) for r in rows] for rows in tiles]
    start = (iota((sub, LANES), 0) + row0).astype(I16)

    def body(i, at):
        s = pl.multiple_of(row0 + i * sub, sub)
        for t, rows in enumerate(cols):
            acc = eq_bf16(rows[0], at)
            for r in rows[1:]:
                acc = acc + eq_bf16(r, at)
            dst[pl.ds(s, sub), lane0 + t * LANES : lane0 + (t + 1) * LANES] = acc
        return at + jnp.asarray(sub, I16)

    lax.fori_loop(0, height // sub, body, start, unroll=unroll)


def row_copies(src, dst, sems, starts, size, targets=None):
    targets = starts if targets is None else targets
    return [
        pltpu.make_async_copy(src.at[pl.ds(a, size), :], dst.at[pl.ds(b, size), :], sems.at[k])
        for k, (a, b) in enumerate(zip(starts, targets))
    ]


def chunks(total):
    return range(0, total, CHUNK)


def lane_tiles(rows, first=0, last=None):
    last = rows.shape[1] // LANES if last is None else last
    return [
        [rows[k : k + 1, t * LANES : (t + 1) * LANES] for k in range(rows.shape[0])]
        for t in range(first, last)
    ]


def block_of(shape):
    row = iota(shape, 1)
    peer = jnp.floor((row.astype(F32) + 0.5) * (1.0 / ROWS)).astype(I32)
    return peer, row - peer * ROWS


def place_rows(dst, slots):
    c = iota((1, slots * LANES), 1)
    build_counts(dst, lane_tiles((c & 127) * ROWS + HALF_DEPTH + (c >> 7)), dst.shape[0])


def take_rows(dst, slots):
    peer, within = block_of((1, dst.shape[1]))
    slot = within - HALF_DEPTH
    build_counts(dst, lane_tiles(jnp.where(slot >= 0, slot * LANES + peer, -1)), slots * LANES)


def send_index(picked, rows):
    peers = picked.shape[1]
    table = jnp.concatenate([picked >> 5, picked & 31], axis=0).astype(F32).astype(BF)
    peer, within = block_of((1, rows))
    spread = jnp.where(iota((peers, rows), 0) == peer, 1.0, 0.0).astype(BF)
    out = dot(table, spread)
    node = out[:HALF_DEPTH, :] * 32.0 + out[HALF_DEPTH:, :]
    hit = iota((HALF_DEPTH, rows), 0) == within
    index = jnp.sum(jnp.where(hit, node, 0.0), axis=0, keepdims=True)
    return jnp.where(within >= HALF_DEPTH, -1.0, index).astype(I32)


def encode_kernel(
    feat_ref, inc_h, edges, send, owner, nodes, obs, msg, ginc, target, g, r, c_s, inc, sem
):
    feat = feat_ref[0]
    rows = msg.shape[0]
    load = pltpu.make_async_copy(inc_h, inc, sem)
    load.start()
    build_counts(g, lane_tiles(edges[...]), inc.shape[0])
    picked = jnp.where(feat == 0, send[:HALF_DEPTH, :], send[HALF_DEPTH:, :])
    build_counts(r, lane_tiles(send_index(picked, rows)), ginc.shape[1])
    place_rows(c_s, 3)
    sites = owner.shape[1]
    own = owner[...]
    member = jnp.where(iota((LANES, sites), 0) == own, 1.0, 0.0)
    member_b = member.astype(BF)
    upper = jnp.where(iota((sites, sites), 0) < iota((sites, sites), 1), 1.0, 0.0).astype(BF)
    rank = jnp.sum(dot(member_b, upper) * member, axis=0, keepdims=True)
    target[...] = own * ROWS + HALF_DEPTH + rank.astype(I32)
    slot0 = (2 * feat).astype(F32)
    obs_0 = dot(jnp.where(rank == slot0, member, 0.0).astype(BF), obs[...])
    obs_1 = dot(jnp.where(rank == slot0 + 1.0, member, 0.0).astype(BF), obs[...])
    n = nodes[...]
    high = ((n >> 5) + 1).astype(F32)
    low = (n & 31).astype(F32)
    lists = [jnp.where(rank == float(k), v, 0.0) for v in (high, low) for k in range(SLOTS)]
    lists.append(jnp.zeros((LANES - 2 * SLOTS * n.shape[0], sites), F32))
    listed = dot(member_b, jnp.concatenate(lists, axis=0).astype(BF), 1, 1)
    site_rows = dot(c_s[...], jnp.concatenate([obs_0, obs_1, listed], axis=0).astype(BF))
    load.wait()
    mean = (dot(inc[...], g[...], 0, 0) * (1.0 / edges.shape[0])).astype(BF)
    ginc[...] = mean
    msg[...] = (dot(mean, r[...]).T + site_rows).astype(BF)


def prepare_kernel(
    edges, mask, w_in, w_node1, w_node2, w_out, m_h, w_cat, w_cat_t, w_ho, w_ho_t, w_io, w_io_t, m, sems
):
    rows = edges.shape[1]
    width = w_in.shape[1]
    variables = w_in.shape[0]
    wi = w_in[...]
    for k in range(2):
        w1 = w_node1[k * width : (k + 1) * width, :]
        w_cat[k * variables : (k + 1) * variables, :] = dot(wi, w1).astype(BF)
        w_cat_t[:, k * variables : (k + 1) * variables] = dot(w1, wi, 0, 1).astype(BF)
    w_ho[...] = dot(w_node2[...], w_out[...]).astype(BF)
    w_ho_t[...] = dot(w_out[...], w_node2[...], 0, 1).astype(BF)
    w_io[...] = dot(wi, w_out[...]).astype(BF)
    w_io_t[...] = dot(w_out[...], wi, 0, 1).astype(BF)
    e = edges[...]
    h = e - rows
    r = h & 15
    halo_row = rows + (r >> 3) * ((m.shape[0] - rows) // 2) + (h >> 4) * ROWS + (r & 7)
    at = jnp.where(mask[...] > 0, jnp.where(e < rows, e, halo_row), -1)
    tiles = lane_tiles(at)
    copies = row_copies(m, m_h, sems, chunks(m.shape[0]), CHUNK)
    for row0, copy in zip(chunks(m.shape[0]), copies):
        for first in range(0, len(tiles), 4):
            build_counts(m, tiles[first : first + 4], CHUNK, first * LANES, row0)
        copy.start()
    for copy in copies:
        copy.wait()


def mix_kernel(feat_ref, msg, ginc, m_h, part, node, c_s, m, sems):
    feat = feat_ref[0]
    rows = ginc.shape[1]
    half = rows // 2
    halo = rows + feat * msg.shape[0]
    starts = [feat * half] + [halo + k for k in chunks(msg.shape[0])]
    copies = row_copies(m_h, m, sems, starts, CHUNK, chunks(m.shape[0]))
    for copy in copies:
        copy.start()
    take_rows(c_s, 3)
    got = msg[...]
    sites = dot(c_s[...], got).T
    part[:, rows:] = sites[:, : 2 * LANES].astype(BF)
    lists = sites[: 2 * node.shape[0], 2 * LANES :]
    node[...] = ((lists[: node.shape[0], :] - 1.0) * 32.0 + lists[node.shape[0] :, :]).astype(I32)
    copies[0].wait()
    acc = dot(ginc[:, pl.ds(pl.multiple_of(feat * half, half), half)], m[:half, :])
    for k, copy in zip(chunks(msg.shape[0]), copies[1:]):
        copy.wait()
        acc = acc + dot(msg[k : k + CHUNK, :], m[half + k : half + k + CHUNK, :], 0, 0)
    part[:, :rows] = acc.astype(BF)


def site_kernel(node, s):
    degree = node.shape[0] // SLOTS
    tiles = [[node[k * degree + j : k * degree + j + 1, :] for j in range(degree)] for k in range(SLOTS)]
    build_counts(s, tiles, s.shape[0])


def node_kernel(
    feat_ref, part, other, ginc, m_h, s, w_cat, w_cat_t, w_ho, w_ho_t, w_io, w_io_t, msg, own, slope_s, c_s, m, sems
):
    feat = feat_ref[0]
    variables, rows = ginc.shape
    copies = row_copies(m_h, m, sems, chunks(m.shape[0]), CHUNK)
    for copy in copies:
        copy.start()
    place_rows(c_s, SLOTS)
    gi = ginc[...]
    agg = (part[:, :rows].astype(F32) + other[:, :rows].astype(F32)).astype(BF)
    pre = dot(w_cat_t[...], jnp.concatenate([gi, agg], axis=0))
    sig = 1.0 / (1.0 + jnp.exp(-pre))
    hidden = (pre * sig).astype(BF)
    slope_s[...] = sig * (1.0 + pre * (1.0 - sig))
    readout = (dot(w_ho_t[...], hidden) + dot(w_io_t[...], gi)).astype(BF)
    values = dot(readout, s[...])
    mine = part[:, rows:].astype(F32)
    theirs = other[:, rows:].astype(F32)
    first = jnp.where(feat == 0, mine, theirs)
    second = jnp.where(feat == 0, theirs, mine)
    diff = (values - jnp.concatenate([first, second], axis=1)).astype(BF)
    d = dot(diff, s[...], 1, 1).astype(BF)
    inner = (dot(w_ho[...], d) * slope_s[...]).astype(BF)
    n = variables // 2
    cols = pl.ds(pl.multiple_of(feat * n, n), n)
    agg_cols = pl.ds(pl.multiple_of(variables + feat * n, n), n)
    both = dot(jnp.concatenate([w_cat[cols, :], w_cat[agg_cols, :]], axis=0), inner)
    agg_grad = both[n:, :].T.astype(BF)
    placed = dot(c_s[...], values.T.astype(BF))
    for copy in copies:
        copy.wait()
    own[...] = dot(w_io[cols, :], d) + both[:n, :] + dot(m[:rows, :], agg_grad).T
    count = msg.shape[0]
    low = dot(m[rows : rows + count, :], agg_grad)
    high = dot(m[rows + count :, :], agg_grad)
    msg[...] = (jnp.concatenate([low, high], axis=1) + placed).astype(BF)


def scatter_kernel(edges, g_h, g, sems):
    tiles = lane_tiles(edges[...])
    copies = row_copies(g, g_h, sems, chunks(g.shape[0]), CHUNK)
    for row0, copy in zip(chunks(g.shape[0]), copies):
        build_counts(g, tiles, CHUNK, 0, row0)
        copy.start()
    for copy in copies:
        copy.wait()


def finish_kernel(msg, send, own, target, g_h, out_h, pred, r, p_s, g, out, in_sems, out_sems, *, degree):
    copies = row_copies(g_h, g, in_sems, chunks(g.shape[0]), CHUNK)
    for copy in copies:
        copy.start()
    count = msg.shape[0]
    for k in range(2):
        picked = send[k * HALF_DEPTH : (k + 1) * HALF_DEPTH, :]
        build_counts(r, lane_tiles(send_index(picked, count)), r.shape[0], k * count)
    build_counts(p_s, lane_tiles(target[...]), count)
    back = msg[...].T
    n = own.shape[0]
    pred[...] = dot(back, p_s[...]).T.astype(BF)
    grad = own[...] + dot(back[:n, :], r[:, :count], 1, 1) + dot(back[n:, :], r[:, count:], 1, 1)
    grad = (grad * (1.0 / degree)).astype(BF)
    stores = []
    for k, (a, copy) in enumerate(zip(chunks(g.shape[0]), copies)):
        copy.wait()
        out[:, a : a + CHUNK] = dot(grad, g[a : a + CHUNK, :], 1, 1)
        stores.append(
            pltpu.make_async_copy(
                out.at[:, pl.ds(a, CHUNK)], out_h.at[:, pl.ds(a, CHUNK)], out_sems.at[k]
            )
        )
        stores[-1].start()
    for store in stores:
        store.wait()


SCALAR = pl.BlockSpec(memory_space=pltpu.SMEM)
FULL = pl.BlockSpec(memory_space=pltpu.VMEM)
HBM = pl.BlockSpec(memory_space=pl.ANY)
STAY, LEAVE, COPY = "stay", "leave", "copy"


def vmem(x):
    return pltpu.with_memory_space_constraint(x, pltpu.VMEM)


def dma(n):
    return pltpu.SemaphoreType.DMA((n,))


def call(kernel, outs, args, scratch=(), scalar=True, far=(), name=None):
    return pl.pallas_call(
        kernel,
        out_shape=[
            pltpu.VMEM(s, t) if where == STAY else jax.ShapeDtypeStruct(s, t) for s, t, where in outs
        ],
        in_specs=[
            SCALAR if scalar and k == 0 else HBM if k in far else FULL for k in range(len(args))
        ],
        out_specs=[HBM if where == COPY else FULL for _, _, where in outs],
        scratch_shapes=list(scratch),
        name=name,
    )(*args)


def exchange(msg, domains):
    x = msg.reshape(domains, ROWS // 4, 4, msg.shape[1])
    x = lax.all_to_all(x, "dom", split_axis=0, concat_axis=0, tiled=True)
    return x.reshape(msg.shape)


def local(
    increments,
    w_in,
    w_node1,
    w_node2,
    w_out,
    grid_edges,
    mesh_edges,
    mesh_mask,
    send_rows,
    site_owner,
    site_nodes,
    site_obs,
):
    domains = lax.axis_size("dom")
    feat = lax.axis_index("feat").astype(I32).reshape(1)
    grid_rows, variables = increments.shape
    mesh_rows = mesh_edges.shape[0]
    inner = w_node2.shape[0]
    site_count = site_obs.shape[0]
    rows = domains * ROWS
    degree = grid_edges.shape[1]
    n = variables // 2
    neighbours = mesh_rows + 2 * rows
    grid_t = grid_edges.T
    send_t = send_rows[0].T
    msg, ginc, target = call(
        encode_kernel,
        [
            ((rows, variables), BF, LEAVE),
            ((variables, mesh_rows), BF, LEAVE),
            ((1, site_count), I32, LEAVE),
        ],
        (feat, increments, grid_t, send_t, site_owner.T, site_nodes.T, site_obs),
        [
            pltpu.VMEM((grid_rows, mesh_rows), BF),
            pltpu.VMEM((mesh_rows, rows), BF),
            pltpu.VMEM((rows, 3 * LANES), BF),
            pltpu.VMEM((grid_rows, variables), BF),
            pltpu.SemaphoreType.DMA,
        ],
        far=(1,),
        name="encode",
    )
    m, *weights = call(
        prepare_kernel,
        [
            ((neighbours, mesh_rows), BF, COPY),
            ((2 * variables, inner), BF, LEAVE),
            ((inner, 2 * variables), BF, LEAVE),
            ((inner, variables), BF, LEAVE),
            ((variables, inner), BF, LEAVE),
            ((variables, variables), BF, LEAVE),
            ((variables, variables), BF, LEAVE),
        ],
        (mesh_edges.T, mesh_mask.T, w_in, w_node1, w_node2, w_out),
        [pltpu.VMEM((neighbours, mesh_rows), BF), dma(neighbours // CHUNK)],
        scalar=False,
        name="prepare",
    )
    got = exchange(msg, domains)
    part, node = call(
        mix_kernel,
        [
            ((variables, mesh_rows + 2 * LANES), BF, STAY),
            ((SLOTS * site_nodes.shape[1], LANES), I32, STAY),
        ],
        (feat, vmem(got), ginc, m),
        [
            pltpu.VMEM((3 * LANES, rows), BF),
            pltpu.VMEM((mesh_rows // 2 + rows, mesh_rows), BF),
            dma((mesh_rows // 2 + rows) // CHUNK),
        ],
        far=(3,),
        name="mix",
    )
    other = lax.ppermute(part, "feat", SWAP)
    (sites,) = call(
        site_kernel,
        [((mesh_rows, SLOTS * domains), BF, STAY)],
        (vmem(node),),
        scalar=False,
        name="sites",
    )
    back, own = call(
        node_kernel,
        [((rows, variables), BF, LEAVE), ((n, mesh_rows), F32, LEAVE)],
        (feat, vmem(part), vmem(other), ginc, m, vmem(sites), *weights),
        [
            pltpu.VMEM((inner, mesh_rows), F32),
            pltpu.VMEM((rows, SLOTS * LANES), BF),
            pltpu.VMEM((neighbours, mesh_rows), BF),
            dma(neighbours // CHUNK),
        ],
        far=(4,),
        name="node",
    )
    got_back = exchange(back, domains)
    (g,) = call(
        scatter_kernel,
        [((grid_rows, mesh_rows), BF, COPY)],
        (grid_t,),
        [pltpu.VMEM((grid_rows, mesh_rows), BF), dma(grid_rows // CHUNK)],
        scalar=False,
        name="scatter",
    )

    def finish(*refs):
        finish_kernel(*refs, degree=degree)

    grad, site_pred = call(
        finish,
        [((n, grid_rows), F32, COPY), ((site_count, variables), BF, LEAVE)],
        (vmem(got_back), send_t, own, target, g),
        [
            pltpu.VMEM((mesh_rows, 2 * rows), BF),
            pltpu.VMEM((rows, site_count), BF),
            pltpu.VMEM((grid_rows, mesh_rows), BF),
            pltpu.VMEM((n, grid_rows), F32),
            dma(grid_rows // CHUNK),
            dma(grid_rows // CHUNK),
        ],
        scalar=False,
        far=(4,),
        name="finish",
    )
    return (grad.T, site_pred)


def solution(mesh):
    return jax.shard_map(
        local,
        mesh=mesh,
        in_specs=(
            P("dom", None),
            P(),
            P(),
            P(),
            P(),
            P("dom", None),
            P("dom", None),
            P("dom", None),
            P("dom", None, None),
            P("dom", None),
            P("dom", None),
            P("dom", None),
        ),
        out_specs=(P("dom", "feat"), P("dom", None)),
        check_vma=False,
    )
```

time: 96 us -> 92.5 us (0.964)
  starting transfers between devices: 26.9 us -> 25 us
  Pallas kernels: 49.1 us -> 47.6 us
    ppermute x1 -> x0, starting transfers between devices: 1.91 us -> none  [local(): take = lax.ppermute(give, 'feat', SWAP)]
    pallas_call x8 -> x7, Pallas kernels: 49.1 us -> 47.6 us  [call(): pl.pallas_call(kernel, out_shape=[pltpu.VMEM(s, t) if where == STAY else...]
    ppermute x1 -> x0, waiting for transfers between devices: 1.2 us -> none  [local(): take = lax.ppermute(give, 'feat', SWAP)]
  transfers between devices with their start and end apart: 4 -> 3, of which waited for: 4 -> 3; matrix products, arithmetic and copies ran while one was open for 0% -> 0% of each run, Pallas kernels for 18% -> 18%
where the time goes in v3:
time: 92.5 us; the launch traced here: 92.1 us
  Pallas kernels  47.6 us (51%)
  starting transfers between devices  25 us (27%)
  waiting for transfers between devices  18.6 us (20%)
    pallas_call x7, Pallas kernels, call(): pl.pallas_call(kernel, out_shape=[pltpu.VMEM(s, t) if where == STAY else...  47.6 us
    all_to_all x2, starting transfers between devices, exchange(): x = lax.all_to_all(x, 'dom', split_axis=0, concat_axis=0, tiled=True)  22.5 us
    all_to_all x2, waiting for transfers between devices, exchange(): x = lax.all_to_all(x, 'dom', split_axis=0, concat_axis=0, tiled=True)  18.3 us
    ppermute x1, starting transfers between devices, local(): other = lax.ppermute(part, 'feat', SWAP)  2.5 us
  transfers between devices with their start and end apart: 3, of which 3 were waited for; matrix products, arithmetic and copies ran while one was open for 0% of the time, Pallas kernels for 18%

profile of v3, /device:TPU:1, one launch (start us, length us, event | category | flops | bytes accessed | tf_op | source)
XLA Modules:
  0.0 92.1 jit_solution(7190879385233932959)
XLA Ops:
  0.6 9.5 %encode.1 = (bf16[1536,128]{1,0:T(8,128)(2,1)}, bf16[128,1024]{1,0:T(8,128)(2,1)}, s32[1,256]{1,0:T(1,128)}) custom-call(s32[1]{0:T(128)} %bitcast.feat_ref, bf16[4096,128]{1,0:T(8,128)(2,1)} %inc_h.1, s32[4,1024]{1,0:T(4,128)} %bitcast.18, s32[16,128]{1,0:T(8,128)} %bitcast.22, s32[1,256]{1,0:T(1,128)} %bitcast.25, s32[8,256]{1,0:T(8,128)} %bitcast.24, ...), custom_call_target="tpu_custom_call" | custom-call | tf_op jit(solution)/shard_map/encode/pallas_call | solution.py:282
  10.2 16.3 %all-to-all-start = ((bf16[128,3,4,128]{3,2,1,0:T(4,128)(2,1)}), bf16[128,3,4,128]{3,2,1,0:T(4,128)(2,1)S(1)}, u32[]{:S(2)}, u32[]{:S(2)}) async-start(bf16[128,3,4,128]{3,2,1,0:T(4,128)(2,1)} %bitcast.17), calls=%async_computation | async-start | bytes 786432 | tf_op jit(solution)/shard_map/all_to_all | solution.py:298
  26.5 9.6 %prepare.1 = (bf16[4096,1024]{1,0:T(8,128)(2,1)}, bf16[256,512]{1,0:T(8,128)(2,1)}, bf16[512,256]{1,0:T(8,128)(2,1)}, bf16[512,128]{1,0:T(8,128)(2,1)}, bf16[128...) custom-call(s32[6,1024]{1,0:T(8,128)} %bitcast.20, s32[6,1024]{1,0:T(8,128)} %bitcast.21, ...), custom_call_target="tpu_custom_call" | custom-call | tf_op jit(solution)/shard_map/prepare/pallas_call | solution.py:282
  36.1 7.0 %all-to-all-done = bf16[128,3,4,128]{3,2,1,0:T(4,128)(2,1)S(1)} async-done(((bf16[128,3,4,128]{3,2,1,0:T(4,128)(2,1)}), bf16[128,3,4,128]{3,2,1,0:T(4,128)(2,1)S(1)}, u32[]{:S(2)}, u32[]{:S(2)}) %all-to-all-start) | async-done | bytes 393248 | tf_op jit(solution)/shard_map/all_to_all | solution.py:298
  43.1 3.7 %mix.1 = (bf16[128,1280]{1,0:T(8,128)(2,1)S(1)}, s32[32,128]{1,0:T(8,128)S(1)}) custom-call(s32[1]{0:T(128)} %bitcast.feat_ref, bf16[1536,128]{1,0:T(8,128)(2,1)S(1)} %bitcast.14, bf16[128,1024]{1,0:T(8,128)(2,1)} %get-tuple-element.19.ginc, bf16[4096,1024]{1,0:T(8,128)(2,1)} %get-tuple-element.20.m_h), custom_call_target="tpu_custom_call" | custom-call | tf_op jit(solution)/shard_map/mix/pallas_call | solution.py:282
  46.8 2.5 %collective-permute-start = (bf16[128,1280]{1,0:T(8,128)(2,1)S(1)}, bf16[128,1280]{1,0:T(8,128)(2,1)S(1)}, u32[]{:S(2)}, u32[]{:S(2)}) collective-permute-start(bf16[128,1280]{1,0:T(8,128)(2,1)S(1)} %get-tuple-element.21.part), channel_id=1, source_target_pairs={{0,1},{1,0},{2,3},{3,2},{4,5},{5,4},{6,7},{7,6},{8,9},{9,8},{10,11... | collective-permute-start | bytes 983048 | tf_op jit(solution)/shard_map/ppermute | solution.py:378
  49.3 1.0 %sites.1.s = bf16[1024,512]{1,0:T(8,128)(2,1)S(1)} custom-call(s32[32,128]{1,0:T(8,128)S(1)} %get-tuple-element.22.node), custom_call_target="tpu_custom_call" | custom-call | tf_op jit(solution)/shard_map/sites/pallas_call | solution.py:282
  50.3 0.3 collective-permute-done.other
  50.6 8.5 %node.1 = (bf16[1536,128]{1,0:T(8,128)(2,1)}, f32[64,1024]{1,0:T(8,128)}) custom-call(s32[1]{0:T(128)} %bitcast.feat_ref, bf16[128,1280]{1,0:T(8,128)(2,1)S(1)} %get-tuple-element.21.part, bf16[128,1280]{1,0:T(8,128)(2,1)S(1)} %collective-permute-done.other, bf16[128,1024]{1,0:T(8,128)(2,1)} %get-tuple-element.19.ginc, ...), custom_call_target="tpu_custom_call" | custom-call | tf_op jit(solution)/shard_map/node/pallas_call | solution.py:282
  59.1 6.2 %all-to-all-start.1 = ((bf16[128,3,4,128]{3,2,1,0:T(4,128)(2,1)}), bf16[128,3,4,128]{3,2,1,0:T(4,128)(2,1)S(1)}, u32[]{:S(2)}, u32[]{:S(2)}) async-start(bf16[128,3,4,128]{3,2,1,0:T(4,128)(2,1)} %bitcast.16), calls=%async_computation.1 | async-start | bytes 786432 | tf_op jit(solution)/shard_map/all_to_all | solution.py:298
  65.3 5.6 %scatter.1.refs_4_ = bf16[4096,1024]{1,0:T(8,128)(2,1)} custom-call(s32[4,1024]{1,0:T(4,128)} %bitcast.19), custom_call_target="tpu_custom_call" | custom-call | tf_op jit(solution)/shard_map/scatter/pallas_call | solution.py:282
  70.9 11.3 %all-to-all-done.1 = bf16[128,3,4,128]{3,2,1,0:T(4,128)(2,1)S(1)} async-done(((bf16[128,3,4,128]{3,2,1,0:T(4,128)(2,1)}), bf16[128,3,4,128]{3,2,1,0:T(4,128)(2,1)S(1)}, u32[]{:S(2)}, u32[]{:S(2)}) %all-to-all-start.1) | async-done | bytes 393248 | tf_op jit(solution)/shard_map/all_to_all | solution.py:298
  82.2 9.8 %finish.1 = (f32[64,4096]{1,0:T(8,128)}, bf16[256,128]{1,0:T(8,128)(2,1)}) custom-call(bf16[1536,128]{1,0:T(8,128)(2,1)S(1)} %bitcast.15, s32[16,128]{1,0:T(8,128)} %bitcast.23, f32[64,1024]{1,0:T(8,128)} %get-tuple-element.30.refs_2_, s32[1,256]{1,0:T(1,128)} %get-tuple-element.31.refs_3_, bf16[4096,1024]{1,0:T(8,128)(2,1)} %scatter.1.refs_4_), custom_call_target="tpu_custom_call" | custom-call | tf_op jit(solution)/shard_map/finish/pallas_call | solution.py:282
Async XLA Ops:
  10.2 32.9 %all-to-all-start = ((bf16[128,3,4,128]{3,2,1,0:T(4,128)(2,1)}), bf16[128,3,4,128]{3,2,1,0:T(4,128)(2,1)S(1)}, u32[]{:S(2)}, u32[]{:S(2)}) async-start(bf16[128,3,4,128]{3,2,1,0:T(4,128)(2,1)} %bitcast.17), calls=%async_computation | async-start | bytes 786432 | tf_op jit(solution)/shard_map/all_to_all | solution.py:298
  46.8 3.8 %collective-permute-start = (bf16[128,1280]{1,0:T(8,128)(2,1)S(1)}, bf16[128,1280]{1,0:T(8,128)(2,1)S(1)}, u32[]{:S(2)}, u32[]{:S(2)}) collective-permute-start(bf16[128,1280]{1,0:T(8,128)(2,1)S(1)} %get-tuple-element.21.part), channel_id=1, source_target_pairs={{0,1},{1,0},{2,3},{3,2},{4,5},{5,4},{6,7},{7,6},{8,9},{9,8},{10,11... | collective-permute-start | bytes 983048 | tf_op jit(solution)/shard_map/ppermute | solution.py:378
  59.1 23.1 %all-to-all-start.1 = ((bf16[128,3,4,128]{3,2,1,0:T(4,128)(2,1)}), bf16[128,3,4,128]{3,2,1,0:T(4,128)(2,1)S(1)}, u32[]{:S(2)}, u32[]{:S(2)}) async-start(bf16[128,3,4,128]{3,2,1,0:T(4,128)(2,1)} %bitcast.16), calls=%async_computation.1 | async-start | bytes 786432 | tf_op jit(solution)/shard_map/all_to_all | solution.py:298

commit v4 on v3

--- a/solution.py
+++ b/solution.py
@@ -45,6 +45,26 @@
     lax.fori_loop(0, height // sub, body, start, unroll=unroll)
 
 
+def build_rows(dst, index, rows, degree, block=128, unroll=2, after=None):
+    start = iota((block, LANES), 1).astype(I16)
+    for n, s in enumerate(range(0, rows, block)):
+        cols = [
+            jnp.broadcast_to(index[s : s + block, k : k + 1], (block, LANES)).astype(I16)
+            for k in range(degree)
+        ]
+
+        def body(w, at, s=s, cols=cols):
+            acc = eq_bf16(cols[0], at)
+            for c in cols[1:]:
+                acc = acc + eq_bf16(c, at)
+            dst[s : s + block, pl.ds(pl.multiple_of(w * LANES, LANES), LANES)] = acc
+            return at + jnp.asarray(LANES, I16)
+
+        lax.fori_loop(0, dst.shape[1] // LANES, body, start, unroll=unroll)
+        if after is not None:
+            after(n)
+
+
 def row_copies(src, dst, sems, starts, size, targets=None):
     targets = starts if targets is None else targets
     return [
@@ -65,67 +85,46 @@
     ]
 
 
-def block_of(shape):
-    row = iota(shape, 1)
-    peer = jnp.floor((row.astype(F32) + 0.5) * (1.0 / ROWS)).astype(I32)
-    return peer, row - peer * ROWS
-
-
-def place_rows(dst, slots):
-    c = iota((1, slots * LANES), 1)
-    build_counts(dst, lane_tiles((c & 127) * ROWS + HALF_DEPTH + (c >> 7)), dst.shape[0])
-
-
-def take_rows(dst, slots):
-    peer, within = block_of((1, dst.shape[1]))
-    slot = within - HALF_DEPTH
-    build_counts(dst, lane_tiles(jnp.where(slot >= 0, slot * LANES + peer, -1)), slots * LANES)
-
-
-def send_index(picked, rows):
-    peers = picked.shape[1]
-    table = jnp.concatenate([picked >> 5, picked & 31], axis=0).astype(F32).astype(BF)
-    peer, within = block_of((1, rows))
-    spread = jnp.where(iota((peers, rows), 0) == peer, 1.0, 0.0).astype(BF)
-    out = dot(table, spread)
-    node = out[:HALF_DEPTH, :] * 32.0 + out[HALF_DEPTH:, :]
-    hit = iota((HALF_DEPTH, rows), 0) == within
-    index = jnp.sum(jnp.where(hit, node, 0.0), axis=0, keepdims=True)
-    return jnp.where(within >= HALF_DEPTH, -1.0, index).astype(I32)
+def peer_rows(k):
+    return pl.ds(k, LANES, stride=ROWS)
 
 
 def encode_kernel(
-    feat_ref, inc_h, edges, send, owner, nodes, obs, msg, ginc, target, g, r, c_s, inc, sem
+    feat_ref, inc_h, edges, send, owner, nodes, obs, msg, ginc, target, g, r, wide, inc, sem
 ):
     feat = feat_ref[0]
-    rows = msg.shape[0]
     load = pltpu.make_async_copy(inc_h, inc, sem)
     load.start()
     build_counts(g, lane_tiles(edges[...]), inc.shape[0])
     picked = jnp.where(feat == 0, send[:HALF_DEPTH, :], send[HALF_DEPTH:, :])
-    build_counts(r, lane_tiles(send_index(picked, rows)), ginc.shape[1])
-    place_rows(c_s, 3)
+    build_counts(r, [[picked[k : k + 1, :]] for k in range(HALF_DEPTH)], r.shape[0])
     sites = owner.shape[1]
     own = owner[...]
     member = jnp.where(iota((LANES, sites), 0) == own, 1.0, 0.0)
     member_b = member.astype(BF)
     upper = jnp.where(iota((sites, sites), 0) < iota((sites, sites), 1), 1.0, 0.0).astype(BF)
     rank = jnp.sum(dot(member_b, upper) * member, axis=0, keepdims=True)
-    target[...] = own * ROWS + HALF_DEPTH + rank.astype(I32)
-    slot0 = (2 * feat).astype(F32)
-    obs_0 = dot(jnp.where(rank == slot0, member, 0.0).astype(BF), obs[...])
-    obs_1 = dot(jnp.where(rank == slot0 + 1.0, member, 0.0).astype(BF), obs[...])
+    target[...] = rank.astype(I32) * LANES + own
+    for k in range(2):
+        slot = (2 * feat + k).astype(F32)
+        wide[peer_rows(HALF_DEPTH + k), :] = dot(
+            jnp.where(rank == slot, member, 0.0).astype(BF), obs[...]
+        )
     n = nodes[...]
     high = ((n >> 5) + 1).astype(F32)
     low = (n & 31).astype(F32)
     lists = [jnp.where(rank == float(k), v, 0.0) for v in (high, low) for k in range(SLOTS)]
     lists.append(jnp.zeros((LANES - 2 * SLOTS * n.shape[0], sites), F32))
-    listed = dot(member_b, jnp.concatenate(lists, axis=0).astype(BF), 1, 1)
-    site_rows = dot(c_s[...], jnp.concatenate([obs_0, obs_1, listed], axis=0).astype(BF))
+    listed = jnp.concatenate(lists, axis=0).astype(BF)
+    wide[peer_rows(HALF_DEPTH + 2), :] = dot(member_b, listed, 1, 1)
+    wide[peer_rows(HALF_DEPTH + 3), :] = jnp.zeros((LANES, LANES), F32)
     load.wait()
     mean = (dot(inc[...], g[...], 0, 0) * (1.0 / edges.shape[0])).astype(BF)
     ginc[...] = mean
-    msg[...] = (dot(mean, r[...]).T + site_rows).astype(BF)
+    out = dot(mean, r[...])
+    for k in range(HALF_DEPTH):
+        wide[peer_rows(k), :] = out[:, k * LANES : (k + 1) * LANES].T
+    msg[...] = wide[...].astype(BF)
 
 
 def prepare_kernel(
@@ -146,8 +145,7 @@
     e = edges[...]
     h = e - rows
     r = h & 15
-    halo_row = rows + (r >> 3) * ((m.shape[0] - rows) // 2) + (h >> 4) * ROWS + (r & 7)
-    at = jnp.where(mask[...] > 0, jnp.where(e < rows, e, halo_row), -1)
+    at = jnp.where(mask[...] > 0, jnp.where(e < rows, e, rows + r * LANES + (h >> 4)), -1)
     tiles = lane_tiles(at)
     copies = row_copies(m, m_h, sems, chunks(m.shape[0]), CHUNK)
     for row0, copy in zip(chunks(m.shape[0]), copies):
@@ -158,26 +156,30 @@
         copy.wait()
 
 
-def mix_kernel(feat_ref, msg, ginc, m_h, part, node, c_s, m, sems):
+def mix_kernel(feat_ref, msg, ginc, m_h, part, node, wide, m, sems):
     feat = feat_ref[0]
     rows = ginc.shape[1]
     half = rows // 2
-    halo = rows + feat * msg.shape[0]
-    starts = [feat * half] + [halo + k for k in chunks(msg.shape[0])]
+    count = HALF_DEPTH * LANES
+    halo = rows + feat * count
+    starts = [feat * half] + [halo + k for k in range(0, count, CHUNK)]
     copies = row_copies(m_h, m, sems, starts, CHUNK, chunks(m.shape[0]))
     for copy in copies:
         copy.start()
-    take_rows(c_s, 3)
-    got = msg[...]
-    sites = dot(c_s[...], got).T
-    part[:, rows:] = sites[:, : 2 * LANES].astype(BF)
-    lists = sites[: 2 * node.shape[0], 2 * LANES :]
-    node[...] = ((lists[: node.shape[0], :] - 1.0) * 32.0 + lists[node.shape[0] :, :]).astype(I32)
+    wide[...] = msg[...].astype(F32)
+    for k in range(2):
+        part[:, rows + k * LANES : rows + (k + 1) * LANES] = (
+            wide[peer_rows(HALF_DEPTH + k), :].T.astype(BF)
+        )
+    lists = wide[peer_rows(HALF_DEPTH + 2), :].T
+    n = node.shape[0]
+    node[...] = ((lists[:n, :] - 1.0) * 32.0 + lists[n : 2 * n, :]).astype(I32)
+    got = jnp.concatenate([wide[peer_rows(k), :].T for k in range(HALF_DEPTH)], axis=1).astype(BF)
     copies[0].wait()
     acc = dot(ginc[:, pl.ds(pl.multiple_of(feat * half, half), half)], m[:half, :])
-    for k, copy in zip(chunks(msg.shape[0]), copies[1:]):
+    for k, copy in zip(range(0, count, CHUNK), copies[1:]):
         copy.wait()
-        acc = acc + dot(msg[k : k + CHUNK, :], m[half + k : half + k + CHUNK, :], 0, 0)
+        acc = acc + dot(got[:, k : k + CHUNK], m[half + k : half + k + CHUNK, :])
     part[:, :rows] = acc.astype(BF)
 
 
@@ -188,14 +190,13 @@
 
 
 def node_kernel(
-    feat_ref, part, other, ginc, m_h, s, w_cat, w_cat_t, w_ho, w_ho_t, w_io, w_io_t, msg, own, slope_s, c_s, m, sems
+    feat_ref, part, other, ginc, m_h, s, w_cat, w_cat_t, w_ho, w_ho_t, w_io, w_io_t, msg, own, slope_s, wide, m, sems
 ):
     feat = feat_ref[0]
     variables, rows = ginc.shape
     copies = row_copies(m_h, m, sems, chunks(m.shape[0]), CHUNK)
     for copy in copies:
         copy.start()
-    place_rows(c_s, SLOTS)
     gi = ginc[...]
     agg = (part[:, :rows].astype(F32) + other[:, :rows].astype(F32)).astype(BF)
     pre = dot(w_cat_t[...], jnp.concatenate([gi, agg], axis=0))
@@ -216,50 +217,60 @@
     agg_cols = pl.ds(pl.multiple_of(variables + feat * n, n), n)
     both = dot(jnp.concatenate([w_cat[cols, :], w_cat[agg_cols, :]], axis=0), inner)
     agg_grad = both[n:, :].T.astype(BF)
-    placed = dot(c_s[...], values.T.astype(BF))
+    site_rows = values.T
+    for k in range(SLOTS):
+        wide[peer_rows(HALF_DEPTH + k), :] = site_rows[k * LANES : (k + 1) * LANES, :]
     for copy in copies:
         copy.wait()
     own[...] = dot(w_io[cols, :], d) + both[:n, :] + dot(m[:rows, :], agg_grad).T
-    count = msg.shape[0]
+    count = HALF_DEPTH * LANES
     low = dot(m[rows : rows + count, :], agg_grad)
     high = dot(m[rows + count :, :], agg_grad)
-    msg[...] = (jnp.concatenate([low, high], axis=1) + placed).astype(BF)
-
-
-def scatter_kernel(edges, g_h, g, sems):
-    tiles = lane_tiles(edges[...])
-    copies = row_copies(g, g_h, sems, chunks(g.shape[0]), CHUNK)
-    for row0, copy in zip(chunks(g.shape[0]), copies):
-        build_counts(g, tiles, CHUNK, 0, row0)
-        copy.start()
+    halo = jnp.concatenate([low, high], axis=1)
+    for k in range(HALF_DEPTH):
+        wide[peer_rows(k), :] = halo[k * LANES : (k + 1) * LANES, :]
+    msg[...] = wide[...].astype(BF)
+
+
+def scatter_kernel(edges, target, g_h, target_col, g, sems):
+    e = edges[...]
+    columns = jnp.concatenate([e, e], axis=0).T
+    block = g.shape[0] // sems.shape[0]
+    copies = row_copies(g, g_h, sems, range(0, g.shape[0], block), block)
+    build_rows(g, columns, g.shape[0], e.shape[0], block, after=lambda n: copies[n].start())
+    target_col[...] = jnp.broadcast_to(target[...], (8, target.shape[1])).T[:, :1]
     for copy in copies:
         copy.wait()
 
 
-def finish_kernel(msg, send, own, target, g_h, out_h, pred, r, p_s, g, out, in_sems, out_sems, *, degree):
-    copies = row_copies(g_h, g, in_sems, chunks(g.shape[0]), CHUNK)
-    for copy in copies:
-        copy.start()
-    count = msg.shape[0]
-    for k in range(2):
-        picked = send[k * HALF_DEPTH : (k + 1) * HALF_DEPTH, :]
-        build_counts(r, lane_tiles(send_index(picked, count)), r.shape[0], k * count)
-    build_counts(p_s, lane_tiles(target[...]), count)
-    back = msg[...].T
+def finish_kernel(msg, send, own, target, g_h, out_h, pred, wide, r, g, out, in_sems, out_sems, *, degree):
+    width = g.shape[1] // in_sems.shape[0]
+    spans = [pl.ds(k * width, width) for k in range(in_sems.shape[0])]
+    loads = [
+        pltpu.make_async_copy(g_h.at[:, at], g.at[:, at], in_sems.at[k]) for k, at in enumerate(spans)
+    ]
+    stores = [
+        pltpu.make_async_copy(out.at[:, at], out_h.at[:, at], out_sems.at[k])
+        for k, at in enumerate(spans)
+    ]
+    for load in loads:
+        load.start()
+    depth = send.shape[0]
+    build_counts(r, [[send[k : k + 1, :]] for k in range(depth)], r.shape[0], unroll=2)
+    wide[...] = msg[...].astype(F32)
+    back = jnp.concatenate([wide[peer_rows(k), :] for k in range(HALF_DEPTH)], axis=0).astype(BF)
+    count = back.shape[0]
     n = own.shape[0]
-    pred[...] = dot(back, p_s[...]).T.astype(BF)
-    grad = own[...] + dot(back[:n, :], r[:, :count], 1, 1) + dot(back[n:, :], r[:, count:], 1, 1)
-    grad = (grad * (1.0 / degree)).astype(BF)
-    stores = []
-    for k, (a, copy) in enumerate(zip(chunks(g.shape[0]), copies)):
-        copy.wait()
-        out[:, a : a + CHUNK] = dot(grad, g[a : a + CHUNK, :], 1, 1)
-        stores.append(
-            pltpu.make_async_copy(
-                out.at[:, pl.ds(a, CHUNK)], out_h.at[:, pl.ds(a, CHUNK)], out_sems.at[k]
-            )
-        )
-        stores[-1].start()
+    low = dot(r[:, :count], back).T
+    high = dot(r[:, count:], back).T
+    grad = ((own[...] + low[:n, :] + high[n:, :]) * (1.0 / degree)).astype(BF)
+    slots = [wide[peer_rows(HALF_DEPTH + k), :] for k in range(SLOTS)]
+    pick = jnp.where(target[...] == iota((target.shape[0], SLOTS * LANES), 1), 1.0, 0.0).astype(BF)
+    pred[...] = dot(pick, jnp.concatenate(slots, axis=0).astype(BF)).astype(BF)
+    for at, load, store in zip(spans, loads, stores):
+        load.wait()
+        out[:, at] = dot(grad, g[:, at])
+        store.start()
     for store in stores:
         store.wait()
 
@@ -322,21 +333,22 @@
     rows = domains * ROWS
     degree = grid_edges.shape[1]
     n = variables // 2
-    neighbours = mesh_rows + 2 * rows
+    neighbours = mesh_rows + 2 * HALF_DEPTH * domains
+    wide = pltpu.VMEM((rows, variables), F32)
     grid_t = grid_edges.T
     send_t = send_rows[0].T
     msg, ginc, target = call(
         encode_kernel,
         [
             ((rows, variables), BF, LEAVE),
-            ((variables, mesh_rows), BF, LEAVE),
+            ((variables, mesh_rows), BF, STAY),
             ((1, site_count), I32, LEAVE),
         ],
         (feat, increments, grid_t, send_t, site_owner.T, site_nodes.T, site_obs),
         [
             pltpu.VMEM((grid_rows, mesh_rows), BF),
-            pltpu.VMEM((mesh_rows, rows), BF),
-            pltpu.VMEM((rows, 3 * LANES), BF),
+            pltpu.VMEM((mesh_rows, HALF_DEPTH * domains), BF),
+            wide,
             pltpu.VMEM((grid_rows, variables), BF),
             pltpu.SemaphoreType.DMA,
         ],
@@ -366,11 +378,11 @@
             ((variables, mesh_rows + 2 * LANES), BF, STAY),
             ((SLOTS * site_nodes.shape[1], LANES), I32, STAY),
         ],
-        (feat, vmem(got), ginc, m),
-        [
-            pltpu.VMEM((3 * LANES, rows), BF),
-            pltpu.VMEM((mesh_rows // 2 + rows, mesh_rows), BF),
-            dma((mesh_rows // 2 + rows) // CHUNK),
+        (feat, vmem(got), vmem(ginc), m),
+        [
+            wide,
+            pltpu.VMEM((neighbours // 2, mesh_rows), BF),
+            dma(neighbours // 2 // CHUNK),
         ],
         far=(3,),
         name="mix",
@@ -385,11 +397,11 @@
     )
     back, own = call(
         node_kernel,
-        [((rows, variables), BF, LEAVE), ((n, mesh_rows), F32, LEAVE)],
-        (feat, vmem(part), vmem(other), ginc, m, vmem(sites), *weights),
+        [((rows, variables), BF, LEAVE), ((n, mesh_rows), F32, STAY)],
+        (feat, vmem(part), vmem(other), vmem(ginc), m, vmem(sites), *weights),
         [
             pltpu.VMEM((inner, mesh_rows), F32),
-            pltpu.VMEM((rows, SLOTS * LANES), BF),
+            wide,
             pltpu.VMEM((neighbours, mesh_rows), BF),
             dma(neighbours // CHUNK),
         ],
@@ -397,11 +409,14 @@
         name="node",
     )
     got_back = exchange(back, domains)
-    (g,) = call(
+    g, target_col = call(
         scatter_kernel,
-        [((grid_rows, mesh_rows), BF, COPY)],
-        (grid_t,),
-        [pltpu.VMEM((grid_rows, mesh_rows), BF), dma(grid_rows // CHUNK)],
+        [
+            ((mesh_rows, grid_rows), BF, COPY),
+            ((site_count, 1), I32, STAY),
+        ],
+        (grid_t, target),
+        [pltpu.VMEM((mesh_rows, grid_rows), BF), dma(8)],
         scalar=False,
         name="scatter",
     )
@@ -412,14 +427,14 @@
     grad, site_pred = call(
         finish,
         [((n, grid_rows), F32, COPY), ((site_count, variables), BF, LEAVE)],
-        (vmem(got_back), send_t, own, target, g),
-        [
-            pltpu.VMEM((mesh_rows, 2 * rows), BF),
-            pltpu.VMEM((rows, site_count), BF),
-            pltpu.VMEM((grid_rows, mesh_rows), BF),
+        (vmem(got_back), send_t, vmem(own), vmem(target_col), g),
+        [
+            wide,
+            pltpu.VMEM((mesh_rows, 2 * HALF_DEPTH * domains), BF),
+            pltpu.VMEM((mesh_rows, grid_rows), BF),
             pltpu.VMEM((n, grid_rows), F32),
-            dma(grid_rows // CHUNK),
-            dma(grid_rows // CHUNK),
+            dma(8),
+            dma(8),
         ],
         scalar=False,
         far=(4,),

time: 92.5 us -> 85.6 us (0.925)
  Pallas kernels: 47.6 us -> 40.8 us
    pallas_call x7, Pallas kernels: 47.6 us -> 40.8 us  [call(): pl.pallas_call(kernel, out_shape=[pltpu.VMEM(s, t) if where == STAY else...]
  transfers between devices with their start and end apart: 3 -> 3, of which waited for: 3 -> 3; matrix products, arithmetic and copies ran while one was open for 0% -> 0% of each run, Pallas kernels for 18% -> 19%
where the time goes in v4:
time: 85.6 us; the launch traced here: 85.1 us
  Pallas kernels  40.8 us (48%)
  starting transfers between devices  25 us (29%)
  waiting for transfers between devices  18.4 us (21%)
  between operations  0.86 us (1%)
    pallas_call x7, Pallas kernels, call(): pl.pallas_call(kernel, out_shape=[pltpu.VMEM(s, t) if where == STAY else...  40.8 us
    all_to_all x2, starting transfers between devices, exchange(): x = lax.all_to_all(x, 'dom', split_axis=0, concat_axis=0, tiled=True)  22.7 us
    all_to_all x2, waiting for transfers between devices, exchange(): x = lax.all_to_all(x, 'dom', split_axis=0, concat_axis=0, tiled=True)  18.1 us
    ppermute x1, starting transfers between devices, local(): other = lax.ppermute(part, 'feat', SWAP)  2.32 us
  transfers between devices with their start and end apart: 3, of which 3 were waited for; matrix products, arithmetic and copies ran while one was open for 0% of the time, Pallas kernels for 19%

profile of v4, /device:TPU:1, one launch (start us, length us, event | category | flops | bytes accessed | tf_op | source)
XLA Modules:
  0.0 85.1 jit_solution(14839654735901771667)
XLA Ops:
  0.6 8.1 %encode.1 = (bf16[1536,128]{1,0:T(8,128)(2,1)}, bf16[128,1024]{1,0:T(8,128)(2,1)S(1)}, s32[1,256]{1,0:T(1,128)}) custom-call(s32[1]{0:T(128)} %bitcast.feat_ref, bf16[4096,128]{1,0:T(8,128)(2,1)} %inc_h.1, s32[4,1024]{1,0:T(4,128)} %bitcast.18, s32[16,128]{1,0:T(8,128)} %bitcast.22, s32[1,256]{1,0:T(1,128)} %bitcast.25, s32[8,256]{1,0:T(8,128)} %bitcast.24, ...), custom_call_target="tpu_custom_call" | custom-call | tf_op jit(solution)/shard_map/encode/pallas_call | solution.py:293
  8.8 16.3 %all-to-all-start = ((bf16[128,3,4,128]{3,2,1,0:T(4,128)(2,1)}), bf16[128,3,4,128]{3,2,1,0:T(4,128)(2,1)S(1)}, u32[]{:S(2)}, u32[]{:S(2)}) async-start(bf16[128,3,4,128]{3,2,1,0:T(4,128)(2,1)} %bitcast.17), calls=%async_computation | async-start | bytes 786432 | tf_op jit(solution)/shard_map/all_to_all | solution.py:309
  25.1 8.1 %prepare.1 = (bf16[3072,1024]{1,0:T(8,128)(2,1)}, bf16[256,512]{1,0:T(8,128)(2,1)}, bf16[512,256]{1,0:T(8,128)(2,1)}, bf16[512,128]{1,0:T(8,128)(2,1)}, bf16[128...) custom-call(s32[6,1024]{1,0:T(8,128)} %bitcast.20, s32[6,1024]{1,0:T(8,128)} %bitcast.21, ...), custom_call_target="tpu_custom_call" | custom-call | tf_op jit(solution)/shard_map/prepare/pallas_call | solution.py:293
  33.2 8.5 %all-to-all-done = bf16[128,3,4,128]{3,2,1,0:T(4,128)(2,1)S(1)} async-done(((bf16[128,3,4,128]{3,2,1,0:T(4,128)(2,1)}), bf16[128,3,4,128]{3,2,1,0:T(4,128)(2,1)S(1)}, u32[]{:S(2)}, u32[]{:S(2)}) %all-to-all-start) | async-done | bytes 393248 | tf_op jit(solution)/shard_map/all_to_all | solution.py:309
  41.7 2.2 %mix.1 = (bf16[128,1280]{1,0:T(8,128)(2,1)S(1)}, s32[32,128]{1,0:T(8,128)S(1)}) custom-call(s32[1]{0:T(128)} %bitcast.feat_ref, bf16[1536,128]{1,0:T(8,128)(2,1)S(1)} %bitcast.14, bf16[128,1024]{1,0:T(8,128)(2,1)S(1)} %get-tuple-element.21.ginc, bf16[3072,1024]{1,0:T(8,128)(2,1)} %get-tuple-element.22.m_h), custom_call_target="tpu_custom_call" | custom-call | tf_op jit(solution)/shard_map/mix/pallas_call | solution.py:293
  43.9 2.3 %collective-permute-start = (bf16[128,1280]{1,0:T(8,128)(2,1)S(1)}, bf16[128,1280]{1,0:T(8,128)(2,1)S(1)}, u32[]{:S(2)}, u32[]{:S(2)}) collective-permute-start(bf16[128,1280]{1,0:T(8,128)(2,1)S(1)} %get-tuple-element.23.part), channel_id=1, source_target_pairs={{0,1},{1,0},{2,3},{3,2},{4,5},{5,4},{6,7},{7,6},{8,9},{9,8},{10,11... | collective-permute-start | bytes 983048 | tf_op jit(solution)/shard_map/ppermute | solution.py:390
  46.3 1.0 %sites.1.s = bf16[1024,512]{1,0:T(8,128)(2,1)S(1)} custom-call(s32[32,128]{1,0:T(8,128)S(1)} %get-tuple-element.24.node), custom_call_target="tpu_custom_call" | custom-call | tf_op jit(solution)/shard_map/sites/pallas_call | solution.py:293
  47.2 0.3 collective-permute-done.other
  47.5 7.6 %node.1 = (bf16[1536,128]{1,0:T(8,128)(2,1)}, f32[64,1024]{1,0:T(8,128)S(1)}) custom-call(s32[1]{0:T(128)} %bitcast.feat_ref, bf16[128,1280]{1,0:T(8,128)(2,1)S(1)} %get-tuple-element.23.part, bf16[128,1280]{1,0:T(8,128)(2,1)S(1)} %collective-permute-done.other, bf16[128,1024]{1,0:T(8,128)(2,1)S(1)} %get-tuple-element.21.ginc, ...), custom_call_target="tpu_custom_call" | custom-call | tf_op jit(solution)/shard_map/node/pallas_call | solution.py:293
  55.1 6.4 %all-to-all-start.1 = ((bf16[128,3,4,128]{3,2,1,0:T(4,128)(2,1)}), bf16[128,3,4,128]{3,2,1,0:T(4,128)(2,1)S(1)}, u32[]{:S(2)}, u32[]{:S(2)}) async-start(bf16[128,3,4,128]{3,2,1,0:T(4,128)(2,1)} %bitcast.16), calls=%async_computation.1 | async-start | bytes 786432 | tf_op jit(solution)/shard_map/all_to_all | solution.py:309
  61.5 7.1 %scatter.1 = (bf16[1024,4096]{1,0:T(8,128)(2,1)}, s32[256,1]{1,0:T(8,128)S(1)}) custom-call(s32[4,1024]{1,0:T(4,128)} %bitcast.19, s32[1,256]{1,0:T(1,128)} %get-tuple-element.33.target), custom_call_target="tpu_custom_call" | custom-call | tf_op jit(solution)/shard_map/scatter/pallas_call | solution.py:293
  68.6 9.6 %all-to-all-done.1 = bf16[128,3,4,128]{3,2,1,0:T(4,128)(2,1)S(1)} async-done(((bf16[128,3,4,128]{3,2,1,0:T(4,128)(2,1)}), bf16[128,3,4,128]{3,2,1,0:T(4,128)(2,1)S(1)}, u32[]{:S(2)}, u32[]{:S(2)}) %all-to-all-start.1) | async-done | bytes 393248 | tf_op jit(solution)/shard_map/all_to_all | solution.py:309
  78.2 6.8 %finish.1 = (f32[64,4096]{1,0:T(8,128)}, bf16[256,128]{1,0:T(8,128)(2,1)}) custom-call(bf16[1536,128]{1,0:T(8,128)(2,1)S(1)} %bitcast.15, s32[16,128]{1,0:T(8,128)} %bitcast.23, f32[64,1024]{1,0:T(8,128)S(1)} %get-tuple-element.32.refs_2_, s32[256,1]{1,0:T(8,128)S(1)} %get-tuple-element.34.refs_3_, bf16[1024,4096]{1,0:T(8,128)(2,1)} %get-tuple-element.35.refs_4_), custom_call_target="tpu_custom_call" | custom-call | tf_op jit(solution)/shard_map/finish/pallas_call | solution.py:293
Async XLA Ops:
  8.8 32.9 %all-to-all-start = ((bf16[128,3,4,128]{3,2,1,0:T(4,128)(2,1)}), bf16[128,3,4,128]{3,2,1,0:T(4,128)(2,1)S(1)}, u32[]{:S(2)}, u32[]{:S(2)}) async-start(bf16[128,3,4,128]{3,2,1,0:T(4,128)(2,1)} %bitcast.17), calls=%async_computation | async-start | bytes 786432 | tf_op jit(solution)/shard_map/all_to_all | solution.py:309
  43.9 3.6 %collective-permute-start = (bf16[128,1280]{1,0:T(8,128)(2,1)S(1)}, bf16[128,1280]{1,0:T(8,128)(2,1)S(1)}, u32[]{:S(2)}, u32[]{:S(2)}) collective-permute-start(bf16[128,1280]{1,0:T(8,128)(2,1)S(1)} %get-tuple-element.23.part), channel_id=1, source_target_pairs={{0,1},{1,0},{2,3},{3,2},{4,5},{5,4},{6,7},{7,6},{8,9},{9,8},{10,11... | collective-permute-start | bytes 983048 | tf_op jit(solution)/shard_map/ppermute | solution.py:390
  55.1 23.1 %all-to-all-start.1 = ((bf16[128,3,4,128]{3,2,1,0:T(4,128)(2,1)}), bf16[128,3,4,128]{3,2,1,0:T(4,128)(2,1)S(1)}, u32[]{:S(2)}, u32[]{:S(2)}) async-start(bf16[128,3,4,128]{3,2,1,0:T(4,128)(2,1)} %bitcast.16), calls=%async_computation.1 | async-start | bytes 786432 | tf_op jit(solution)/shard_map/all_to_all | solution.py:309

commit v5 on v4

--- a/solution.py
+++ b/solution.py
@@ -90,9 +90,9 @@
 
 
 def encode_kernel(
-    feat_ref, inc_h, edges, send, owner, nodes, obs, msg, ginc, target, g, r, wide, inc, sem
-):
-    feat = feat_ref[0]
+    inc_h, edges, send, owner, nodes, obs, msg, ginc, target, g, r, wide, inc, sem
+):
+    feat = lax.axis_index("feat")
     load = pltpu.make_async_copy(inc_h, inc, sem)
     load.start()
     build_counts(g, lane_tiles(edges[...]), inc.shape[0])
@@ -128,9 +128,22 @@
 
 
 def prepare_kernel(
-    edges, mask, w_in, w_node1, w_node2, w_out, m_h, w_cat, w_cat_t, w_ho, w_ho_t, w_io, w_io_t, m, sems
+    edges, mask, ginc, w_in, w_node1, w_node2, w_out, m_h, part, w_cat, w_cat_t, w_ho, w_ho_t, w_io, w_io_t, m, sems
 ):
     rows = edges.shape[1]
+    e = edges[...]
+    h = e - rows
+    r = h & 15
+    at = jnp.where(mask[...] > 0, jnp.where(e < rows, e, rows + r * LANES + (h >> 4)), -1)
+    tiles = lane_tiles(at)
+    copies = row_copies(m, m_h, sems, chunks(m.shape[0]), CHUNK)
+    for row0, copy in zip(chunks(m.shape[0]), copies):
+        for first in range(0, len(tiles), 4):
+            build_counts(m, tiles[first : first + 4], CHUNK, first * LANES, row0)
+        copy.start()
+    half = rows // 2
+    own = pl.ds(pl.multiple_of(lax.axis_index("feat") * half, half), half)
+    part[...] = dot(ginc[:, own], m[own, :])
     width = w_in.shape[1]
     variables = w_in.shape[0]
     wi = w_in[...]
@@ -142,28 +155,17 @@
     w_ho_t[...] = dot(w_out[...], w_node2[...], 0, 1).astype(BF)
     w_io[...] = dot(wi, w_out[...]).astype(BF)
     w_io_t[...] = dot(w_out[...], wi, 0, 1).astype(BF)
-    e = edges[...]
-    h = e - rows
-    r = h & 15
-    at = jnp.where(mask[...] > 0, jnp.where(e < rows, e, rows + r * LANES + (h >> 4)), -1)
-    tiles = lane_tiles(at)
-    copies = row_copies(m, m_h, sems, chunks(m.shape[0]), CHUNK)
-    for row0, copy in zip(chunks(m.shape[0]), copies):
-        for first in range(0, len(tiles), 4):
-            build_counts(m, tiles[first : first + 4], CHUNK, first * LANES, row0)
-        copy.start()
     for copy in copies:
         copy.wait()
 
 
-def mix_kernel(feat_ref, msg, ginc, m_h, part, node, wide, m, sems):
-    feat = feat_ref[0]
-    rows = ginc.shape[1]
-    half = rows // 2
+def mix_kernel(msg, own_part, m_h, part, node, wide, m, sems):
+    feat = lax.axis_index("feat")
+    rows = own_part.shape[1]
     count = HALF_DEPTH * LANES
     halo = rows + feat * count
-    starts = [feat * half] + [halo + k for k in range(0, count, CHUNK)]
-    copies = row_copies(m_h, m, sems, starts, CHUNK, chunks(m.shape[0]))
+    starts = [halo + k for k in chunks(count)]
+    copies = row_copies(m_h, m, sems, starts, CHUNK, chunks(count))
     for copy in copies:
         copy.start()
     wide[...] = msg[...].astype(F32)
@@ -175,11 +177,10 @@
     n = node.shape[0]
     node[...] = ((lists[:n, :] - 1.0) * 32.0 + lists[n : 2 * n, :]).astype(I32)
     got = jnp.concatenate([wide[peer_rows(k), :].T for k in range(HALF_DEPTH)], axis=1).astype(BF)
-    copies[0].wait()
-    acc = dot(ginc[:, pl.ds(pl.multiple_of(feat * half, half), half)], m[:half, :])
-    for k, copy in zip(range(0, count, CHUNK), copies[1:]):
+    acc = own_part[...]
+    for k, copy in zip(chunks(count), copies):
         copy.wait()
-        acc = acc + dot(got[:, k : k + CHUNK], m[half + k : half + k + CHUNK, :])
+        acc = acc + dot(got[:, k : k + CHUNK], m[k : k + CHUNK, :])
     part[:, :rows] = acc.astype(BF)
 
 
@@ -190,11 +191,11 @@
 
 
 def node_kernel(
-    feat_ref, part, other, ginc, m_h, s, w_cat, w_cat_t, w_ho, w_ho_t, w_io, w_io_t, msg, own, slope_s, wide, m, sems
-):
-    feat = feat_ref[0]
+    part, other, ginc, m_h, s, w_cat, w_cat_t, w_ho, w_ho_t, w_io, w_io_t, msg, own, agg_out, slope_s, wide, m, sems
+):
+    feat = lax.axis_index("feat")
     variables, rows = ginc.shape
-    copies = row_copies(m_h, m, sems, chunks(m.shape[0]), CHUNK)
+    copies = row_copies(m_h, m, sems, [rows + k for k in chunks(m.shape[0])], CHUNK, chunks(m.shape[0]))
     for copy in copies:
         copy.start()
     gi = ginc[...]
@@ -217,37 +218,49 @@
     agg_cols = pl.ds(pl.multiple_of(variables + feat * n, n), n)
     both = dot(jnp.concatenate([w_cat[cols, :], w_cat[agg_cols, :]], axis=0), inner)
     agg_grad = both[n:, :].T.astype(BF)
+    agg_out[...] = agg_grad
+    own[...] = dot(w_io[cols, :], d) + both[:n, :]
     site_rows = values.T
     for k in range(SLOTS):
         wide[peer_rows(HALF_DEPTH + k), :] = site_rows[k * LANES : (k + 1) * LANES, :]
     for copy in copies:
         copy.wait()
-    own[...] = dot(w_io[cols, :], d) + both[:n, :] + dot(m[:rows, :], agg_grad).T
     count = HALF_DEPTH * LANES
-    low = dot(m[rows : rows + count, :], agg_grad)
-    high = dot(m[rows + count :, :], agg_grad)
+    low = dot(m[:count, :], agg_grad)
+    high = dot(m[count:, :], agg_grad)
     halo = jnp.concatenate([low, high], axis=1)
     for k in range(HALF_DEPTH):
         wide[peer_rows(k), :] = halo[k * LANES : (k + 1) * LANES, :]
     msg[...] = wide[...].astype(BF)
 
 
-def scatter_kernel(edges, target, g_h, target_col, g, sems):
+def scatter_kernel(
+    edges, target, send, own_in, agg_grad, m_h, g_h, near, target_col, send_out, own, g, m, sems, m_sem
+):
+    load = pltpu.make_async_copy(m_h.at[pl.ds(0, m.shape[0]), :], m, m_sem)
+    load.start()
+    send_out[...] = send[...]
+    target_col[...] = jnp.broadcast_to(target[...], (8, target.shape[1])).T[:, :1]
     e = edges[...]
     columns = jnp.concatenate([e, e], axis=0).T
     block = g.shape[0] // sems.shape[0]
     copies = row_copies(g, g_h, sems, range(0, g.shape[0], block), block)
     build_rows(g, columns, g.shape[0], e.shape[0], block, after=lambda n: copies[n].start())
-    target_col[...] = jnp.broadcast_to(target[...], (8, target.shape[1])).T[:, :1]
+    build_rows(near, columns - g.shape[1], near.shape[0], e.shape[0], block)
+    load.wait()
+    own[...] = own_in[...] + dot(m[...], agg_grad[...]).T
     for copy in copies:
         copy.wait()
 
 
-def finish_kernel(msg, send, own, target, g_h, out_h, pred, wide, r, g, out, in_sems, out_sems, *, degree):
-    width = g.shape[1] // in_sems.shape[0]
-    spans = [pl.ds(k * width, width) for k in range(in_sems.shape[0])]
+def finish_kernel(
+    msg, send, own, target, near, g_h, out_h, pred, wide, r, g, out, in_sems, out_sems, *, degree
+):
+    far = g.shape[1]
+    spans = [pl.ds(k, CHUNK) for k in chunks(far + near.shape[1])]
     loads = [
-        pltpu.make_async_copy(g_h.at[:, at], g.at[:, at], in_sems.at[k]) for k, at in enumerate(spans)
+        pltpu.make_async_copy(g_h.at[:, at], g.at[:, at], in_sems.at[k])
+        for k, at in enumerate(spans[: far // CHUNK])
     ]
     stores = [
         pltpu.make_async_copy(out.at[:, at], out_h.at[:, at], out_sems.at[k])
@@ -267,6 +280,8 @@
     slots = [wide[peer_rows(HALF_DEPTH + k), :] for k in range(SLOTS)]
     pick = jnp.where(target[...] == iota((target.shape[0], SLOTS * LANES), 1), 1.0, 0.0).astype(BF)
     pred[...] = dot(pick, jnp.concatenate(slots, axis=0).astype(BF)).astype(BF)
+    out[:, far:] = dot(grad, near[...])
+    stores[-1].start()
     for at, load, store in zip(spans, loads, stores):
         load.wait()
         out[:, at] = dot(grad, g[:, at])
@@ -275,7 +290,6 @@
         store.wait()
 
 
-SCALAR = pl.BlockSpec(memory_space=pltpu.SMEM)
 FULL = pl.BlockSpec(memory_space=pltpu.VMEM)
 HBM = pl.BlockSpec(memory_space=pl.ANY)
 STAY, LEAVE, COPY = "stay", "leave", "copy"
@@ -289,15 +303,13 @@
     return pltpu.SemaphoreType.DMA((n,))
 
 
-def call(kernel, outs, args, scratch=(), scalar=True, far=(), name=None):
+def call(kernel, outs, args, scratch=(), far=(), name=None):
     return pl.pallas_call(
         kernel,
         out_shape=[
             pltpu.VMEM(s, t) if where == STAY else jax.ShapeDtypeStruct(s, t) for s, t, where in outs
         ],
-        in_specs=[
-            SCALAR if scalar and k == 0 else HBM if k in far else FULL for k in range(len(args))
-        ],
+        in_specs=[HBM if k in far else FULL for k in range(len(args))],
         out_specs=[HBM if where == COPY else FULL for _, _, where in outs],
         scratch_shapes=list(scratch),
         name=name,
@@ -325,7 +337,6 @@
     site_obs,
 ):
     domains = lax.axis_size("dom")
-    feat = lax.axis_index("feat").astype(I32).reshape(1)
     grid_rows, variables = increments.shape
     mesh_rows = mesh_edges.shape[0]
     inner = w_node2.shape[0]
@@ -344,7 +355,7 @@
             ((variables, mesh_rows), BF, STAY),
             ((1, site_count), I32, LEAVE),
         ],
-        (feat, increments, grid_t, send_t, site_owner.T, site_nodes.T, site_obs),
+        (increments, grid_t, send_t, site_owner.T, site_nodes.T, site_obs),
         [
             pltpu.VMEM((grid_rows, mesh_rows), BF),
             pltpu.VMEM((mesh_rows, HALF_DEPTH * domains), BF),
@@ -352,13 +363,14 @@
             pltpu.VMEM((grid_rows, variables), BF),
             pltpu.SemaphoreType.DMA,
         ],
-        far=(1,),
+        far=(0,),
         name="encode",
     )
-    m, *weights = call(
+    m, own_part, *weights = call(
         prepare_kernel,
         [
             ((neighbours, mesh_rows), BF, COPY),
+            ((variables, mesh_rows), F32, STAY),
             ((2 * variables, inner), BF, LEAVE),
             ((inner, 2 * variables), BF, LEAVE),
             ((inner, variables), BF, LEAVE),
@@ -366,9 +378,8 @@
             ((variables, variables), BF, LEAVE),
             ((variables, variables), BF, LEAVE),
         ],
-        (mesh_edges.T, mesh_mask.T, w_in, w_node1, w_node2, w_out),
+        (mesh_edges.T, mesh_mask.T, vmem(ginc), w_in, w_node1, w_node2, w_out),
         [pltpu.VMEM((neighbours, mesh_rows), BF), dma(neighbours // CHUNK)],
-        scalar=False,
         name="prepare",
     )
     got = exchange(msg, domains)
@@ -378,13 +389,13 @@
             ((variables, mesh_rows + 2 * LANES), BF, STAY),
             ((SLOTS * site_nodes.shape[1], LANES), I32, STAY),
         ],
-        (feat, vmem(got), vmem(ginc), m),
+        (vmem(got), vmem(own_part), m),
         [
             wide,
-            pltpu.VMEM((neighbours // 2, mesh_rows), BF),
-            dma(neighbours // 2 // CHUNK),
-        ],
-        far=(3,),
+            pltpu.VMEM((HALF_DEPTH * domains, mesh_rows), BF),
+            dma(HALF_DEPTH * domains // CHUNK),
+        ],
+        far=(2,),
         name="mix",
     )
     other = lax.ppermute(part, "feat", SWAP)
@@ -392,32 +403,44 @@
         site_kernel,
         [((mesh_rows, SLOTS * domains), BF, STAY)],
         (vmem(node),),
-        scalar=False,
         name="sites",
     )
-    back, own = call(
+    back, own, agg_grad = call(
         node_kernel,
-        [((rows, variables), BF, LEAVE), ((n, mesh_rows), F32, STAY)],
-        (feat, vmem(part), vmem(other), vmem(ginc), m, vmem(sites), *weights),
+        [
+            ((rows, variables), BF, LEAVE),
+            ((n, mesh_rows), F32, LEAVE),
+            ((mesh_rows, n), BF, LEAVE),
+        ],
+        (vmem(part), vmem(other), vmem(ginc), m, vmem(sites), *weights),
         [
             pltpu.VMEM((inner, mesh_rows), F32),
             wide,
-            pltpu.VMEM((neighbours, mesh_rows), BF),
-            dma(neighbours // CHUNK),
-        ],
-        far=(4,),
+            pltpu.VMEM((neighbours - mesh_rows, mesh_rows), BF),
+            dma((neighbours - mesh_rows) // CHUNK),
+        ],
+        far=(3,),
         name="node",
     )
     got_back = exchange(back, domains)
-    g, target_col = call(
+    far = grid_rows - CHUNK
+    g, near, target_col, send_near, own = call(
         scatter_kernel,
         [
-            ((mesh_rows, grid_rows), BF, COPY),
+            ((mesh_rows, far), BF, COPY),
+            ((mesh_rows, CHUNK), BF, STAY),
             ((site_count, 1), I32, STAY),
-        ],
-        (grid_t, target),
-        [pltpu.VMEM((mesh_rows, grid_rows), BF), dma(8)],
-        scalar=False,
+            (send_t.shape, I32, STAY),
+            ((n, mesh_rows), F32, STAY),
+        ],
+        (grid_t, target, send_t, own, agg_grad, m),
+        [
+            pltpu.VMEM((mesh_rows, far), BF),
+            pltpu.VMEM((mesh_rows, mesh_rows), BF),
+            dma(8),
+            pltpu.SemaphoreType.DMA,
+        ],
+        far=(5,),
         name="scatter",
     )
 
@@ -427,17 +450,16 @@
     grad, site_pred = call(
         finish,
         [((n, grid_rows), F32, COPY), ((site_count, variables), BF, LEAVE)],
-        (vmem(got_back), send_t, vmem(own), vmem(target_col), g),
+        (vmem(got_back), vmem(send_near), vmem(own), vmem(target_col), vmem(near), g),
         [
             wide,
             pltpu.VMEM((mesh_rows, 2 * HALF_DEPTH * domains), BF),
-            pltpu.VMEM((mesh_rows, grid_rows), BF),
+            pltpu.VMEM((mesh_rows, far), BF),
             pltpu.VMEM((n, grid_rows), F32),
-            dma(8),
-            dma(8),
-        ],
-        scalar=False,
-        far=(4,),
+            dma(far // CHUNK),
+            dma(grid_rows // CHUNK),
+        ],
+        far=(5,),
         name="finish",
     )
     return (grad.T, site_pred)

time: 85.6 us -> 83.5 us (0.975)
  waiting for transfers between devices: 18.4 us -> 17.3 us
  Pallas kernels: 40.8 us -> 39.9 us
    all_to_all x2, waiting for transfers between devices: 18.1 us -> 17 us  [exchange(): x = lax.all_to_all(x, 'dom', split_axis=0, concat_axis=0, tiled=True)]
    pallas_call x7, Pallas kernels: 40.8 us -> 39.9 us  [call(): pl.pallas_call(kernel, out_shape=[pltpu.VMEM(s, t) if where == STAY else...]
  transfers between devices with their start and end apart: 3 -> 3, of which waited for: 3 -> 3; matrix products, arithmetic and copies ran while one was open for 0% -> 0% of each run, Pallas kernels for 19% -> 21%
where the time goes in v5:
time: 83.5 us; the launch traced here: 83.1 us
  Pallas kernels  39.9 us (48%)
  starting transfers between devices  25 us (30%)
  waiting for transfers between devices  17.3 us (21%)
  between operations  0.85 us (1%)
    pallas_call x7, Pallas kernels, call(): pl.pallas_call(kernel, out_shape=[pltpu.VMEM(s, t) if where == STAY else...  39.9 us
    all_to_all x2, starting transfers between devices, exchange(): x = lax.all_to_all(x, 'dom', split_axis=0, concat_axis=0, tiled=True)  22.7 us
    all_to_all x2, waiting for transfers between devices, exchange(): x = lax.all_to_all(x, 'dom', split_axis=0, concat_axis=0, tiled=True)  17 us
    ppermute x1, starting transfers between devices, local(): other = lax.ppermute(part, 'feat', SWAP)  2.33 us
  transfers between devices with their start and end apart: 3, of which 3 were waited for; matrix products, arithmetic and copies ran while one was open for 0% of the time, Pallas kernels for 21%

profile of v5, /device:TPU:1, one launch (start us, length us, event | category | flops | bytes accessed | tf_op | source)
XLA Modules:
  0.0 83.1 jit_solution(5123331513339543619)
XLA Ops:
  0.6 8.1 %encode.1 = (bf16[1536,128]{1,0:T(8,128)(2,1)}, bf16[128,1024]{1,0:T(8,128)(2,1)S(1)}, s32[1,256]{1,0:T(1,128)}) custom-call(bf16[4096,128]{1,0:T(8,128)(2,1)} %inc_h.1, s32[4,1024]{1,0:T(4,128)} %bitcast.17, s32[16,128]{1,0:T(8,128)} %bitcast.19, s32[1,256]{1,0:T(1,128)} %bitcast.24, s32[8,256]{1,0:T(8,128)} %bitcast.23, bf16[256,128]{1,0:T(8,128)(2,1)} %obs.1), custom_call_target="tpu_custom_call" | custom-call | tf_op jit(solution)/shard_map/encode/pallas_call | solution.py:307
  8.8 16.3 %all-to-all-start = ((bf16[128,3,4,128]{3,2,1,0:T(4,128)(2,1)}), bf16[128,3,4,128]{3,2,1,0:T(4,128)(2,1)S(1)}, u32[]{:S(2)}, u32[]{:S(2)}) async-start(bf16[128,3,4,128]{3,2,1,0:T(4,128)(2,1)} %bitcast.16), calls=%async_computation | async-start | bytes 786432 | tf_op jit(solution)/shard_map/all_to_all | solution.py:321
  25.1 7.9 %prepare.1 = (bf16[3072,1024]{1,0:T(8,128)(2,1)}, f32[128,1024]{1,0:T(8,128)S(1)}, bf16[256,512]{1,0:T(8,128)(2,1)}, bf16[512,256]{1,0:T(8,128)(2,1)}, bf16[512,...) custom-call(s32[6,1024]{1,0:T(8,128)} %bitcast.21, ...), custom_call_target="tpu_custom_call" | custom-call | tf_op jit(solution)/shard_map/prepare/pallas_call | solution.py:307
  33.0 8.7 %all-to-all-done = bf16[128,3,4,128]{3,2,1,0:T(4,128)(2,1)S(1)} async-done(((bf16[128,3,4,128]{3,2,1,0:T(4,128)(2,1)}), bf16[128,3,4,128]{3,2,1,0:T(4,128)(2,1)S(1)}, u32[]{:S(2)}, u32[]{:S(2)}) %all-to-all-start) | async-done | bytes 393248 | tf_op jit(solution)/shard_map/all_to_all | solution.py:321
  41.7 2.0 %mix.1 = (bf16[128,1280]{1,0:T(8,128)(2,1)S(1)}, s32[32,128]{1,0:T(8,128)S(1)}) custom-call(bf16[1536,128]{1,0:T(8,128)(2,1)S(1)} %bitcast.13, f32[128,1024]{1,0:T(8,128)S(1)} %get-tuple-element.27.own_part, bf16[3072,1024]{1,0:T(8,128)(2,1)} %get-tuple-element.28.m_h), custom_call_target="tpu_custom_call" | custom-call | tf_op jit(solution)/shard_map/mix/pallas_call | solution.py:307
  43.7 2.3 %collective-permute-start = (bf16[128,1280]{1,0:T(8,128)(2,1)S(1)}, bf16[128,1280]{1,0:T(8,128)(2,1)S(1)}, u32[]{:S(2)}, u32[]{:S(2)}) collective-permute-start(bf16[128,1280]{1,0:T(8,128)(2,1)S(1)} %get-tuple-element.29.part), channel_id=1, source_target_pairs={{0,1},{1,0},{2,3},{3,2},{4,5},{5,4},{6,7},{7,6},{8,9},{9,8},{10,11... | collective-permute-start | bytes 983048 | tf_op jit(solution)/shard_map/ppermute | solution.py:401
  46.0 1.0 %sites.1.s = bf16[1024,512]{1,0:T(8,128)(2,1)S(1)} custom-call(s32[32,128]{1,0:T(8,128)S(1)} %get-tuple-element.30.node), custom_call_target="tpu_custom_call" | custom-call | tf_op jit(solution)/shard_map/sites/pallas_call | solution.py:307
  47.0 0.3 collective-permute-done.other
  47.3 6.6 %node.1 = (bf16[1536,128]{1,0:T(8,128)(2,1)}, f32[64,1024]{1,0:T(8,128)}, bf16[1024,64]{1,0:T(8,128)(2,1)}) custom-call(bf16[128,1280]{1,0:T(8,128)(2,1)S(1)} %get-tuple-element.29.part, bf16[128,1280]{1,0:T(8,128)(2,1)S(1)} %collective-permute-done.other, bf16[128,1024]{1,0:T(8,128)(2,1)S(1)} %get-tuple-element.26.ginc, ...), custom_call_target="tpu_custom_call" | custom-call | tf_op jit(solution)/shard_map/node/pallas_call | solution.py:307
  53.9 6.4 %all-to-all-start.1 = ((bf16[128,3,4,128]{3,2,1,0:T(4,128)(2,1)}), bf16[128,3,4,128]{3,2,1,0:T(4,128)(2,1)S(1)}, u32[]{:S(2)}, u32[]{:S(2)}) async-start(bf16[128,3,4,128]{3,2,1,0:T(4,128)(2,1)} %bitcast.15), calls=%async_computation.1 | async-start | bytes 786432 | tf_op jit(solution)/shard_map/all_to_all | solution.py:321
  60.3 8.4 %scatter.1 = (bf16[1024,3584]{1,0:T(8,128)(2,1)}, bf16[1024,512]{1,0:T(8,128)(2,1)S(1)}, s32[256,1]{1,0:T(8,128)S(1)}, s32[16,128]{1,0:T(8,128)S(1)}, f32[64,1024]{1,0:T(8,128)S(1)}) custom-call(s32[4,1024]{1,0:T(4,128)} %bitcast.18, s32[1,256]{1,0:T(1,128)} %get-tuple-element.38.target, s32[16,128]{1,0:T(8,128)} %bitcast.20, ...), custom_call_target="tpu_custom_call" | custom-call | tf_op jit(solution)/shard_map/scatter/pallas_call | solution.py:307
  68.7 8.4 %all-to-all-done.1 = bf16[128,3,4,128]{3,2,1,0:T(4,128)(2,1)S(1)} async-done(((bf16[128,3,4,128]{3,2,1,0:T(4,128)(2,1)}), bf16[128,3,4,128]{3,2,1,0:T(4,128)(2,1)S(1)}, u32[]{:S(2)}, u32[]{:S(2)}) %all-to-all-start.1) | async-done | bytes 393248 | tf_op jit(solution)/shard_map/all_to_all | solution.py:321
  77.0 5.9 %finish.1 = (f32[64,4096]{1,0:T(8,128)}, bf16[256,128]{1,0:T(8,128)(2,1)}) custom-call(bf16[1536,128]{1,0:T(8,128)(2,1)S(1)} %bitcast.14, s32[16,128]{1,0:T(8,128)S(1)} %get-tuple-element.41.refs_1_, f32[64,1024]{1,0:T(8,128)S(1)} %get-tuple-element.42.refs_2_, s32[256,1]{1,0:T(8,128)S(1)} %get-tuple-element.43.refs_3_, ...), custom_call_target="tpu_custom_call" | custom-call | tf_op jit(solution)/shard_map/finish/pallas_call | solution.py:307
Async XLA Ops:
  8.8 32.9 %all-to-all-start = ((bf16[128,3,4,128]{3,2,1,0:T(4,128)(2,1)}), bf16[128,3,4,128]{3,2,1,0:T(4,128)(2,1)S(1)}, u32[]{:S(2)}, u32[]{:S(2)}) async-start(bf16[128,3,4,128]{3,2,1,0:T(4,128)(2,1)} %bitcast.16), calls=%async_computation | async-start | bytes 786432 | tf_op jit(solution)/shard_map/all_to_all | solution.py:321
  43.7 3.6 %collective-permute-start = (bf16[128,1280]{1,0:T(8,128)(2,1)S(1)}, bf16[128,1280]{1,0:T(8,128)(2,1)S(1)}, u32[]{:S(2)}, u32[]{:S(2)}) collective-permute-start(bf16[128,1280]{1,0:T(8,128)(2,1)S(1)} %get-tuple-element.29.part), channel_id=1, source_target_pairs={{0,1},{1,0},{2,3},{3,2},{4,5},{5,4},{6,7},{7,6},{8,9},{9,8},{10,11... | collective-permute-start | bytes 983048 | tf_op jit(solution)/shard_map/ppermute | solution.py:401
  53.9 23.1 %all-to-all-start.1 = ((bf16[128,3,4,128]{3,2,1,0:T(4,128)(2,1)}), bf16[128,3,4,128]{3,2,1,0:T(4,128)(2,1)S(1)}, u32[]{:S(2)}, u32[]{:S(2)}) async-start(bf16[128,3,4,128]{3,2,1,0:T(4,128)(2,1)} %bitcast.15), calls=%async_computation.1 | async-start | bytes 786432 | tf_op jit(solution)/shard_map/all_to_all | solution.py:321

commit v6 on v5

--- a/solution.py
+++ b/solution.py
@@ -14,6 +14,7 @@
 SLOTS = 4
 ROWS = HALF_DEPTH + SLOTS
 SWAP = [(0, 1), (1, 0)]
+PIECES = 2
 CHUNK = 512
 
 
@@ -191,10 +192,37 @@
 
 
 def node_kernel(
-    part, other, ginc, m_h, s, w_cat, w_cat_t, w_ho, w_ho_t, w_io, w_io_t, msg, own, agg_out, slope_s, wide, m, sems
+    part,
+    other,
+    ginc,
+    m_h,
+    s,
+    w_cat_h,
+    w_cat_t,
+    w_ho_h,
+    w_ho_t,
+    w_io_h,
+    w_io_t,
+    msg,
+    own,
+    agg_out,
+    slope_s,
+    wide,
+    m,
+    sems,
+    w_cat,
+    w_ho,
+    w_io,
+    w_sems,
 ):
     feat = lax.axis_index("feat")
     variables, rows = ginc.shape
+    late = [
+        pltpu.make_async_copy(a, b, w_sems.at[k])
+        for k, (a, b) in enumerate(((w_ho_h, w_ho), (w_cat_h, w_cat), (w_io_h, w_io)))
+    ]
+    for copy in late:
+        copy.start()
     copies = row_copies(m_h, m, sems, [rows + k for k in chunks(m.shape[0])], CHUNK, chunks(m.shape[0]))
     for copy in copies:
         copy.start()
@@ -212,6 +240,8 @@
     second = jnp.where(feat == 0, theirs, mine)
     diff = (values - jnp.concatenate([first, second], axis=1)).astype(BF)
     d = dot(diff, s[...], 1, 1).astype(BF)
+    for copy in late:
+        copy.wait()
     inner = (dot(w_ho[...], d) * slope_s[...]).astype(BF)
     n = variables // 2
     cols = pl.ds(pl.multiple_of(feat * n, n), n)
@@ -257,10 +287,12 @@
     msg, send, own, target, near, g_h, out_h, pred, wide, r, g, out, in_sems, out_sems, *, degree
 ):
     far = g.shape[1]
-    spans = [pl.ds(k, CHUNK) for k in chunks(far + near.shape[1])]
+    piece = far // PIECES
+    spans = [(k, piece) for k in range(0, far, piece)] + [(far, near.shape[1])]
+    spans = [pl.ds(*span) for span in spans]
     loads = [
         pltpu.make_async_copy(g_h.at[:, at], g.at[:, at], in_sems.at[k])
-        for k, at in enumerate(spans[: far // CHUNK])
+        for k, at in enumerate(spans[:-1])
     ]
     stores = [
         pltpu.make_async_copy(out.at[:, at], out_h.at[:, at], out_sems.at[k])
@@ -372,11 +404,11 @@
             ((neighbours, mesh_rows), BF, COPY),
             ((variables, mesh_rows), F32, STAY),
             ((2 * variables, inner), BF, LEAVE),
-            ((inner, 2 * variables), BF, LEAVE),
+            ((inner, 2 * variables), BF, STAY),
             ((inner, variables), BF, LEAVE),
-            ((variables, inner), BF, LEAVE),
+            ((variables, inner), BF, STAY),
             ((variables, variables), BF, LEAVE),
-            ((variables, variables), BF, LEAVE),
+            ((variables, variables), BF, STAY),
         ],
         (mesh_edges.T, mesh_mask.T, vmem(ginc), w_in, w_node1, w_node2, w_out),
         [pltpu.VMEM((neighbours, mesh_rows), BF), dma(neighbours // CHUNK)],
@@ -412,23 +444,33 @@
             ((n, mesh_rows), F32, LEAVE),
             ((mesh_rows, n), BF, LEAVE),
         ],
-        (vmem(part), vmem(other), vmem(ginc), m, vmem(sites), *weights),
+        (
+            vmem(part),
+            vmem(other),
+            vmem(ginc),
+            m,
+            vmem(sites),
+            *[vmem(w) if k % 2 else w for k, w in enumerate(weights)],
+        ),
         [
             pltpu.VMEM((inner, mesh_rows), F32),
             wide,
             pltpu.VMEM((neighbours - mesh_rows, mesh_rows), BF),
             dma((neighbours - mesh_rows) // CHUNK),
-        ],
-        far=(3,),
+            *[pltpu.VMEM(w.shape, BF) for w in (weights[0], weights[2], weights[4])],
+            dma(3),
+        ],
+        far=(3, 5, 7, 9),
         name="node",
     )
     got_back = exchange(back, domains)
-    far = grid_rows - CHUNK
+    near_cells = 3 * CHUNK // 2
+    far = grid_rows - near_cells
     g, near, target_col, send_near, own = call(
         scatter_kernel,
         [
             ((mesh_rows, far), BF, COPY),
-            ((mesh_rows, CHUNK), BF, STAY),
+            ((mesh_rows, near_cells), BF, STAY),
             ((site_count, 1), I32, STAY),
             (send_t.shape, I32, STAY),
             ((n, mesh_rows), F32, STAY),
@@ -456,8 +498,8 @@
             pltpu.VMEM((mesh_rows, 2 * HALF_DEPTH * domains), BF),
             pltpu.VMEM((mesh_rows, far), BF),
             pltpu.VMEM((n, grid_rows), F32),
-            dma(far // CHUNK),
-            dma(grid_rows // CHUNK),
+            dma(PIECES),
+            dma(PIECES + 1),
         ],
         far=(5,),
         name="finish",

time: 83.5 us -> 82.2 us (0.984)
  Pallas kernels: 39.9 us -> 38.2 us
    pallas_call x7, Pallas kernels: 39.9 us -> 38.2 us  [call(): pl.pallas_call(kernel, out_shape=[pltpu.VMEM(s, t) if where == STAY else...]
where the time goes in v6:
time: 82.2 us; the launch traced here: 81.8 us
  Pallas kernels  38.2 us (46%)
  starting transfers between devices  25 us (30%)
  waiting for transfers between devices  17.7 us (22%)
  between operations  0.85 us (1%)
    pallas_call x7, Pallas kernels, call(): pl.pallas_call(kernel, out_shape=[pltpu.VMEM(s, t) if where == STAY else...  38.2 us
    all_to_all x2, starting transfers between devices, exchange(): x = lax.all_to_all(x, 'dom', split_axis=0, concat_axis=0, tiled=True)  22.7 us
    all_to_all x2, waiting for transfers between devices, exchange(): x = lax.all_to_all(x, 'dom', split_axis=0, concat_axis=0, tiled=True)  17.4 us
    ppermute x1, starting transfers between devices, local(): other = lax.ppermute(part, 'feat', SWAP)  2.33 us
  transfers between devices with their start and end apart: 3, of which 3 were waited for; matrix products, arithmetic and copies ran while one was open for 0% of the time, Pallas kernels for 21%

profile of v6, /device:TPU:1, one launch (start us, length us, event | category | flops | bytes accessed | tf_op | source)
XLA Modules:
  0.0 81.8 jit_solution(18384329259363170812)
XLA Ops:
  0.6 8.1 %encode.1 = (bf16[1536,128]{1,0:T(8,128)(2,1)}, bf16[128,1024]{1,0:T(8,128)(2,1)S(1)}, s32[1,256]{1,0:T(1,128)}) custom-call(bf16[4096,128]{1,0:T(8,128)(2,1)} %inc_h.1, s32[4,1024]{1,0:T(4,128)} %bitcast.17, s32[16,128]{1,0:T(8,128)} %bitcast.19, s32[1,256]{1,0:T(1,128)} %bitcast.24, s32[8,256]{1,0:T(8,128)} %bitcast.23, bf16[256,128]{1,0:T(8,128)(2,1)} %obs.1), custom_call_target="tpu_custom_call" | custom-call | tf_op jit(solution)/shard_map/encode/pallas_call | solution.py:339
  8.8 16.3 %all-to-all-start = ((bf16[128,3,4,128]{3,2,1,0:T(4,128)(2,1)}), bf16[128,3,4,128]{3,2,1,0:T(4,128)(2,1)S(1)}, u32[]{:S(2)}, u32[]{:S(2)}) async-start(bf16[128,3,4,128]{3,2,1,0:T(4,128)(2,1)} %bitcast.16), calls=%async_computation | async-start | bytes 786432 | tf_op jit(solution)/shard_map/all_to_all | solution.py:353
  25.1 7.6 %prepare.1 = (bf16[3072,1024]{1,0:T(8,128)(2,1)}, f32[128,1024]{1,0:T(8,128)S(1)}, bf16[256,512]{1,0:T(8,128)(2,1)}, bf16[512,256]{1,0:T(8,128)(2,1)S(1)}, bf16[...) custom-call(s32[6,1024]{1,0:T(8,128)} %bitcast.21, ...), custom_call_target="tpu_custom_call" | custom-call | tf_op jit(solution)/shard_map/prepare/pallas_call | solution.py:339
  32.7 9.0 %all-to-all-done = bf16[128,3,4,128]{3,2,1,0:T(4,128)(2,1)S(1)} async-done(((bf16[128,3,4,128]{3,2,1,0:T(4,128)(2,1)}), bf16[128,3,4,128]{3,2,1,0:T(4,128)(2,1)S(1)}, u32[]{:S(2)}, u32[]{:S(2)}) %all-to-all-start) | async-done | bytes 393248 | tf_op jit(solution)/shard_map/all_to_all | solution.py:353
  41.7 2.0 %mix.1 = (bf16[128,1280]{1,0:T(8,128)(2,1)S(1)}, s32[32,128]{1,0:T(8,128)S(1)}) custom-call(bf16[1536,128]{1,0:T(8,128)(2,1)S(1)} %bitcast.13, f32[128,1024]{1,0:T(8,128)S(1)} %get-tuple-element.27.own_part, bf16[3072,1024]{1,0:T(8,128)(2,1)} %get-tuple-element.28.m_h), custom_call_target="tpu_custom_call" | custom-call | tf_op jit(solution)/shard_map/mix/pallas_call | solution.py:339
  43.7 2.3 %collective-permute-start = (bf16[128,1280]{1,0:T(8,128)(2,1)S(1)}, bf16[128,1280]{1,0:T(8,128)(2,1)S(1)}, u32[]{:S(2)}, u32[]{:S(2)}) collective-permute-start(bf16[128,1280]{1,0:T(8,128)(2,1)S(1)} %get-tuple-element.29.part), channel_id=1, source_target_pairs={{0,1},{1,0},{2,3},{3,2},{4,5},{5,4},{6,7},{7,6},{8,9},{9,8},{10,11... | collective-permute-start | bytes 983048 | tf_op jit(solution)/shard_map/ppermute | solution.py:433
  46.0 1.0 %sites.1.s = bf16[1024,512]{1,0:T(8,128)(2,1)S(1)} custom-call(s32[32,128]{1,0:T(8,128)S(1)} %get-tuple-element.30.node), custom_call_target="tpu_custom_call" | custom-call | tf_op jit(solution)/shard_map/sites/pallas_call | solution.py:339
  47.0 0.3 collective-permute-done.other
  47.3 5.8 %node.1 = (bf16[1536,128]{1,0:T(8,128)(2,1)}, f32[64,1024]{1,0:T(8,128)}, bf16[1024,64]{1,0:T(8,128)(2,1)}) custom-call(bf16[128,1280]{1,0:T(8,128)(2,1)S(1)} %get-tuple-element.29.part, bf16[128,1280]{1,0:T(8,128)(2,1)S(1)} %collective-permute-done.other, bf16[128,1024]{1,0:T(8,128)(2,1)S(1)} %get-tuple-element.26.ginc, ...), custom_call_target="tpu_custom_call" | custom-call | tf_op jit(solution)/shard_map/node/pallas_call | solution.py:339
  53.1 6.4 %all-to-all-start.1 = ((bf16[128,3,4,128]{3,2,1,0:T(4,128)(2,1)}), bf16[128,3,4,128]{3,2,1,0:T(4,128)(2,1)S(1)}, u32[]{:S(2)}, u32[]{:S(2)}) async-start(bf16[128,3,4,128]{3,2,1,0:T(4,128)(2,1)} %bitcast.15), calls=%async_computation.1 | async-start | bytes 786432 | tf_op jit(solution)/shard_map/all_to_all | solution.py:353
  59.4 8.3 %scatter.1 = (bf16[1024,3328]{1,0:T(8,128)(2,1)}, bf16[1024,768]{1,0:T(8,128)(2,1)S(1)}, s32[256,1]{1,0:T(8,128)S(1)}, s32[16,128]{1,0:T(8,128)S(1)}, f32[64,1024]{1,0:T(8,128)S(1)}) custom-call(s32[4,1024]{1,0:T(4,128)} %bitcast.18, s32[1,256]{1,0:T(1,128)} %get-tuple-element.38.target, s32[16,128]{1,0:T(8,128)} %bitcast.20, ...), custom_call_target="tpu_custom_call" | custom-call | tf_op jit(solution)/shard_map/scatter/pallas_call | solution.py:339
  67.8 8.4 %all-to-all-done.1 = bf16[128,3,4,128]{3,2,1,0:T(4,128)(2,1)S(1)} async-done(((bf16[128,3,4,128]{3,2,1,0:T(4,128)(2,1)}), bf16[128,3,4,128]{3,2,1,0:T(4,128)(2,1)S(1)}, u32[]{:S(2)}, u32[]{:S(2)}) %all-to-all-start.1) | async-done | bytes 393248 | tf_op jit(solution)/shard_map/all_to_all | solution.py:353
  76.2 5.5 %finish.1 = (f32[64,4096]{1,0:T(8,128)}, bf16[256,128]{1,0:T(8,128)(2,1)}) custom-call(bf16[1536,128]{1,0:T(8,128)(2,1)S(1)} %bitcast.14, s32[16,128]{1,0:T(8,128)S(1)} %get-tuple-element.41.refs_1_, f32[64,1024]{1,0:T(8,128)S(1)} %get-tuple-element.42.refs_2_, s32[256,1]{1,0:T(8,128)S(1)} %get-tuple-element.43.refs_3_, ...), custom_call_target="tpu_custom_call" | custom-call | tf_op jit(solution)/shard_map/finish/pallas_call | solution.py:339
Async XLA Ops:
  8.8 32.9 %all-to-all-start = ((bf16[128,3,4,128]{3,2,1,0:T(4,128)(2,1)}), bf16[128,3,4,128]{3,2,1,0:T(4,128)(2,1)S(1)}, u32[]{:S(2)}, u32[]{:S(2)}) async-start(bf16[128,3,4,128]{3,2,1,0:T(4,128)(2,1)} %bitcast.16), calls=%async_computation | async-start | bytes 786432 | tf_op jit(solution)/shard_map/all_to_all | solution.py:353
  43.7 3.6 %collective-permute-start = (bf16[128,1280]{1,0:T(8,128)(2,1)S(1)}, bf16[128,1280]{1,0:T(8,128)(2,1)S(1)}, u32[]{:S(2)}, u32[]{:S(2)}) collective-permute-start(bf16[128,1280]{1,0:T(8,128)(2,1)S(1)} %get-tuple-element.29.part), channel_id=1, source_target_pairs={{0,1},{1,0},{2,3},{3,2},{4,5},{5,4},{6,7},{7,6},{8,9},{9,8},{10,11... | collective-permute-start | bytes 983048 | tf_op jit(solution)/shard_map/ppermute | solution.py:433
  53.1 23.1 %all-to-all-start.1 = ((bf16[128,3,4,128]{3,2,1,0:T(4,128)(2,1)}), bf16[128,3,4,128]{3,2,1,0:T(4,128)(2,1)S(1)}, u32[]{:S(2)}, u32[]{:S(2)}) async-start(bf16[128,3,4,128]{3,2,1,0:T(4,128)(2,1)} %bitcast.15), calls=%async_computation.1 | async-start | bytes 786432 | tf_op jit(solution)/shard_map/all_to_all | solution.py:353

commit v7 on v6

--- a/solution.py
+++ b/solution.py
@@ -91,12 +91,19 @@
 
 
 def encode_kernel(
-    inc_h, edges, send, owner, nodes, obs, msg, ginc, target, g, r, wide, inc, sem
+    inc_h, edges, *refs
 ):
+    small_h, (msg, ginc, target, g, r, wide, inc, sem), (*small, sems) = refs[:4], refs[4:12], refs[12:]
+    send, owner, nodes, obs = small
     feat = lax.axis_index("feat")
     load = pltpu.make_async_copy(inc_h, inc, sem)
+    late = [pltpu.make_async_copy(a, b, sems.at[k]) for k, (a, b) in enumerate(zip(small_h, small))]
+    for copy in late:
+        copy.start()
     load.start()
-    build_counts(g, lane_tiles(edges[...]), inc.shape[0])
+    build_counts(g, lane_tiles(edges[...]), inc.shape[0], unroll=8)
+    for copy in late:
+        copy.wait()
     picked = jnp.where(feat == 0, send[:HALF_DEPTH, :], send[HALF_DEPTH:, :])
     build_counts(r, [[picked[k : k + 1, :]] for k in range(HALF_DEPTH)], r.shape[0])
     sites = owner.shape[1]
@@ -380,6 +387,7 @@
     wide = pltpu.VMEM((rows, variables), F32)
     grid_t = grid_edges.T
     send_t = send_rows[0].T
+    small = (send_t, site_owner.T, site_nodes.T, site_obs)
     msg, ginc, target = call(
         encode_kernel,
         [
@@ -387,15 +395,17 @@
             ((variables, mesh_rows), BF, STAY),
             ((1, site_count), I32, LEAVE),
         ],
-        (increments, grid_t, send_t, site_owner.T, site_nodes.T, site_obs),
+        (increments, grid_t, *small),
         [
             pltpu.VMEM((grid_rows, mesh_rows), BF),
             pltpu.VMEM((mesh_rows, HALF_DEPTH * domains), BF),
             wide,
             pltpu.VMEM((grid_rows, variables), BF),
             pltpu.SemaphoreType.DMA,
-        ],
-        far=(0,),
+            *[pltpu.VMEM(v.shape, v.dtype) for v in small],
+            dma(len(small)),
+        ],
+        far=(0, 2, 3, 4, 5),
         name="encode",
     )
     m, own_part, *weights = call(

time: 82.2 us -> 81.9 us (level)
  no operation moved by 1% of the time
where the time goes in v7:
time: 81.9 us; the launch traced here: 81.5 us
  Pallas kernels  37.9 us (46%)
  starting transfers between devices  25 us (31%)
  waiting for transfers between devices  17.7 us (22%)
  between operations  0.85 us (1%)
    pallas_call x7, Pallas kernels, call(): pl.pallas_call(kernel, out_shape=[pltpu.VMEM(s, t) if where == STAY else...  37.9 us
    all_to_all x2, starting transfers between devices, exchange(): x = lax.all_to_all(x, 'dom', split_axis=0, concat_axis=0, tiled=True)  22.7 us
    all_to_all x2, waiting for transfers between devices, exchange(): x = lax.all_to_all(x, 'dom', split_axis=0, concat_axis=0, tiled=True)  17.4 us
    ppermute x1, starting transfers between devices, local(): other = lax.ppermute(part, 'feat', SWAP)  2.31 us
  transfers between devices with their start and end apart: 3, of which 3 were waited for; matrix products, arithmetic and copies ran while one was open for 0% of the time, Pallas kernels for 21%

profile of v7, /device:TPU:1, one launch (start us, length us, event | category | flops | bytes accessed | tf_op | source)
XLA Modules:
  0.0 81.5 jit_solution(4583916340080171490)
XLA Ops:
  0.6 7.8 %encode.1 = (bf16[1536,128]{1,0:T(8,128)(2,1)}, bf16[128,1024]{1,0:T(8,128)(2,1)S(1)}, s32[1,256]{1,0:T(1,128)}) custom-call(bf16[4096,128]{1,0:T(8,128)(2,1)} %inc_h.1, s32[4,1024]{1,0:T(4,128)} %bitcast.17, s32[16,128]{1,0:T(8,128)} %bitcast.19, s32[1,256]{1,0:T(1,128)} %bitcast.24, s32[8,256]{1,0:T(8,128)} %bitcast.23, bf16[256,128]{1,0:T(8,128)(2,1)} %refs_3_.1), custom_call_target="tpu_custom_call" | custom-call | tf_op jit(solution)/shard_map/encode/pallas_call | solution.py:346
  8.5 16.3 %all-to-all-start = ((bf16[128,3,4,128]{3,2,1,0:T(4,128)(2,1)}), bf16[128,3,4,128]{3,2,1,0:T(4,128)(2,1)S(1)}, u32[]{:S(2)}, u32[]{:S(2)}) async-start(bf16[128,3,4,128]{3,2,1,0:T(4,128)(2,1)} %bitcast.16), calls=%async_computation | async-start | bytes 786432 | tf_op jit(solution)/shard_map/all_to_all | solution.py:360
  24.8 7.6 %prepare.1 = (bf16[3072,1024]{1,0:T(8,128)(2,1)}, f32[128,1024]{1,0:T(8,128)S(1)}, bf16[256,512]{1,0:T(8,128)(2,1)}, bf16[512,256]{1,0:T(8,128)(2,1)S(1)}, bf16[...) custom-call(s32[6,1024]{1,0:T(8,128)} %bitcast.21, ...), custom_call_target="tpu_custom_call" | custom-call | tf_op jit(solution)/shard_map/prepare/pallas_call | solution.py:346
  32.4 9.0 %all-to-all-done = bf16[128,3,4,128]{3,2,1,0:T(4,128)(2,1)S(1)} async-done(((bf16[128,3,4,128]{3,2,1,0:T(4,128)(2,1)}), bf16[128,3,4,128]{3,2,1,0:T(4,128)(2,1)S(1)}, u32[]{:S(2)}, u32[]{:S(2)}) %all-to-all-start) | async-done | bytes 393248 | tf_op jit(solution)/shard_map/all_to_all | solution.py:360
  41.4 2.0 %mix.1 = (bf16[128,1280]{1,0:T(8,128)(2,1)S(1)}, s32[32,128]{1,0:T(8,128)S(1)}) custom-call(bf16[1536,128]{1,0:T(8,128)(2,1)S(1)} %bitcast.13, f32[128,1024]{1,0:T(8,128)S(1)} %get-tuple-element.27.own_part, bf16[3072,1024]{1,0:T(8,128)(2,1)} %get-tuple-element.28.m_h), custom_call_target="tpu_custom_call" | custom-call | tf_op jit(solution)/shard_map/mix/pallas_call | solution.py:346
  43.4 2.3 %collective-permute-start = (bf16[128,1280]{1,0:T(8,128)(2,1)S(1)}, bf16[128,1280]{1,0:T(8,128)(2,1)S(1)}, u32[]{:S(2)}, u32[]{:S(2)}) collective-permute-start(bf16[128,1280]{1,0:T(8,128)(2,1)S(1)} %get-tuple-element.29.part), channel_id=1, source_target_pairs={{0,1},{1,0},{2,3},{3,2},{4,5},{5,4},{6,7},{7,6},{8,9},{9,8},{10,11... | collective-permute-start | bytes 983048 | tf_op jit(solution)/shard_map/ppermute | solution.py:443
  45.7 1.0 %sites.1.s = bf16[1024,512]{1,0:T(8,128)(2,1)S(1)} custom-call(s32[32,128]{1,0:T(8,128)S(1)} %get-tuple-element.30.node), custom_call_target="tpu_custom_call" | custom-call | tf_op jit(solution)/shard_map/sites/pallas_call | solution.py:346
  46.7 0.3 collective-permute-done.other
  47.0 5.8 %node.1 = (bf16[1536,128]{1,0:T(8,128)(2,1)}, f32[64,1024]{1,0:T(8,128)}, bf16[1024,64]{1,0:T(8,128)(2,1)}) custom-call(bf16[128,1280]{1,0:T(8,128)(2,1)S(1)} %get-tuple-element.29.part, bf16[128,1280]{1,0:T(8,128)(2,1)S(1)} %collective-permute-done.other, bf16[128,1024]{1,0:T(8,128)(2,1)S(1)} %get-tuple-element.26.ginc, ...), custom_call_target="tpu_custom_call" | custom-call | tf_op jit(solution)/shard_map/node/pallas_call | solution.py:346
  52.8 6.4 %all-to-all-start.1 = ((bf16[128,3,4,128]{3,2,1,0:T(4,128)(2,1)}), bf16[128,3,4,128]{3,2,1,0:T(4,128)(2,1)S(1)}, u32[]{:S(2)}, u32[]{:S(2)}) async-start(bf16[128,3,4,128]{3,2,1,0:T(4,128)(2,1)} %bitcast.15), calls=%async_computation.1 | async-start | bytes 786432 | tf_op jit(solution)/shard_map/all_to_all | solution.py:360
  59.1 8.3 %scatter.1 = (bf16[1024,3328]{1,0:T(8,128)(2,1)}, bf16[1024,768]{1,0:T(8,128)(2,1)S(1)}, s32[256,1]{1,0:T(8,128)S(1)}, s32[16,128]{1,0:T(8,128)S(1)}, f32[64,1024]{1,0:T(8,128)S(1)}) custom-call(s32[4,1024]{1,0:T(4,128)} %bitcast.18, s32[1,256]{1,0:T(1,128)} %get-tuple-element.38.target, s32[16,128]{1,0:T(8,128)} %bitcast.20, ...), custom_call_target="tpu_custom_call" | custom-call | tf_op jit(solution)/shard_map/scatter/pallas_call | solution.py:346
  67.5 8.4 %all-to-all-done.1 = bf16[128,3,4,128]{3,2,1,0:T(4,128)(2,1)S(1)} async-done(((bf16[128,3,4,128]{3,2,1,0:T(4,128)(2,1)}), bf16[128,3,4,128]{3,2,1,0:T(4,128)(2,1)S(1)}, u32[]{:S(2)}, u32[]{:S(2)}) %all-to-all-start.1) | async-done | bytes 393248 | tf_op jit(solution)/shard_map/all_to_all | solution.py:360
  75.9 5.5 %finish.1 = (f32[64,4096]{1,0:T(8,128)}, bf16[256,128]{1,0:T(8,128)(2,1)}) custom-call(bf16[1536,128]{1,0:T(8,128)(2,1)S(1)} %bitcast.14, s32[16,128]{1,0:T(8,128)S(1)} %get-tuple-element.41.refs_1_, f32[64,1024]{1,0:T(8,128)S(1)} %get-tuple-element.42.refs_2_, s32[256,1]{1,0:T(8,128)S(1)} %get-tuple-element.43.refs_3_, ...), custom_call_target="tpu_custom_call" | custom-call | tf_op jit(solution)/shard_map/finish/pallas_call | solution.py:346
Async XLA Ops:
  8.5 33.0 %all-to-all-start = ((bf16[128,3,4,128]{3,2,1,0:T(4,128)(2,1)}), bf16[128,3,4,128]{3,2,1,0:T(4,128)(2,1)S(1)}, u32[]{:S(2)}, u32[]{:S(2)}) async-start(bf16[128,3,4,128]{3,2,1,0:T(4,128)(2,1)} %bitcast.16), calls=%async_computation | async-start | bytes 786432 | tf_op jit(solution)/shard_map/all_to_all | solution.py:360
  43.4 3.6 %collective-permute-start = (bf16[128,1280]{1,0:T(8,128)(2,1)S(1)}, bf16[128,1280]{1,0:T(8,128)(2,1)S(1)}, u32[]{:S(2)}, u32[]{:S(2)}) collective-permute-start(bf16[128,1280]{1,0:T(8,128)(2,1)S(1)} %get-tuple-element.29.part), channel_id=1, source_target_pairs={{0,1},{1,0},{2,3},{3,2},{4,5},{5,4},{6,7},{7,6},{8,9},{9,8},{10,11... | collective-permute-start | bytes 983048 | tf_op jit(solution)/shard_map/ppermute | solution.py:443
  52.8 23.1 %all-to-all-start.1 = ((bf16[128,3,4,128]{3,2,1,0:T(4,128)(2,1)}), bf16[128,3,4,128]{3,2,1,0:T(4,128)(2,1)S(1)}, u32[]{:S(2)}, u32[]{:S(2)}) async-start(bf16[128,3,4,128]{3,2,1,0:T(4,128)(2,1)} %bitcast.15), calls=%async_computation.1 | async-start | bytes 786432 | tf_op jit(solution)/shard_map/all_to_all | solution.py:360

commit v8 on v7

--- a/solution.py
+++ b/solution.py
@@ -308,7 +308,7 @@
     for load in loads:
         load.start()
     depth = send.shape[0]
-    build_counts(r, [[send[k : k + 1, :]] for k in range(depth)], r.shape[0], unroll=2)
+    build_counts(r, [[send[k : k + 1, :]] for k in range(depth)], r.shape[0], unroll=8)
     wide[...] = msg[...].astype(F32)
     back = jnp.concatenate([wide[peer_rows(k), :] for k in range(HALF_DEPTH)], axis=0).astype(BF)
     count = back.shape[0]

time: 81.9 us -> 81.9 us (level)
  no operation moved by 1% of the time
where the time goes in v8:
time: 81.9 us; the launch traced here: 81.5 us
  Pallas kernels  37.9 us (46%)
  starting transfers between devices  25 us (31%)
  waiting for transfers between devices  17.7 us (22%)
  between operations  0.85 us (1%)
    pallas_call x7, Pallas kernels, call(): pl.pallas_call(kernel, out_shape=[pltpu.VMEM(s, t) if where == STAY else...  37.9 us
    all_to_all x2, starting transfers between devices, exchange(): x = lax.all_to_all(x, 'dom', split_axis=0, concat_axis=0, tiled=True)  22.7 us
    all_to_all x2, waiting for transfers between devices, exchange(): x = lax.all_to_all(x, 'dom', split_axis=0, concat_axis=0, tiled=True)  17.4 us
    ppermute x1, starting transfers between devices, local(): other = lax.ppermute(part, 'feat', SWAP)  2.31 us
  transfers between devices with their start and end apart: 3, of which 3 were waited for; matrix products, arithmetic and copies ran while one was open for 0% of the time, Pallas kernels for 21%

profile of v8, /device:TPU:1, one launch (start us, length us, event | category | flops | bytes accessed | tf_op | source)
XLA Modules:
  0.0 81.5 jit_solution(8459558858084225533)
XLA Ops:
  0.6 7.8 %encode.1 = (bf16[1536,128]{1,0:T(8,128)(2,1)}, bf16[128,1024]{1,0:T(8,128)(2,1)S(1)}, s32[1,256]{1,0:T(1,128)}) custom-call(bf16[4096,128]{1,0:T(8,128)(2,1)} %inc_h.1, s32[4,1024]{1,0:T(4,128)} %bitcast.17, s32[16,128]{1,0:T(8,128)} %bitcast.19, s32[1,256]{1,0:T(1,128)} %bitcast.24, s32[8,256]{1,0:T(8,128)} %bitcast.23, bf16[256,128]{1,0:T(8,128)(2,1)} %refs_3_.1), custom_call_target="tpu_custom_call" | custom-call | tf_op jit(solution)/shard_map/encode/pallas_call | solution.py:346
  8.5 16.3 %all-to-all-start = ((bf16[128,3,4,128]{3,2,1,0:T(4,128)(2,1)}), bf16[128,3,4,128]{3,2,1,0:T(4,128)(2,1)S(1)}, u32[]{:S(2)}, u32[]{:S(2)}) async-start(bf16[128,3,4,128]{3,2,1,0:T(4,128)(2,1)} %bitcast.16), calls=%async_computation | async-start | bytes 786432 | tf_op jit(solution)/shard_map/all_to_all | solution.py:360
  24.8 7.6 %prepare.1 = (bf16[3072,1024]{1,0:T(8,128)(2,1)}, f32[128,1024]{1,0:T(8,128)S(1)}, bf16[256,512]{1,0:T(8,128)(2,1)}, bf16[512,256]{1,0:T(8,128)(2,1)S(1)}, bf16[...) custom-call(s32[6,1024]{1,0:T(8,128)} %bitcast.21, ...), custom_call_target="tpu_custom_call" | custom-call | tf_op jit(solution)/shard_map/prepare/pallas_call | solution.py:346
  32.4 9.0 %all-to-all-done = bf16[128,3,4,128]{3,2,1,0:T(4,128)(2,1)S(1)} async-done(((bf16[128,3,4,128]{3,2,1,0:T(4,128)(2,1)}), bf16[128,3,4,128]{3,2,1,0:T(4,128)(2,1)S(1)}, u32[]{:S(2)}, u32[]{:S(2)}) %all-to-all-start) | async-done | bytes 393248 | tf_op jit(solution)/shard_map/all_to_all | solution.py:360
  41.4 2.0 %mix.1 = (bf16[128,1280]{1,0:T(8,128)(2,1)S(1)}, s32[32,128]{1,0:T(8,128)S(1)}) custom-call(bf16[1536,128]{1,0:T(8,128)(2,1)S(1)} %bitcast.13, f32[128,1024]{1,0:T(8,128)S(1)} %get-tuple-element.27.own_part, bf16[3072,1024]{1,0:T(8,128)(2,1)} %get-tuple-element.28.m_h), custom_call_target="tpu_custom_call" | custom-call | tf_op jit(solution)/shard_map/mix/pallas_call | solution.py:346
  43.4 2.3 %collective-permute-start = (bf16[128,1280]{1,0:T(8,128)(2,1)S(1)}, bf16[128,1280]{1,0:T(8,128)(2,1)S(1)}, u32[]{:S(2)}, u32[]{:S(2)}) collective-permute-start(bf16[128,1280]{1,0:T(8,128)(2,1)S(1)} %get-tuple-element.29.part), channel_id=1, source_target_pairs={{0,1},{1,0},{2,3},{3,2},{4,5},{5,4},{6,7},{7,6},{8,9},{9,8},{10,11... | collective-permute-start | bytes 983048 | tf_op jit(solution)/shard_map/ppermute | solution.py:443
  45.7 1.0 %sites.1.s = bf16[1024,512]{1,0:T(8,128)(2,1)S(1)} custom-call(s32[32,128]{1,0:T(8,128)S(1)} %get-tuple-element.30.node), custom_call_target="tpu_custom_call" | custom-call | tf_op jit(solution)/shard_map/sites/pallas_call | solution.py:346
  46.7 0.3 collective-permute-done.other
  47.0 5.8 %node.1 = (bf16[1536,128]{1,0:T(8,128)(2,1)}, f32[64,1024]{1,0:T(8,128)}, bf16[1024,64]{1,0:T(8,128)(2,1)}) custom-call(bf16[128,1280]{1,0:T(8,128)(2,1)S(1)} %get-tuple-element.29.part, bf16[128,1280]{1,0:T(8,128)(2,1)S(1)} %collective-permute-done.other, bf16[128,1024]{1,0:T(8,128)(2,1)S(1)} %get-tuple-element.26.ginc, ...), custom_call_target="tpu_custom_call" | custom-call | tf_op jit(solution)/shard_map/node/pallas_call | solution.py:346
  52.8 6.4 %all-to-all-start.1 = ((bf16[128,3,4,128]{3,2,1,0:T(4,128)(2,1)}), bf16[128,3,4,128]{3,2,1,0:T(4,128)(2,1)S(1)}, u32[]{:S(2)}, u32[]{:S(2)}) async-start(bf16[128,3,4,128]{3,2,1,0:T(4,128)(2,1)} %bitcast.15), calls=%async_computation.1 | async-start | bytes 786432 | tf_op jit(solution)/shard_map/all_to_all | solution.py:360
  59.1 8.3 %scatter.1 = (bf16[1024,3328]{1,0:T(8,128)(2,1)}, bf16[1024,768]{1,0:T(8,128)(2,1)S(1)}, s32[256,1]{1,0:T(8,128)S(1)}, s32[16,128]{1,0:T(8,128)S(1)}, f32[64,1024]{1,0:T(8,128)S(1)}) custom-call(s32[4,1024]{1,0:T(4,128)} %bitcast.18, s32[1,256]{1,0:T(1,128)} %get-tuple-element.38.target, s32[16,128]{1,0:T(8,128)} %bitcast.20, ...), custom_call_target="tpu_custom_call" | custom-call | tf_op jit(solution)/shard_map/scatter/pallas_call | solution.py:346
  67.5 8.4 %all-to-all-done.1 = bf16[128,3,4,128]{3,2,1,0:T(4,128)(2,1)S(1)} async-done(((bf16[128,3,4,128]{3,2,1,0:T(4,128)(2,1)}), bf16[128,3,4,128]{3,2,1,0:T(4,128)(2,1)S(1)}, u32[]{:S(2)}, u32[]{:S(2)}) %all-to-all-start.1) | async-done | bytes 393248 | tf_op jit(solution)/shard_map/all_to_all | solution.py:360
  75.9 5.4 %finish.1 = (f32[64,4096]{1,0:T(8,128)}, bf16[256,128]{1,0:T(8,128)(2,1)}) custom-call(bf16[1536,128]{1,0:T(8,128)(2,1)S(1)} %bitcast.14, s32[16,128]{1,0:T(8,128)S(1)} %get-tuple-element.41.refs_1_, f32[64,1024]{1,0:T(8,128)S(1)} %get-tuple-element.42.refs_2_, s32[256,1]{1,0:T(8,128)S(1)} %get-tuple-element.43.refs_3_, ...), custom_call_target="tpu_custom_call" | custom-call | tf_op jit(solution)/shard_map/finish/pallas_call | solution.py:346
Async XLA Ops:
  8.5 33.0 %all-to-all-start = ((bf16[128,3,4,128]{3,2,1,0:T(4,128)(2,1)}), bf16[128,3,4,128]{3,2,1,0:T(4,128)(2,1)S(1)}, u32[]{:S(2)}, u32[]{:S(2)}) async-start(bf16[128,3,4,128]{3,2,1,0:T(4,128)(2,1)} %bitcast.16), calls=%async_computation | async-start | bytes 786432 | tf_op jit(solution)/shard_map/all_to_all | solution.py:360
  43.4 3.6 %collective-permute-start = (bf16[128,1280]{1,0:T(8,128)(2,1)S(1)}, bf16[128,1280]{1,0:T(8,128)(2,1)S(1)}, u32[]{:S(2)}, u32[]{:S(2)}) collective-permute-start(bf16[128,1280]{1,0:T(8,128)(2,1)S(1)} %get-tuple-element.29.part), channel_id=1, source_target_pairs={{0,1},{1,0},{2,3},{3,2},{4,5},{5,4},{6,7},{7,6},{8,9},{9,8},{10,11... | collective-permute-start | bytes 983048 | tf_op jit(solution)/shard_map/ppermute | solution.py:443
  52.8 23.1 %all-to-all-start.1 = ((bf16[128,3,4,128]{3,2,1,0:T(4,128)(2,1)}), bf16[128,3,4,128]{3,2,1,0:T(4,128)(2,1)S(1)}, u32[]{:S(2)}, u32[]{:S(2)}) async-start(bf16[128,3,4,128]{3,2,1,0:T(4,128)(2,1)} %bitcast.15), calls=%async_computation.1 | async-start | bytes 786432 | tf_op jit(solution)/shard_map/all_to_all | solution.py:360
